TPU v7x, 512 devices: a whole 4x4x16 slice. The times are simulated.
512 devices in a mesh: shard: 16 (over z), dp: 32 (over x, y, core).
Axes of the slice: x: 4, y: 4, z: 16, core: 2. Of those that a mesh axis runs over, the one named last changes fastest.
Arguments:
- cache_state: float32 [32, 16, 256, 384], P('dp', 'shard'), as said below
- table_state: float32 [32, 16, 512, 384], P('dp', 'shard'), as said below
- batch_idx: int32 [32, 16, 1024, 8], P('dp', 'shard'), may hold values from 0 to 255
- loss_grad: float32 [32, 16, 1024], P('dp', 'shard'), may hold values from -6 to 6
- w_first: bfloat16 [1024, 1024], replicated, may hold values from -0.1875 to 0.1875
- head: float32 [1024], replicated, may hold values from -6 to 6
- home: int32 [32, 8192], P('dp'), may hold values from 0 to 8191, as said below
- fetch_rows: int32 [32, 16, 16, 16], P('dp', 'shard'), may hold values from 0 to 8191, as said below
- fetch_counts: int32 [32, 16, 16], P('dp', 'shard'), may hold values from 0 to 16, as said below
- evict_rows: int32 [32, 16, 16, 16], P('dp', 'shard'), may hold values from 0 to 8191, as said below
- evict_from: int32 [32, 16, 16, 16], P('dp', 'shard'), may hold values from 0 to 255, as said below
- evict_counts: int32 [32, 16, 16], P('dp', 'shard'), may hold values from 0 to 16, as said below
Outputs:
- grad_first: bfloat16 [1024, 1024], P('shard')
- table_after: float32 [32, 16, 512, 384], P('dp', 'shard')
- fetched: float32 [32, 16, 16, 16, 384], P('dp', 'shard')
Inputs may be any that keep to these rules, and one draw needn't show every extreme that they name: In each group home is a permutation; row r belongs to owner home[r] // 512. `fetch_rows`: every entry, live or not, names a row of the owner whose list it is in; no row is live both in a fetch list and in a write-back list of the same group. `fetch_counts`: in every group some owner gets 16 from every device. `evict_rows`: every entry names a row of the owner whose list it is in; live entries of a group are all different rows. `evict_from`: the entries of one device are all different. `evict_counts`: in every group some owner gets 16 from every device. `cache_state`: the last 128 entries of a row are positive. `table_state`: the last 128 entries of a row are positive.
All inputs are finite; a program needn't handle non-finite values.
Results may differ from a plain program's by a relative error of at most 0.0061.
Values sent between devices are 32-bit elements; how exact they have to be, the bound alone decides.
No kernel may reach another device: no remote copies, remote signals or barrier semaphores. Data moves between devices by JAX's collectives and lax.ppermute only.
A program may use at most 64 MiB of HBM per device.

v0:
```python
import math

import jax
import jax.numpy as jnp
from jax import lax
from jax.sharding import PartitionSpec as P

beta_one = 0.9
beta_two = 0.999
learn_rate = 0.05
epsilon = 1e-08
bias_one = 1.0 - 0.9**10
bias_two = 1.0 - 0.999**10


def adam_rows(state, grads, embed):
    value = state[:, :embed]
    first = state[:, embed : 2 * embed]
    second = state[:, 2 * embed :]
    first = beta_one * first + (1.0 - beta_one) * grads
    second = beta_two * second + (1.0 - beta_two) * grads * grads
    value = value - learn_rate * (first / bias_one) / (jnp.sqrt(second / bias_two) + epsilon)
    return jnp.concatenate([value, first, second], axis=1)


def local(
    cache_state,
    table_state,
    batch_idx,
    loss_grad,
    w_first,
    head,
    home,
    fetch_rows,
    fetch_counts,
    evict_rows,
    evict_from,
    evict_counts,
):
    group = lax.axis_size("shard")
    cache = cache_state[0, 0]
    table = table_state[0, 0]
    batch = batch_idx[0, 0]
    loss = loss_grad[0, 0]
    home_map = home[0]
    wanted = fetch_rows[0, 0]
    gone = evict_rows[0, 0]
    gone_from = evict_from[0, 0]
    width = cache.shape[1]
    embed = width // 3
    table_rows = table.shape[0]
    cache_rows = cache.shape[0]
    capacity = wanted.shape[1]
    mlp_width = w_first.shape[0]
    samples = batch.shape[0]
    within = jnp.arange(capacity, dtype=jnp.int32)[None, :]
    wanted_live = within < fetch_counts[0, 0][:, None]
    gone_live = within < evict_counts[0, 0][:, None]
    place = (
        jnp.take(
            home_map,
            lax.all_to_all(wanted, "shard", split_axis=0, concat_axis=0, tiled=True),
            axis=0,
        )
        % table_rows
    )
    arrived = lax.all_to_all(
        jnp.take(table, place, axis=0), "shard", split_axis=0, concat_axis=0, tiled=True
    )
    flat_batch = batch.reshape(-1)
    looked = jnp.take(cache[:, :embed], flat_batch, axis=0)
    inputs = looked.reshape(samples, mlp_width).astype(jnp.bfloat16)
    pre = jnp.dot(inputs, w_first, preferred_element_type=jnp.float32)
    sigma = jax.nn.sigmoid(pre)
    delta = (loss[:, None] * head[None, :] * sigma * (1.0 + pre * (1.0 - sigma))).astype(
        jnp.bfloat16
    )
    back = lax.dot_general(
        delta, w_first, (((1,), (1,)), ((), ())), preferred_element_type=jnp.float32
    )
    positions = jnp.arange(cache_rows, dtype=jnp.int32)
    onehot = (flat_batch[:, None] == positions[None, :]).astype(jnp.float32)
    grads = lax.dot_general(
        onehot,
        back.reshape(-1, embed),
        (((0,), (0,)), ((), ())),
        precision=lax.Precision.HIGHEST,
        preferred_element_type=jnp.float32,
    )
    updated = adam_rows(cache, grads, embed)
    sent_rows = jnp.take(updated, gone_from.reshape(-1), axis=0).reshape(group, capacity, width)
    sent_slots = jnp.where(gone_live, jnp.take(home_map, gone, axis=0) % table_rows, table_rows)
    got_rows, got_slots = (
        lax.all_to_all(sent_rows, "shard", split_axis=0, concat_axis=0, tiled=True),
        lax.all_to_all(sent_slots, "shard", split_axis=0, concat_axis=0, tiled=True),
    )
    new_table = table.at[got_slots.reshape(-1)].set(got_rows.reshape(-1, width), mode="drop")
    fetched = jnp.where(wanted_live[:, :, None], arrived, jnp.zeros_like(arrived))
    scale = 1.0 / math.sqrt(samples * group * lax.axis_size("dp"))
    partial_rows = lax.psum_scatter(
        lax.dot_general(
            inputs, delta, (((0,), (0,)), ((), ())), preferred_element_type=jnp.float32
        ),
        "shard",
        scatter_dimension=0,
        tiled=True,
    )
    mine = lax.psum(partial_rows, "dp")
    grad_first = (mine * scale).astype(jnp.bfloat16)
    return (grad_first, new_table[None, None], fetched[None, None])


def solution(mesh):
    placed = (
        P("dp", "shard", None, None),
        P("dp", "shard", None, None),
        P("dp", "shard", None, None),
        P("dp", "shard", None),
        P(),
        P(),
        P("dp", None),
        P("dp", "shard", None, None),
        P("dp", "shard", None),
        P("dp", "shard", None, None),
        P("dp", "shard", None, None),
        P("dp", "shard", None),
    )
    return jax.shard_map(
        local,
        mesh=mesh,
        in_specs=placed,
        out_specs=(
            P("shard", None),
            P("dp", "shard", None, None),
            P("dp", "shard", None, None, None),
        ),
        check_vma=False,
    )
```

profile of v0, /device:TPU:1, one launch (start us, length us, event | category | flops | bytes accessed | tf_op | source)
XLA Modules:
  0.0 311.4 jit_solution(12262826087370051198)
XLA Ops:
  7.2 0.0 copy-start
  7.2 0.0 copy-start.4
  7.2 0.0 reduce-scatter.2.cloned.1.call-start
  7.2 1.3 copy.40
  8.5 0.9 copy.27
  9.5 0.0 copy-done.4
  9.5 1.9 copy.26
  11.4 1.5 slice.23
  13.0 0.9 copy.28
  13.9 0.3 reshape_squeeze.13
  14.3 29.2 %gather_fusion = bf16[8192,128]{1,0:T(8,128)(2,1)} fusion(bf16[256,128]{1,0:T(8,128)(2,1)S(1)} %copy.28, s32[8192]{0:T(1024)S(1)} %broadcast_clamp_fusion), kind=kCustom, calls=%fused_computation.2 | custom fusion | bytes 4227072 | tf_op jit(solution)/shard_map/jit(_take)/gather | solution.py:71
  43.5 4.2 %gather.20 = bf16[1024,1024]{1,0:T(8,128)(2,1)} reshape(bf16[8192,128]{1,0:T(8,128)(2,1)} %gather_fusion) | data formatting | bytes 4194304 | tf_op jit(solution)/shard_map/jit(_take)/gather | solution.py:71
  47.7 0.9 copy.25
  48.5 4.0 %broadcast_in_dim.62 = pred[1024,8,128]{2,1,0:T(8,128)(4,1)S(1)} broadcast(pred[1024,8]{1,0:T(8,128)(4,1)} %copy.25), dimensions={0,1} | broadcast | bytes 1056768 | tf_op jit(solution)/shard_map/jit(_take)/broadcast_in_dim | solution.py:71
  52.5 0.0 copy-done
  52.6 0.0 copy-done.9
  52.6 0.0 copy-done.10
  52.6 0.0 copy-start.3
  52.6 5.1 %multiply_convert_fusion = bf16[1024,1024]{1,0:T(8,128)(2,1)S(1)} fusion(f32[1024]{0:T(1024)S(1)} %copy-done.9, f32[1024]{0:T(1024)S(1)} %bitcast.67, bf16[1024,1024]{1,0:T(8,128)(2,1)S(1)} %copy-done, bf16[1024,1024]{1,0:T(8,128)(2,1)} %gather.20, pred[128,8,8,128]{3,2,1,0:T(8,128)(4,1)S(1)} %bitcast.56), kind=kOutput, calls=%fused_computation.9 | convolution fusion | flops 2159017984 | bytes 7348224 | tf_op jit(solution)/shard_map/dot_general | solution.py:73
  57.7 1.4 copy-done.11
  59.1 0.0 copy-done.3
  59.1 4.5 %fusion.4 = f32[1024,1024]{1,0:T(8,128)} fusion(bf16[1024,1024]{1,0:T(8,128)(2,1)S(1)} %multiply_convert_fusion, bf16[1024,1024]{1,0:T(8,128)(2,1)S(1)} %copy-done.3, pred[128,8,8,128]{3,2,1,0:T(8,128)(4,1)S(1)} %bitcast.57), kind=kOutput, calls=%fused_computation.25 | convolution fusion | flops 2148532224 | bytes 9437184 | tf_op jit(solution)/shard_map/dot_general | solution.py:101
  63.5 0.0 reduce-scatter.2.cloned.1.call-update
  63.5 15.7 %all-to-all-start.2 = ((s32[16,1,16]{2,1,0:T(1,128)}), s32[16,1,16]{2,1,0:T(1,128)S(1)}, u32[]{:S(2)}, u32[]{:S(2)}) async-start(s32[16,1,16]{2,1,0:T(1,128)} %bitcast.16), calls=%async_computation.3 | async-start | bytes 16384 | tf_op jit(solution)/shard_map/all_to_all | solution.py:62
  79.3 0.3 reshape_squeeze.15
  79.5 0.1 reshape.224
  79.6 1.7 gather_fusion.3
  81.4 0.1 reshape.227
  81.5 5.9 %fusion.13 = f32[1024,1024]{1,0:T(8,128)} fusion(bf16[1024,1024]{1,0:T(8,128)(2,1)} %copy-done.11, bf16[1024,1024]{1,0:T(8,128)(2,1)S(1)} %copy-done), kind=kOutput, calls=%fused_computation.53 | convolution fusion | flops 2147483648 | bytes 8388608 | tf_op jit(solution)/shard_map/dot_general | solution.py:78
  87.4 4.9 %reshape.168 = f32[8192,128]{1,0:T(8,128)} reshape(f32[1024,1024]{1,0:T(8,128)} %fusion.13) | data formatting | bytes 8388608 | tf_op jit(solution)/shard_map/reshape | solution.py:85
  92.3 0.0 copy-done.5
  92.3 0.1 reshape_squeeze.16
  92.4 7.0 %divide_subtract_fusion = (f32[256,128]{0,1:T(8,128)S(1)}, f32[256,128]{0,1:T(8,128)S(1)}, f32[256,128]{0,1:T(8,128)S(1)}) fusion(f32[256,384]{0,1:T(8,128)} %bitcast.59, f32[8192,128]{1,0:T(8,128)} %reshape.168, s32[8192]{0:T(1024)S(1)} %reshape_squeeze.15), kind=kOutput, calls=%fused_computation.22 | convolution fusion | flops 3223715840 | bytes 5013504 | tf_op jit(solution)/shard_map/dot_general | solution.py:83
  99.4 0.8 pad_maximum_fusion
  100.2 0.7 fusion.7
  100.9 1.2 copy.30
  102.0 1.7 gather_fusion.1
  103.8 0.0 all-to-all-done.2
  103.8 11.4 %all-to-all-start = ((s32[16,1,16]{2,1,0:T(1,128)}), s32[16,1,16]{2,1,0:T(1,128)S(1)}, u32[]{:S(2)}, u32[]{:S(2)}) async-start(s32[16,1,16]{2,1,0:T(1,128)} %bitcast.8), calls=%async_computation.1 | async-start | bytes 16384 | tf_op jit(solution)/shard_map/all_to_all | solution.py:95
  115.2 1.9 broadcast_select_fusion.1
  117.1 9.5 %all-to-all-done = s32[16,1,16]{2,1,0:T(1,128)S(1)} async-done(((s32[16,1,16]{2,1,0:T(1,128)}), s32[16,1,16]{2,1,0:T(1,128)S(1)}, u32[]{:S(2)}, u32[]{:S(2)}) %all-to-all-start) | async-done | bytes 1056 | tf_op jit(solution)/shard_map/all_to_all | solution.py:95
  126.6 3.6 %all-to-all-start.1 = ((f32[16,16,384]{2,1,0:T(8,128)}), f32[16,16,384]{2,1,0:T(8,128)S(1)}, u32[]{:S(2)}, u32[]{:S(2)}) async-start(f32[16,16,384]{2,1,0:T(8,128)} %broadcast_select_fusion.1), calls=%async_computation.2 | async-start | bytes 786432 | tf_op jit(solution)/shard_map/all_to_all | solution.py:94
  130.2 0.1 reshape.228
  130.3 1.7 gather_fusion.4
  132.0 0.1 reshape.231
  132.1 0.1 reshape.204
  132.2 1.7 gather_fusion.2
  133.9 1.9 broadcast_select_fusion
  135.8 17.8 %all-to-all-done.1 = f32[16,16,384]{2,1,0:T(8,128)S(1)} async-done(((f32[16,16,384]{2,1,0:T(8,128)}), f32[16,16,384]{2,1,0:T(8,128)S(1)}, u32[]{:S(2)}, u32[]{:S(2)}) %all-to-all-start.1) | async-done | bytes 393248 | tf_op jit(solution)/shard_map/all_to_all | solution.py:94
  153.6 10.1 %all-to-all-start.3 = ((f32[16,16,384]{2,1,0:T(8,128)}), f32[16,16,384]{2,1,0:T(8,128)}, u32[]{:S(2)}, u32[]{:S(2)}) async-start(f32[16,16,384]{2,1,0:T(8,128)} %broadcast_select_fusion), calls=%async_computation.4 | async-start | bytes 786432 | tf_op jit(solution)/shard_map/all_to_all | solution.py:67
  163.7 0.0 all-reduce.2.cloned.1.call-start
  163.8 0.1 iota_compare_fusion.2
  163.8 0.5 broadcast.135
  164.3 0.7 reduce.3
  165.0 0.1 reshape.167
  165.1 1.7 scatter_fusion
  166.8 0.0 copy-start.2
  166.9 0.0 reduce-scatter.2.cloned.1.call-done
  166.9 0.0 all-reduce.2.cloned.1.call-update
  166.9 13.7 %all-to-all-done.3 = f32[16,16,384]{2,1,0:T(8,128)} async-done(((f32[16,16,384]{2,1,0:T(8,128)}), f32[16,16,384]{2,1,0:T(8,128)}, u32[]{:S(2)}, u32[]{:S(2)}) %all-to-all-start.3) | async-done | bytes 393248 | tf_op jit(solution)/shard_map/all_to_all | solution.py:67
  180.6 1.8 select_bitcast_fusion
  182.4 120.5 %all-reduce.2.cloned.1.call-done = f32[64,1024]{1,0:T(8,128)} async-done(((f32[64,1024]{1,0:T(8,128)}), f32[64,1024]{1,0:T(8,128)}) %all-reduce.2.cloned.1.call-update) | async-done | bytes 262160 | tf_op jit(solution)/shard_map/psum | solution.py:108
  303.0 1.6 multiply_convert_fusion.1
  304.6 0.0 copy-done.2
  (25 shorter events, 0.2 us)
Async XLA Ops:
  7.2 45.4 %copy-start = (bf16[1024,1024]{1,0:T(8,128)(2,1)S(1)}, bf16[1024,1024]{1,0:T(8,128)(2,1)}, u32[]{:S(2)}) copy-start(bf16[1024,1024]{1,0:T(8,128)(2,1)} %param.18) | copy-start | bytes 6291460
  7.2 2.3 copy-start.4
  7.2 159.7 %reduce-scatter.2.cloned.1.call-start = ((), (), s32[]{:S(2)}) async-start(), calls=%async_computation.5 | async-start | bytes 4456448 | tf_op jit(solution)/shard_map/reduce_scatter | solution.py:100
  43.5 9.1 %copy-start.9 = (f32[1024]{0:T(1024)S(1)}, f32[1024]{0:T(1024)}, u32[]{:S(2)}) copy-start(f32[1024]{0:T(1024)} %param.19) | copy-start | bytes 12292
  43.5 9.1 %copy-start.10 = (f32[1,1,1024]{2,1,0:T(1,128)S(1)}, f32[1,1,1024]{2,1,0:T(1,128)}, u32[]{:S(2)}) copy-start(f32[1,1,1024]{2,1,0:T(1,128)} %param.17) | copy-start | bytes 12292
  52.6 6.5 %copy-start.3 = (bf16[1024,1024]{1,0:T(8,128)(2,1)S(1)}, bf16[1024,1024]{1,0:T(8,128)(2,1)}, u32[]{:S(2)}) copy-start(bf16[1024,1024]{1,0:T(8,128)(2,1)} %gather.20) | copy-start | bytes 6291460
  57.7 1.4 copy-start.11
  63.5 16.0 %copy-start.6 = (s32[1,1,16,16]{3,2,1,0:T(8,128)S(1)}, s32[1,1,16,16]{3,2,1,0:T(8,128)}, u32[]{:S(2)}) copy-start(s32[1,1,16,16]{3,2,1,0:T(8,128)} %param.23) | copy-start | bytes 3076
  63.5 16.1 %copy-start.1 = (s32[1,8192]{1,0:T(1,128)S(1)}, s32[1,8192]{1,0:T(1,128)}, u32[]{:S(2)}) copy-start(s32[1,8192]{1,0:T(1,128)} %param.20) | copy-start | bytes 98308
  63.5 40.2 %all-to-all-start.2 = ((s32[16,1,16]{2,1,0:T(1,128)}), s32[16,1,16]{2,1,0:T(1,128)S(1)}, u32[]{:S(2)}, u32[]{:S(2)}) async-start(s32[16,1,16]{2,1,0:T(1,128)} %bitcast.16), calls=%async_computation.3 | async-start | bytes 16384 | tf_op jit(solution)/shard_map/all_to_all | solution.py:62
  87.4 4.9 %copy-start.5 = (s32[1,1,16,16]{3,2,1,0:T(8,128)S(1)}, s32[1,1,16,16]{3,2,1,0:T(8,128)}, u32[]{:S(2)}) copy-start(s32[1,1,16,16]{3,2,1,0:T(8,128)} %param.24) | copy-start | bytes 3076
  92.4 7.8 %copy-start.7 = (s32[1,1,16]{2,1,0:T(1,128)S(1)}, s32[1,1,16]{2,1,0:T(1,128)}, u32[]{:S(2)}) copy-start(s32[1,1,16]{2,1,0:T(1,128)} %param.25) | copy-start | bytes 196
  103.8 22.8 %all-to-all-start = ((s32[16,1,16]{2,1,0:T(1,128)}), s32[16,1,16]{2,1,0:T(1,128)S(1)}, u32[]{:S(2)}, u32[]{:S(2)}) async-start(s32[16,1,16]{2,1,0:T(1,128)} %bitcast.8), calls=%async_computation.1 | async-start | bytes 16384 | tf_op jit(solution)/shard_map/all_to_all | solution.py:95
  126.6 27.0 %all-to-all-start.1 = ((f32[16,16,384]{2,1,0:T(8,128)}), f32[16,16,384]{2,1,0:T(8,128)S(1)}, u32[]{:S(2)}, u32[]{:S(2)}) async-start(f32[16,16,384]{2,1,0:T(8,128)} %broadcast_select_fusion.1), calls=%async_computation.2 | async-start | bytes 786432 | tf_op jit(solution)/shard_map/all_to_all | solution.py:94
  132.2 31.6 %copy-start.8 = (s32[1,1,16]{2,1,0:T(1,128)S(1)}, s32[1,1,16]{2,1,0:T(1,128)}, u32[]{:S(2)}) copy-start(s32[1,1,16]{2,1,0:T(1,128)} %param.22) | copy-start | bytes 196
  153.6 27.0 %all-to-all-start.3 = ((f32[16,16,384]{2,1,0:T(8,128)}), f32[16,16,384]{2,1,0:T(8,128)}, u32[]{:S(2)}, u32[]{:S(2)}) async-start(f32[16,16,384]{2,1,0:T(8,128)} %broadcast_select_fusion), calls=%async_computation.4 | async-start | bytes 786432 | tf_op jit(solution)/shard_map/all_to_all | solution.py:67
  163.7 139.3 %all-reduce.2.cloned.1.call-start = ((), (), s32[]{:S(2)}) async-start(), calls=%async_computation.6 | async-start | bytes 524288 | tf_op jit(solution)/shard_map/psum | solution.py:108
  166.8 137.8 %copy-start.2 = (f32[512,384]{1,0:T(8,128)}, f32[512,384]{1,0:T(8,128)S(1)}, u32[]{:S(2)}) copy-start(f32[512,384]{1,0:T(8,128)S(1)} %scatter_fusion) | copy-start | bytes 2359300
Sparse Core Ops, SparseCore 0:
  63.7 89.7 reduce-scatter.1
  167.7 135.1 all-reduce.1
where the time goes:
time: 313 us; the launch traced here: 311 us
  waiting for transfers between devices  162 us (52%)
  local copies, waits for them, and re-layouts  62.6 us (20%)
  starting transfers between devices  40.9 us (13%)
  matrix products  22.5 us (7%)
  between operations  14.3 us (5%)
  other arithmetic  9.51 us (3%)
    psum x1, waiting for transfers between devices, local(): mine = lax.psum(partial_rows, 'dp')  121 us
    gather x2, local copies, waits for them, and re-layouts, local(): looked = jnp.take(cache[:, :embed], flat_batch, axis=0)  33.4 us
    all_to_all x1, waiting for transfers between devices, local(): lax.all_to_all(sent_rows, 'shard', split_axis=0, concat_axis=0, tiled=True)  17.8 us
    all_to_all x1, starting transfers between devices, local(): lax.all_to_all(wanted, 'shard', split_axis=0, concat_axis=0, tiled=True)  15.7 us
    all_to_all x1, waiting for transfers between devices, local(): lax.all_to_all(jnp.take(table, place, axis=0), 'shard', split_axis=0, con...  13.7 us
    all_to_all x1, starting transfers between devices, local(): lax.all_to_all(sent_slots, 'shard', split_axis=0, concat_axis=0, tiled=True)  11.4 us
    all_to_all x1, starting transfers between devices, local(): lax.all_to_all(jnp.take(table, place, axis=0), 'shard', split_axis=0, con...  10.1 us
    all_to_all x1, waiting for transfers between devices, local(): lax.all_to_all(sent_slots, 'shard', split_axis=0, concat_axis=0, tiled=True)  9.54 us
  transfers between devices with their start and end apart: 6, of which 4 were waited for; matrix products, arithmetic and copies ran while one was open for 12% of the time, Pallas kernels for 0%

commit v1 on v0

v1 whole, which is shorter than its diff:
```python
import math

import jax
import jax.numpy as jnp
from jax import lax
from jax.experimental import pallas as pl
from jax.experimental.pallas import tpu as pltpu
from jax.sharding import PartitionSpec as P

beta_one = 0.9
beta_two = 0.999
learn_rate = 0.05
epsilon = 1e-08
bias_one = 1.0 - 0.9**10
bias_two = 1.0 - 0.999**10
NN = (((1,), (0,)), ((), ()))
NT = (((1,), (1,)), ((), ()))
TN = (((0,), (0,)), ((), ()))
side = 4


def full(shape):
    return pl.BlockSpec(shape, lambda j, o: tuple(0 for _ in shape))


def column(row):
    return jnp.transpose(jnp.broadcast_to(row, (8, row.shape[1])))[:, :1]


def onehot(batch_row, rows):
    shape = (rows, batch_row.shape[1])
    hit = lax.broadcasted_iota(jnp.int32, shape, 0) == batch_row
    return hit.astype(jnp.float32).astype(jnp.bfloat16)


def hidden(inputs, loss, head, w, delta_ref, grad_ref):
    pre = lax.dot_general(w, inputs, TN, preferred_element_type=jnp.float32)
    sigma = jax.nn.sigmoid(pre)
    delta = (loss * column(head) * sigma * (1.0 + pre * (1.0 - sigma))).astype(jnp.bfloat16)
    delta_ref[...] = delta
    grad_ref[...] = lax.dot_general(inputs, delta, NT, preferred_element_type=jnp.float32)


def first_kernel(order, cache_ref, batch_ref, loss_ref, head_ref, w_ref, grad_ref, delta_ref, inputs_ref):
    rows = cache_ref.shape[0]
    features = batch_ref.shape[0]
    embed = inputs_ref.shape[0] // features

    @pl.when(pl.program_id(0) == 0)
    def _():
        looked = jnp.transpose(cache_ref[...]).astype(jnp.bfloat16)
        for f in range(features):
            pick = onehot(batch_ref[f : f + 1, :], rows)
            inputs_ref[f * embed : (f + 1) * embed, :] = lax.dot_general(
                looked, pick, NN, preferred_element_type=jnp.float32
            ).astype(jnp.bfloat16)

    hidden(inputs_ref[...], loss_ref[...], head_ref[...], w_ref[...], delta_ref, grad_ref)


def second_kernel(order, inputs_ref, loss_ref, head_ref, w_ref, grad_ref, delta_ref):
    hidden(inputs_ref[...], loss_ref[...], head_ref[...], w_ref[...], delta_ref, grad_ref)


def forward_half(order, cache, batch_t, inputs, loss, head, w):
    samples = loss.shape[1]
    width = w.shape[0]
    half = width // 2
    block = half // 2
    steps = half // block
    tail_specs = [
        full((1, samples)),
        pl.BlockSpec((1, block), lambda j, o: (0, o[j])),
        pl.BlockSpec((width, block), lambda j, o: (0, o[j])),
    ]
    grad = jax.ShapeDtypeStruct((width, half), jnp.float32)
    delta = jax.ShapeDtypeStruct((half, samples), jnp.bfloat16)
    grad_spec = pl.BlockSpec((width, block), lambda j, o: (0, j))
    delta_spec = pl.BlockSpec((block, samples), lambda j, o: (j, 0))
    if inputs is None:
        rows = cache.shape[0]
        embed = cache.shape[1] // 3
        return pl.pallas_call(
            first_kernel,
            out_shape=(grad, delta, jax.ShapeDtypeStruct((width, samples), jnp.bfloat16)),
            grid_spec=pltpu.PrefetchScalarGridSpec(
                num_scalar_prefetch=1,
                grid=(steps,),
                in_specs=[pl.BlockSpec((rows, embed), lambda j, o: (0, 0)), full(batch_t.shape)] + tail_specs,
                out_specs=(grad_spec, delta_spec, full((width, samples))),
            ),
            name="forward_first",
        )(order, cache, batch_t, loss, head, w)
    return pl.pallas_call(
        second_kernel,
        out_shape=(grad, delta),
        grid_spec=pltpu.PrefetchScalarGridSpec(
            num_scalar_prefetch=1,
            grid=(steps,),
            in_specs=[full((width, samples))] + tail_specs,
            out_specs=(grad_spec, delta_spec),
        ),
        name="forward_second",
    )(order, inputs, loss, head, w)


def backward_kernel(where, cache_ref, batch_ref, delta_a, delta_b, w_a, w_b, sent_ref, acc_ref, upd_ref):
    rows, width = cache_ref.shape
    embed = width // 3
    step = pl.program_id(0)
    back = lax.dot_general(w_a[...], delta_a[...], NN, preferred_element_type=jnp.float32)
    back += lax.dot_general(w_b[...], delta_b[...], NN, preferred_element_type=jnp.float32)
    total = None
    for k in range(w_a.shape[0] // embed):
        part = back[k * embed : (k + 1) * embed]
        high = part.astype(jnp.bfloat16)
        low = (part - high.astype(jnp.float32)).astype(jnp.bfloat16)
        pick = onehot(batch_ref[0, k : k + 1, :], rows)
        add = lax.dot_general(jnp.concatenate([high, low], 0), pick, NT, preferred_element_type=jnp.float32)
        total = add if total is None else total + add

    @pl.when(step == 0)
    def _():
        acc_ref[...] = total

    @pl.when(step > 0)
    def _():
        acc_ref[...] += total

    @pl.when(step == pl.num_programs(0) - 1)
    def _():
        grads = jnp.transpose(acc_ref[:embed, :] + acc_ref[embed:, :])
        value = cache_ref[:, :embed]
        first = cache_ref[:, embed : 2 * embed]
        second = cache_ref[:, 2 * embed :]
        first = beta_one * first + (1.0 - beta_one) * grads
        second = beta_two * second + (1.0 - beta_two) * grads * grads
        upd_ref[:, :embed] = value - learn_rate * (first / bias_one) / (jnp.sqrt(second / bias_two) + epsilon)
        upd_ref[:, embed : 2 * embed] = first
        upd_ref[:, 2 * embed :] = second

        def move(i, carry):
            for u in range(8):
                r = i * 8 + u
                sent_ref[pl.ds(r, 1), :] = upd_ref[pl.ds(where[r], 1), :]
            return carry

        lax.fori_loop(0, sent_ref.shape[0] // 8, move, 0)


def backward(where, cache, batch_t, delta_a, delta_b, w):
    rows, width3 = cache.shape
    embed = width3 // 3
    features, samples = batch_t.shape
    width = w.shape[0]
    half = width // 2
    steps = features // 2
    count = where.shape[0] - 2
    return pl.pallas_call(
        backward_kernel,
        out_shape=jax.ShapeDtypeStruct((count, width3), jnp.float32),
        grid_spec=pltpu.PrefetchScalarGridSpec(
            num_scalar_prefetch=1,
            grid=(steps,),
            in_specs=[
                full((rows, width3)),
                pl.BlockSpec((1, 2, samples), lambda j, o: (j, 0, 0)),
                full((half, samples)),
                full((half, samples)),
                pl.BlockSpec((2 * embed, half), lambda j, o: (j, o[count])),
                pl.BlockSpec((2 * embed, half), lambda j, o: (j, o[count + 1])),
            ],
            out_specs=full((count, width3)),
            scratch_shapes=[pltpu.VMEM((2 * embed, rows), jnp.float32), pltpu.VMEM((rows, width3), jnp.float32)],
        ),
        name="backward",
    )(where, cache, batch_t.reshape(steps, 2, samples), delta_a, delta_b, w, w)


def swap_pairs():
    return [(d, d ^ 1) for d in range(2 * side * side)]


def ring_pairs(step_x, step_y):
    return [
        ((x * side + y) * 2 + c, (((x + step_x) % side) * side + (y + step_y) % side) * 2 + c)
        for x in range(side)
        for y in range(side)
        for c in range(2)
    ]


def pick_block(a, i, axis):
    return lax.dynamic_index_in_dim(a, i & (side - 1), axis, keepdims=False)


def spread(a, i, axis, along_x):
    total = pick_block(a, i, axis)
    parts = [
        lax.ppermute(pick_block(a, i + s, axis), "dp", ring_pairs(s, 0) if along_x else ring_pairs(0, s))
        for s in range(1, side)
    ]
    return total + parts[0] + parts[1] + parts[2]


def reduce_gradient(send, keep, place):
    x, y = place >> 3, (place >> 1) & (side - 1)
    group = lax.axis_size("shard")
    mine = keep + lax.ppermute(send, "dp", swap_pairs())
    width, half = mine.shape
    mine = mine.reshape(group, 2, side, width // (group * 2 * side), side, half // side)
    even, odd = mine[:, 0], mine[:, 1]
    even = spread(even, x, 3, True)
    odd = spread(odd, y, 1, False)
    even = spread(even, y, 1, False)
    odd = spread(odd, x, 2, True)
    both = jnp.stack([even, odd], 1)
    both = lax.all_to_all(both, "shard", split_axis=0, concat_axis=0, tiled=True)
    return jnp.sum(both, 0)


def local(
    cache_state,
    table_state,
    batch_idx,
    loss_grad,
    w_first,
    head,
    home,
    fetch_rows,
    fetch_counts,
    evict_rows,
    evict_from,
    evict_counts,
):
    group = lax.axis_size("shard")
    devices = lax.axis_size("dp")
    place = lax.axis_index("dp").astype(jnp.uint32)
    core = (place & 1).astype(jnp.int32)
    cache = cache_state[0, 0]
    table = table_state[0, 0]
    batch_t = batch_idx[0, 0].T
    loss = loss_grad[0]
    home_map = home[0]
    wanted = fetch_rows[0, 0]
    gone = evict_rows[0, 0]
    width = cache.shape[1]
    table_rows = table.shape[0]
    capacity = wanted.shape[1]
    samples = loss.shape[1]
    mlp_width = w_first.shape[0]
    within = jnp.arange(capacity, dtype=jnp.int32)[None, :]
    wanted_live = within < fetch_counts[0, 0][:, None]
    gone_live = within < evict_counts[0, 0][:, None]

    slots = jnp.take(home_map, jnp.concatenate([wanted, gone], 1), axis=0) % table_rows
    live = jnp.concatenate([jnp.ones_like(wanted_live), gone_live], 1)
    asked = lax.all_to_all(
        jnp.where(live, slots, table_rows), "shard", split_axis=0, concat_axis=0, tiled=True
    )
    got_slots = asked[:, capacity:]
    arrived = lax.all_to_all(
        jnp.take(table, asked[:, :capacity], axis=0), "shard", split_axis=0, concat_axis=0, tiled=True
    )

    far = 1 - core
    order = jnp.arange(2, dtype=jnp.int32)
    send, delta_a, inputs = forward_half(order + 2 * far, cache, batch_t, None, loss, head[None], w_first)
    keep, delta_b = forward_half(order + 2 * core, cache, batch_t, inputs, loss, head[None], w_first)
    where = jnp.concatenate([evict_from[0, 0].reshape(-1), jnp.stack([far, core]).astype(jnp.int32)])
    sent_rows = backward(where, cache, batch_t, delta_a, delta_b, w_first).reshape(group, capacity, width)
    got_rows = lax.all_to_all(sent_rows, "shard", split_axis=0, concat_axis=0, tiled=True)
    new_table = table.at[got_slots.reshape(-1)].set(got_rows.reshape(-1, width), mode="drop")
    fetched = jnp.where(wanted_live[:, :, None], arrived, jnp.zeros_like(arrived))

    mine = reduce_gradient(send, keep, place)
    scale = 1.0 / math.sqrt(samples * group * devices)
    every = lax.all_to_all(
        jnp.broadcast_to(mine[None], (devices,) + mine.shape), "dp", split_axis=0, concat_axis=0, tiled=True
    )
    rows, columns = mine.shape[1:]
    every = every.reshape(side, side, 2, 2, rows, columns).transpose(3, 1, 4, 2, 0, 5)
    grad_first = (every.reshape(mlp_width // group, mlp_width) * scale).astype(jnp.bfloat16)
    return (grad_first, new_table[None, None], fetched[None, None])


def solution(mesh):
    placed = (
        P("dp", "shard", None, None),
        P("dp", "shard", None, None),
        P("dp", "shard", None, None),
        P("dp", "shard", None),
        P(),
        P(),
        P("dp", None),
        P("dp", "shard", None, None),
        P("dp", "shard", None),
        P("dp", "shard", None, None),
        P("dp", "shard", None, None),
        P("dp", "shard", None),
    )
    return jax.shard_map(
        local,
        mesh=mesh,
        in_specs=placed,
        out_specs=(
            P("shard", None),
            P("dp", "shard", None, None),
            P("dp", "shard", None, None, None),
        ),
        check_vma=False,
    )
```

time: 313 us -> 177 us (0.57)
  waiting for transfers between devices: 162 us -> 33 us
  starting transfers between devices: 40.9 us -> 98.9 us
  local copies, waits for them, and re-layouts: 62.6 us -> 10.7 us
  Pallas kernels: 0 us -> 24.2 us
  matrix products: 22.5 us -> 0 us
  between operations: 14.3 us -> 1.08 us
    psum x1 -> x0, waiting for transfers between devices: 121 us -> none  [local(): mine = lax.psum(partial_rows, 'dp')]
    ppermute x0 -> x13, starting transfers between devices: none -> 47 us  [the longest x12 38.2 us: spread(): lax.ppermute(pick_block(a, i + s, axis), 'dp', ring_pairs(s, 0) if along_...]
    gather x8 -> x3, local copies, waits for them, and re-layouts: 40.4 us -> 4.2 us  [the longest x2 3.22 us: local(): jnp.take(home_map, jnp.concatenate([wanted, gone], 1), axis=0) % table_rows]
    pallas_call x0 -> x3, Pallas kernels: none -> 24.2 us  [the longest x1 10.3 us: backward(): pl.pallas_call(backward_kernel, out_shape=jax.ShapeDtypeStruct((count, wi...]
    dot_general x4 -> x0, matrix products: 22.5 us -> none  [the longest x1 6.97 us: local(): lax.dot_general(onehot, back.reshape(-1, embed), (((0,), (0,)), ((), ()))...]
    all_to_all x1, waiting for transfers between devices: 17.8 us -> 0.01 us  [local(): lax.all_to_all(sent_rows, 'shard', split_axis=0, concat_axis=0, tiled=True)]
    all_to_all x1, starting transfers between devices: 3.55 us -> 11.5 us  [local(): lax.all_to_all(sent_rows, 'shard', split_axis=0, concat_axis=0, tiled=True)]
    all_to_all x3 -> x4, waiting for transfers between devices: 23.2 us -> 30.9 us  [the longest x1 14.5 us: local(): lax.all_to_all(jnp.take(table, asked[:, :capacity], axis=0), 'shard', spl...]
  transfers between devices with their start and end apart: 6 -> 18, of which waited for: 4 -> 5; matrix products, arithmetic and copies ran while one was open for 12% -> 9% of each run, Pallas kernels for 0% -> 10%
where the time goes in v1:
time: 177 us; the launch traced here: 176 us
  starting transfers between devices  98.9 us (56%)
  waiting for transfers between devices  33 us (19%)
  Pallas kernels  24.2 us (14%)
  local copies, waits for them, and re-layouts  10.7 us (6%)
  other arithmetic  8.61 us (5%)
    ppermute x12, starting transfers between devices, spread(): lax.ppermute(pick_block(a, i + s, axis), 'dp', ring_pairs(s, 0) if along_...  38.2 us
    all_to_all x1, starting transfers between devices, local(): lax.all_to_all(jnp.broadcast_to(mine[None], (devices,) + mine.shape), 'dp...  15.4 us
    all_to_all x1, waiting for transfers between devices, local(): lax.all_to_all(jnp.take(table, asked[:, :capacity], axis=0), 'shard', spl...  14.5 us
    all_to_all x1, starting transfers between devices, reduce_gradient(): lax.all_to_all(both, 'shard', split_axis=0, concat_axis=0, tiled=True)  11.5 us
    all_to_all x1, starting transfers between devices, local(): lax.all_to_all(sent_rows, 'shard', split_axis=0, concat_axis=0, tiled=True)  11.5 us
    pallas_call x1, Pallas kernels, backward(): pl.pallas_call(backward_kernel, out_shape=jax.ShapeDtypeStruct((count, wi...  10.3 us
    all_to_all x1, waiting for transfers between devices, reduce_gradient(): lax.all_to_all(both, 'shard', split_axis=0, concat_axis=0, tiled=True)  10.1 us
    all_to_all x1, starting transfers between devices, local(): lax.all_to_all(jnp.where(live, slots, table_rows), 'shard', split_axis=0,...  9.57 us
  transfers between devices with their start and end apart: 18, of which 5 were waited for; matrix products, arithmetic and copies ran while one was open for 9% of the time, Pallas kernels for 10%

profile of v1, /device:TPU:1, one launch (start us, length us, event | category | flops | bytes accessed | tf_op | source)
XLA Modules:
  0.0 176.5 jit_solution(14922818244530979389)
XLA Ops:
  0.6 0.0 copy-start
  0.7 1.2 copy.26
  1.8 0.5 iota_add_fusion.order
  2.3 7.1 %forward_first.1 = (f32[1024,512]{1,0:T(8,128)}, bf16[512,1024]{1,0:T(8,128)(2,1)}, bf16[1024,1024]{1,0:T(8,128)(2,1)}) custom-call(s32[2]{0:T(128)} %iota_add_fusion.order, f32[256,384]{1,0:T(8,128)} %bitcast.106, s32[8,1024]{1,0:T(8,128)} %bitcast.109, f32[1,1024]{1,0:T(1,128)} %bitcast.118, f32[1,1024]{1,0:T(1,128)} %bitcast.120, bf16[1024,1024]{1,0:T(8,128)(2,1)} %w_b.1), custom_call_target="tpu_custom_call" | custom-call | tf_op jit(solution)/shard_map/forward_first/pallas_call | solution.py:83
  9.4 8.7 %collective-permute-start = (f32[1024,512]{1,0:T(8,128)}, f32[1024,512]{1,0:T(8,128)S(1)}, u32[]{:S(2)}, u32[]{:S(2)}) collective-permute-start(f32[1024,512]{1,0:T(8,128)} %get-tuple-element.10), channel_id=1, source_target_pairs={{0,1},{1,0},{2,3},{3,2},{4,5},{5,4},{6,7},{7,6},{8,9},{9,8},{10,11... | collective-permute-start | bytes 6291464 | tf_op jit(solution)/shard_map/ppermute | solution.py:209
  18.2 0.1 compare_select_fusion.1
  18.3 0.1 reshape.210
  18.4 0.0 copy-start.6
  18.4 0.0 copy-start.2
  18.4 0.0 copy-start.5
  18.4 3.1 %gather_fusion = s32[512]{0:T(512)S(1)} fusion(s32[8192]{0:T(1024)S(1)} %bitcast.98, s32[1024]{0:T(1024)S(1)} %pad_clamp_fusion.1), kind=kCustom, calls=%fused_computation | custom fusion | bytes 6144 | tf_op jit(solution)/shard_map/jit(_take)/gather | solution.py:256
  21.6 0.1 reshape.209
  21.7 0.1 iota_compare_fusion.1
  21.7 0.7 fusion.11
  22.4 9.6 %all-to-all-start.2 = ((s32[16,1,32]{2,1,0:T(1,128)}), s32[16,1,32]{2,1,0:T(1,128)S(1)}, u32[]{:S(2)}, u32[]{:S(2)}) async-start(s32[16,1,32]{2,1,0:T(1,128)} %bitcast.34), calls=%async_computation.2 | async-start | bytes 16384 | tf_op jit(solution)/shard_map/all_to_all | solution.py:258
  32.0 0.6 reshape.205.batch_ref
  32.6 0.1 reshape_squeeze.3
  32.7 0.5 iota_add_fusion.1.order
  33.2 6.7 %forward_second.1 = (f32[1024,512]{1,0:T(8,128)}, bf16[512,1024]{1,0:T(8,128)(2,1)}) custom-call(s32[2]{0:T(128)} %iota_add_fusion.1.order, bf16[1024,1024]{1,0:T(8,128)(2,1)} %get-tuple-element.8.inputs_ref, f32[1,1024]{1,0:T(1,128)} %bitcast.119, f32[1,1024]{1,0:T(1,128)} %bitcast.121, bf16[1024,1024]{1,0:T(8,128)(2,1)} %w_b.1), custom_call_target="tpu_custom_call" | custom-call | tf_op jit(solution)/shard_map/forward_second/pallas_call | solution.py:94
  40.0 0.7 pad_add_fusion.where
  40.6 10.3 %backward.1 = f32[256,384]{1,0:T(8,128)} custom-call(s32[258]{0:T(512)} %pad_add_fusion.where, f32[256,384]{1,0:T(8,128)} %bitcast.107, s32[4,2,1024]{2,1,0:T(2,128)} %reshape.205.batch_ref, bf16[512,1024]{1,0:T(8,128)(2,1)} %get-tuple-element.11.delta_a, bf16[512,1024]{1,0:T(8,128)(2,1)} %get-tuple-element.12.delta_b, bf16[1024,1024]{1,0:T(8,128)(2,1)} %w_b.1, ...), custom_call_target="tpu_custom_call" | custom-call | tf_op jit(solution)/shard_map/backward/pallas_call | solution.py:159
  51.0 2.1 %add.127 = f32[1024,512]{1,0:T(8,128)S(1)} add(f32[1024,512]{1,0:T(8,128)} %get-tuple-element.9, f32[1024,512]{1,0:T(8,128)S(1)} %collective-permute-done) | non-fusion elementwise | flops 524288 | bytes 6291456 | tf_op jit(solution)/shard_map/add | solution.py:209
  53.0 0.2 fusion.12
  53.2 0.9 dynamic-slice_bitcast_fusion.5
  54.1 3.1 %collective-permute-start.1 = (f32[16,4,8,128]{3,2,1,0:T(8,128)}, f32[16,4,8,128]{3,2,1,0:T(8,128)}, u32[]{:S(2)}, u32[]{:S(2)}) collective-permute-start(f32[16,4,8,128]{3,2,1,0:T(8,128)} %get-tuple-element.15), channel_id=1, source_target_pairs={{0,8},{1,9},{2,10},{3,11},{4,12},{5,13},{6,14},{7,15},{8,16},{9,17... | collective-permute-start | bytes 786440 | tf_op jit(solution)/shard_map/ppermute | solution.py:200
  57.3 4.4 %collective-permute-start.2 = (f32[16,4,8,128]{3,2,1,0:T(8,128)}, f32[16,4,8,128]{3,2,1,0:T(8,128)}, u32[]{:S(2)}, u32[]{:S(2)}) collective-permute-start(f32[16,4,8,128]{3,2,1,0:T(8,128)} %get-tuple-element.16), channel_id=1, source_target_pairs={{0,16},{1,17},{2,18},{3,19},{4,20},{5,21},{6,22},{7,23},{8,24},{9,... | collective-permute-start | bytes 786440 | tf_op jit(solution)/shard_map/ppermute | solution.py:200
  61.6 3.1 %collective-permute-start.3 = (f32[16,4,8,128]{3,2,1,0:T(8,128)}, f32[16,4,8,128]{3,2,1,0:T(8,128)}, u32[]{:S(2)}, u32[]{:S(2)}) collective-permute-start(f32[16,4,8,128]{3,2,1,0:T(8,128)} %get-tuple-element.17), channel_id=1, source_target_pairs={{0,24},{1,25},{2,26},{3,27},{4,28},{5,29},{6,30},{7,31},{8,0},{9,1... | collective-permute-start | bytes 786440 | tf_op jit(solution)/shard_map/ppermute | solution.py:200
  64.7 11.5 %all-to-all-start.3 = ((f32[16,16,384]{2,1,0:T(8,128)}), f32[16,16,384]{2,1,0:T(8,128)S(1)}, u32[]{:S(2)}, u32[]{:S(2)}) async-start(f32[16,16,384]{2,1,0:T(8,128)} %bitcast.105), calls=%async_computation.3 | async-start | bytes 786432 | tf_op jit(solution)/shard_map/all_to_all | solution.py:272
  76.2 0.1 compare_select_fusion
  76.3 0.1 reshape.218
  76.3 0.1 dynamic-slice_bitcast_fusion.2
  76.4 3.2 %collective-permute-start.7 = (f32[16,8,4,128]{3,1,2,0:T(8,128)S(1)}, f32[16,8,4,128]{3,1,2,0:T(8,128)S(1)}, u32[]{:S(2)}, u32[]{:S(2)}) collective-permute-start(f32[16,8,4,128]{3,1,2,0:T(8,128)S(1)} %get-tuple-element.18), channel_id=1, source_target_pairs={{0,2},{1,3},{2,4},{3,5},{4,6},{5,7},{6,0},{7,1},{8,10},{9,11},{10,... | collective-permute-start | bytes 786440 | tf_op jit(solution)/shard_map/ppermute | solution.py:200
  79.6 4.5 %collective-permute-start.8 = (f32[16,8,4,128]{3,1,2,0:T(8,128)S(1)}, f32[16,8,4,128]{3,1,2,0:T(8,128)S(1)}, u32[]{:S(2)}, u32[]{:S(2)}) collective-permute-start(f32[16,8,4,128]{3,1,2,0:T(8,128)S(1)} %get-tuple-element.20), channel_id=1, source_target_pairs={{0,4},{1,5},{2,6},{3,7},{4,0},{5,1},{6,2},{7,3},{8,12},{9,13},{10,... | collective-permute-start | bytes 786440 | tf_op jit(solution)/shard_map/ppermute | solution.py:200
  84.2 3.0 %collective-permute-start.9 = (f32[16,8,4,128]{3,1,2,0:T(8,128)S(1)}, f32[16,8,4,128]{3,1,2,0:T(8,128)S(1)}, u32[]{:S(2)}, u32[]{:S(2)}) collective-permute-start(f32[16,8,4,128]{3,1,2,0:T(8,128)S(1)} %get-tuple-element.19), channel_id=1, source_target_pairs={{0,6},{1,7},{2,0},{3,1},{4,2},{5,3},{6,4},{7,5},{8,14},{9,15},{10,... | collective-permute-start | bytes 786440 | tf_op jit(solution)/shard_map/ppermute | solution.py:200
  87.2 0.0 collective-permute-done.2
  87.2 0.0 collective-permute-done.3
  87.2 1.2 fusion.1
  88.4 2.3 %collective-permute-start.4 = (f32[16,8,128]{2,1,0:T(8,128)S(1)}, f32[16,8,128]{2,1,0:T(8,128)S(1)}, u32[]{:S(2)}, u32[]{:S(2)}) collective-permute-start(f32[16,8,128]{2,1,0:T(8,128)S(1)} %get-tuple-element.21), channel_id=1, source_target_pairs={{0,2},{1,3},{2,4},{3,5},{4,6},{5,7},{6,0},{7,1},{8,10},{9,11},{10,... | collective-permute-start | bytes 196616 | tf_op jit(solution)/shard_map/ppermute | solution.py:200
  90.7 2.7 %collective-permute-start.5 = (f32[16,8,128]{2,1,0:T(8,128)S(1)}, f32[16,8,128]{2,1,0:T(8,128)S(1)}, u32[]{:S(2)}, u32[]{:S(2)}) collective-permute-start(f32[16,8,128]{2,1,0:T(8,128)S(1)} %get-tuple-element.23), channel_id=1, source_target_pairs={{0,4},{1,5},{2,6},{3,7},{4,0},{5,1},{6,2},{7,3},{8,12},{9,13},{10,... | collective-permute-start | bytes 196616 | tf_op jit(solution)/shard_map/ppermute | solution.py:200
  93.5 3.5 %collective-permute-start.6 = (f32[16,8,128]{2,1,0:T(8,128)S(1)}, f32[16,8,128]{2,1,0:T(8,128)S(1)}, u32[]{:S(2)}, u32[]{:S(2)}) collective-permute-start(f32[16,8,128]{2,1,0:T(8,128)S(1)} %get-tuple-element.22), channel_id=1, source_target_pairs={{0,6},{1,7},{2,0},{3,1},{4,2},{5,3},{6,4},{7,5},{8,14},{9,15},{10,... | collective-permute-start | bytes 196616 | tf_op jit(solution)/shard_map/ppermute | solution.py:200
  97.0 0.0 collective-permute-done.8
  97.0 0.1 fusion.3
  97.1 2.2 %collective-permute-start.10 = (f32[16,8,128]{2,1,0:T(8,128)S(1)}, f32[16,8,128]{2,1,0:T(8,128)S(1)}, u32[]{:S(2)}, u32[]{:S(2)}) collective-permute-start(f32[16,8,128]{2,1,0:T(8,128)S(1)} %get-tuple-element.24), channel_id=1, source_target_pairs={{0,8},{1,9},{2,10},{3,11},{4,12},{5,13},{6,14},{7,15},{8,16},{9,17... | collective-permute-start | bytes 196616 | tf_op jit(solution)/shard_map/ppermute | solution.py:200
  99.4 2.8 %collective-permute-start.11 = (f32[16,8,128]{2,1,0:T(8,128)S(1)}, f32[16,8,128]{2,1,0:T(8,128)S(1)}, u32[]{:S(2)}, u32[]{:S(2)}) collective-permute-start(f32[16,8,128]{2,1,0:T(8,128)S(1)} %get-tuple-element.26), channel_id=1, source_target_pairs={{0,16},{1,17},{2,18},{3,19},{4,20},{5,21},{6,22},{7,23},{8,24},{9,... | collective-permute-start | bytes 196616 | tf_op jit(solution)/shard_map/ppermute | solution.py:200
  102.2 3.4 %collective-permute-start.12 = (f32[16,8,128]{2,1,0:T(8,128)S(1)}, f32[16,8,128]{2,1,0:T(8,128)S(1)}, u32[]{:S(2)}, u32[]{:S(2)}) collective-permute-start(f32[16,8,128]{2,1,0:T(8,128)S(1)} %get-tuple-element.25), channel_id=1, source_target_pairs={{0,24},{1,25},{2,26},{3,27},{4,28},{5,29},{6,30},{7,31},{8,0},{9,1... | collective-permute-start | bytes 196616 | tf_op jit(solution)/shard_map/ppermute | solution.py:200
  105.7 0.2 collective-permute-done.11
  105.9 1.9 %collective-permute-done.12 = f32[16,8,128]{2,1,0:T(8,128)S(1)} collective-permute-done((f32[16,8,128]{2,1,0:T(8,128)S(1)}, f32[16,8,128]{2,1,0:T(8,128)S(1)}, u32[]{:S(2)}, u32[]{:S(2)}) %collective-permute-start.12) | collective-permute-done | bytes 65568 | tf_op jit(solution)/shard_map/ppermute | solution.py:200
  107.8 0.7 pad_maximum_fusion
  108.5 11.5 %all-to-all-start = ((f32[16,2,8,128]{3,2,1,0:T(8,128)}), f32[16,2,8,128]{3,2,1,0:T(8,128)S(1)}, u32[]{:S(2)}, u32[]{:S(2)}) async-start(f32[16,2,8,128]{3,2,1,0:T(8,128)} %pad_maximum_fusion), calls=%async_computation | async-start | bytes 262144 | tf_op jit(solution)/shard_map/all_to_all | solution.py:218
  120.0 0.0 copy-start.7
  120.0 1.0 gather_fusion.1
  121.0 0.8 broadcast_select_fusion
  121.8 10.1 %all-to-all-done = f32[16,2,8,128]{3,2,1,0:T(8,128)S(1)} async-done(((f32[16,2,8,128]{3,2,1,0:T(8,128)}), f32[16,2,8,128]{3,2,1,0:T(8,128)S(1)}, u32[]{:S(2)}, u32[]{:S(2)}) %all-to-all-start) | async-done | bytes 131104 | tf_op jit(solution)/shard_map/all_to_all | solution.py:218
  131.9 4.0 %all-to-all-start.4 = ((f32[16,16,384]{2,1,0:T(8,128)}), f32[16,16,384]{2,1,0:T(8,128)S(1)}, u32[]{:S(2)}, u32[]{:S(2)}) async-start(f32[16,16,384]{2,1,0:T(8,128)} %broadcast_select_fusion), calls=%async_computation.4 | async-start | bytes 786432 | tf_op jit(solution)/shard_map/all_to_all | solution.py:262
  136.0 0.1 iota_compare_fusion
  136.1 0.1 reshape.204
  136.2 14.5 %all-to-all-done.4 = f32[16,16,384]{2,1,0:T(8,128)S(1)} async-done(((f32[16,16,384]{2,1,0:T(8,128)}), f32[16,16,384]{2,1,0:T(8,128)S(1)}, u32[]{:S(2)}, u32[]{:S(2)}) %all-to-all-start.4) | async-done | bytes 393248 | tf_op jit(solution)/shard_map/all_to_all | solution.py:262
  150.7 0.7 broadcast_in_dim.52
  151.4 15.4 %all-to-all-start.1 = ((f32[32,2,8,128]{3,2,1,0:T(8,128)}), f32[32,2,8,128]{3,2,1,0:T(8,128)S(1)}, u32[]{:S(2)}, u32[]{:S(2)}) async-start(f32[32,2,8,128]{3,2,1,0:T(8,128)} %broadcast_in_dim.52), calls=%async_computation.1 | async-start | bytes 524288 | tf_op jit(solution)/shard_map/all_to_all | solution.py:278
  166.8 1.7 scatter_fusion
  168.6 0.0 copy-start.1
  168.6 1.0 select_bitcast_fusion
  169.5 6.2 %all-to-all-done.1 = f32[32,2,8,128]{3,2,1,0:T(8,128)S(1)} async-done(((f32[32,2,8,128]{3,2,1,0:T(8,128)}), f32[32,2,8,128]{3,2,1,0:T(8,128)S(1)}, u32[]{:S(2)}, u32[]{:S(2)}) %all-to-all-start.1) | async-done | bytes 262176 | tf_op jit(solution)/shard_map/all_to_all | solution.py:278
  175.8 0.7 copy.18
  (30 shorter events, 0.2 us)
Async XLA Ops:
  0.6 17.8 %copy-start = (s32[1,8192]{1,0:T(1,128)S(1)}, s32[1,8192]{1,0:T(1,128)}, u32[]{:S(2)}) copy-start(s32[1,8192]{1,0:T(1,128)} %param.18) | copy-start | bytes 98308
  0.6 17.5 %copy-start.4 = (s32[1,1,16,16]{3,2,1,0:T(8,128)S(1)}, s32[1,1,16,16]{3,2,1,0:T(8,128)}, u32[]{:S(2)}) copy-start(s32[1,1,16,16]{3,2,1,0:T(8,128)} %param.19) | copy-start | bytes 3076
  0.7 17.5 %copy-start.3 = (s32[1,1,16,16]{3,2,1,0:T(8,128)S(1)}, s32[1,1,16,16]{3,2,1,0:T(8,128)}, u32[]{:S(2)}) copy-start(s32[1,1,16,16]{3,2,1,0:T(8,128)} %param.21) | copy-start | bytes 3076
  9.4 41.5 %collective-permute-start = (f32[1024,512]{1,0:T(8,128)}, f32[1024,512]{1,0:T(8,128)S(1)}, u32[]{:S(2)}, u32[]{:S(2)}) collective-permute-start(f32[1024,512]{1,0:T(8,128)} %get-tuple-element.10), channel_id=1, source_target_pairs={{0,1},{1,0},{2,3},{3,2},{4,5},{5,4},{6,7},{7,6},{8,9},{9,8},{10,11... | collective-permute-start | bytes 6291464 | tf_op jit(solution)/shard_map/ppermute | solution.py:209
  18.4 3.3 %copy-start.6 = (s32[1,1,16]{2,1,0:T(1,128)S(1)}, s32[1,1,16]{2,1,0:T(1,128)}, u32[]{:S(2)}) copy-start(s32[1,1,16]{2,1,0:T(1,128)} %param.23) | copy-start | bytes 196
  18.4 13.6 %copy-start.2 = (s32[1,1,1024,8]{2,3,1,0:T(8,128)S(1)}, s32[1,1,1024,8]{2,3,1,0:T(8,128)}, u32[]{:S(2)}) copy-start(s32[1,1,1024,8]{2,3,1,0:T(8,128)} %param.14) | copy-start | bytes 98308
  18.4 14.2 %copy-start.5 = (s32[1,1,16,16]{3,2,1,0:T(8,128)S(1)}, s32[1,1,16,16]{3,2,1,0:T(8,128)}, u32[]{:S(2)}) copy-start(s32[1,1,16,16]{3,2,1,0:T(8,128)} %param.22) | copy-start | bytes 3076
  22.4 42.3 %all-to-all-start.2 = ((s32[16,1,32]{2,1,0:T(1,128)}), s32[16,1,32]{2,1,0:T(1,128)S(1)}, u32[]{:S(2)}, u32[]{:S(2)}) async-start(s32[16,1,32]{2,1,0:T(1,128)} %bitcast.34), calls=%async_computation.2 | async-start | bytes 16384 | tf_op jit(solution)/shard_map/all_to_all | solution.py:258
  54.1 30.0 %collective-permute-start.1 = (f32[16,4,8,128]{3,2,1,0:T(8,128)}, f32[16,4,8,128]{3,2,1,0:T(8,128)}, u32[]{:S(2)}, u32[]{:S(2)}) collective-permute-start(f32[16,4,8,128]{3,2,1,0:T(8,128)} %get-tuple-element.15), channel_id=1, source_target_pairs={{0,8},{1,9},{2,10},{3,11},{4,12},{5,13},{6,14},{7,15},{8,16},{9,17... | collective-permute-start | bytes 786440 | tf_op jit(solution)/shard_map/ppermute | solution.py:200
  57.3 29.9 %collective-permute-start.2 = (f32[16,4,8,128]{3,2,1,0:T(8,128)}, f32[16,4,8,128]{3,2,1,0:T(8,128)}, u32[]{:S(2)}, u32[]{:S(2)}) collective-permute-start(f32[16,4,8,128]{3,2,1,0:T(8,128)} %get-tuple-element.16), channel_id=1, source_target_pairs={{0,16},{1,17},{2,18},{3,19},{4,20},{5,21},{6,22},{7,23},{8,24},{9,... | collective-permute-start | bytes 786440 | tf_op jit(solution)/shard_map/ppermute | solution.py:200
  61.6 25.5 %collective-permute-start.3 = (f32[16,4,8,128]{3,2,1,0:T(8,128)}, f32[16,4,8,128]{3,2,1,0:T(8,128)}, u32[]{:S(2)}, u32[]{:S(2)}) collective-permute-start(f32[16,4,8,128]{3,2,1,0:T(8,128)} %get-tuple-element.17), channel_id=1, source_target_pairs={{0,24},{1,25},{2,26},{3,27},{4,28},{5,29},{6,30},{7,31},{8,0},{9,1... | collective-permute-start | bytes 786440 | tf_op jit(solution)/shard_map/ppermute | solution.py:200
  64.7 43.8 %all-to-all-start.3 = ((f32[16,16,384]{2,1,0:T(8,128)}), f32[16,16,384]{2,1,0:T(8,128)S(1)}, u32[]{:S(2)}, u32[]{:S(2)}) async-start(f32[16,16,384]{2,1,0:T(8,128)} %bitcast.105), calls=%async_computation.3 | async-start | bytes 786432 | tf_op jit(solution)/shard_map/all_to_all | solution.py:272
  76.4 17.0 %collective-permute-start.7 = (f32[16,8,4,128]{3,1,2,0:T(8,128)S(1)}, f32[16,8,4,128]{3,1,2,0:T(8,128)S(1)}, u32[]{:S(2)}, u32[]{:S(2)}) collective-permute-start(f32[16,8,4,128]{3,1,2,0:T(8,128)S(1)} %get-tuple-element.18), channel_id=1, source_target_pairs={{0,2},{1,3},{2,4},{3,5},{4,6},{5,7},{6,0},{7,1},{8,10},{9,11},{10,... | collective-permute-start | bytes 786440 | tf_op jit(solution)/shard_map/ppermute | solution.py:200
  79.6 17.4 %collective-permute-start.8 = (f32[16,8,4,128]{3,1,2,0:T(8,128)S(1)}, f32[16,8,4,128]{3,1,2,0:T(8,128)S(1)}, u32[]{:S(2)}, u32[]{:S(2)}) collective-permute-start(f32[16,8,4,128]{3,1,2,0:T(8,128)S(1)} %get-tuple-element.20), channel_id=1, source_target_pairs={{0,4},{1,5},{2,6},{3,7},{4,0},{5,1},{6,2},{7,3},{8,12},{9,13},{10,... | collective-permute-start | bytes 786440 | tf_op jit(solution)/shard_map/ppermute | solution.py:200
  84.2 12.8 %collective-permute-start.9 = (f32[16,8,4,128]{3,1,2,0:T(8,128)S(1)}, f32[16,8,4,128]{3,1,2,0:T(8,128)S(1)}, u32[]{:S(2)}, u32[]{:S(2)}) collective-permute-start(f32[16,8,4,128]{3,1,2,0:T(8,128)S(1)} %get-tuple-element.19), channel_id=1, source_target_pairs={{0,6},{1,7},{2,0},{3,1},{4,2},{5,3},{6,4},{7,5},{8,14},{9,15},{10,... | collective-permute-start | bytes 786440 | tf_op jit(solution)/shard_map/ppermute | solution.py:200
  88.4 13.8 %collective-permute-start.4 = (f32[16,8,128]{2,1,0:T(8,128)S(1)}, f32[16,8,128]{2,1,0:T(8,128)S(1)}, u32[]{:S(2)}, u32[]{:S(2)}) collective-permute-start(f32[16,8,128]{2,1,0:T(8,128)S(1)} %get-tuple-element.21), channel_id=1, source_target_pairs={{0,2},{1,3},{2,4},{3,5},{4,6},{5,7},{6,0},{7,1},{8,10},{9,11},{10,... | collective-permute-start | bytes 196616 | tf_op jit(solution)/shard_map/ppermute | solution.py:200
  90.7 14.9 %collective-permute-start.5 = (f32[16,8,128]{2,1,0:T(8,128)S(1)}, f32[16,8,128]{2,1,0:T(8,128)S(1)}, u32[]{:S(2)}, u32[]{:S(2)}) collective-permute-start(f32[16,8,128]{2,1,0:T(8,128)S(1)} %get-tuple-element.23), channel_id=1, source_target_pairs={{0,4},{1,5},{2,6},{3,7},{4,0},{5,1},{6,2},{7,3},{8,12},{9,13},{10,... | collective-permute-start | bytes 196616 | tf_op jit(solution)/shard_map/ppermute | solution.py:200
  93.5 12.2 %collective-permute-start.6 = (f32[16,8,128]{2,1,0:T(8,128)S(1)}, f32[16,8,128]{2,1,0:T(8,128)S(1)}, u32[]{:S(2)}, u32[]{:S(2)}) collective-permute-start(f32[16,8,128]{2,1,0:T(8,128)S(1)} %get-tuple-element.22), channel_id=1, source_target_pairs={{0,6},{1,7},{2,0},{3,1},{4,2},{5,3},{6,4},{7,5},{8,14},{9,15},{10,... | collective-permute-start | bytes 196616 | tf_op jit(solution)/shard_map/ppermute | solution.py:200
  97.1 8.5 %collective-permute-start.10 = (f32[16,8,128]{2,1,0:T(8,128)S(1)}, f32[16,8,128]{2,1,0:T(8,128)S(1)}, u32[]{:S(2)}, u32[]{:S(2)}) collective-permute-start(f32[16,8,128]{2,1,0:T(8,128)S(1)} %get-tuple-element.24), channel_id=1, source_target_pairs={{0,8},{1,9},{2,10},{3,11},{4,12},{5,13},{6,14},{7,15},{8,16},{9,17... | collective-permute-start | bytes 196616 | tf_op jit(solution)/shard_map/ppermute | solution.py:200
  99.4 6.5 %collective-permute-start.11 = (f32[16,8,128]{2,1,0:T(8,128)S(1)}, f32[16,8,128]{2,1,0:T(8,128)S(1)}, u32[]{:S(2)}, u32[]{:S(2)}) collective-permute-start(f32[16,8,128]{2,1,0:T(8,128)S(1)} %get-tuple-element.26), channel_id=1, source_target_pairs={{0,16},{1,17},{2,18},{3,19},{4,20},{5,21},{6,22},{7,23},{8,24},{9,... | collective-permute-start | bytes 196616 | tf_op jit(solution)/shard_map/ppermute | solution.py:200
  102.2 5.6 %collective-permute-start.12 = (f32[16,8,128]{2,1,0:T(8,128)S(1)}, f32[16,8,128]{2,1,0:T(8,128)S(1)}, u32[]{:S(2)}, u32[]{:S(2)}) collective-permute-start(f32[16,8,128]{2,1,0:T(8,128)S(1)} %get-tuple-element.25), channel_id=1, source_target_pairs={{0,24},{1,25},{2,26},{3,27},{4,28},{5,29},{6,30},{7,31},{8,0},{9,1... | collective-permute-start | bytes 196616 | tf_op jit(solution)/shard_map/ppermute | solution.py:200
  108.5 23.4 %all-to-all-start = ((f32[16,2,8,128]{3,2,1,0:T(8,128)}), f32[16,2,8,128]{3,2,1,0:T(8,128)S(1)}, u32[]{:S(2)}, u32[]{:S(2)}) async-start(f32[16,2,8,128]{3,2,1,0:T(8,128)} %pad_maximum_fusion), calls=%async_computation | async-start | bytes 262144 | tf_op jit(solution)/shard_map/all_to_all | solution.py:218
  120.0 16.0 %copy-start.7 = (s32[1,1,16]{2,1,0:T(1,128)S(1)}, s32[1,1,16]{2,1,0:T(1,128)}, u32[]{:S(2)}) copy-start(s32[1,1,16]{2,1,0:T(1,128)} %param.20) | copy-start | bytes 196
  131.9 18.8 %all-to-all-start.4 = ((f32[16,16,384]{2,1,0:T(8,128)}), f32[16,16,384]{2,1,0:T(8,128)S(1)}, u32[]{:S(2)}, u32[]{:S(2)}) async-start(f32[16,16,384]{2,1,0:T(8,128)} %broadcast_select_fusion), calls=%async_computation.4 | async-start | bytes 786432 | tf_op jit(solution)/shard_map/all_to_all | solution.py:262
  151.4 24.3 %all-to-all-start.1 = ((f32[32,2,8,128]{3,2,1,0:T(8,128)}), f32[32,2,8,128]{3,2,1,0:T(8,128)S(1)}, u32[]{:S(2)}, u32[]{:S(2)}) async-start(f32[32,2,8,128]{3,2,1,0:T(8,128)} %broadcast_in_dim.52), calls=%async_computation.1 | async-start | bytes 524288 | tf_op jit(solution)/shard_map/all_to_all | solution.py:278
  168.6 7.9 %copy-start.1 = (f32[512,384]{1,0:T(8,128)}, f32[512,384]{1,0:T(8,128)S(1)}, u32[]{:S(2)}) copy-start(f32[512,384]{1,0:T(8,128)S(1)} %scatter_fusion) | copy-start | bytes 2359300

commit v2 on v1

v2 whole, which is shorter than its diff:
```python
import math

import jax
import jax.numpy as jnp
from jax import lax
from jax.experimental import pallas as pl
from jax.experimental.pallas import tpu as pltpu
from jax.sharding import PartitionSpec as P


beta_one = 0.9
beta_two = 0.999
learn_rate = 0.05
epsilon = 1e-08
bias_one = 1.0 - 0.9**10
bias_two = 1.0 - 0.999**10
NN = (((1,), (0,)), ((), ()))
NT = (((1,), (1,)), ((), ()))
TN = (((0,), (0,)), ((), ()))
side = 4


def full(shape):
    return pl.BlockSpec(shape, lambda j, o: tuple(0 for _ in shape))


def column(row):
    return jnp.transpose(jnp.broadcast_to(row, (8, row.shape[1])))[:, :1]


def onehot(batch_row, rows):
    shape = (rows, batch_row.shape[1])
    hit = lax.broadcasted_iota(jnp.int32, shape, 0) == batch_row
    return hit.astype(jnp.float32).astype(jnp.bfloat16)


def hidden(inputs, loss, head, w, delta_ref):
    pre = lax.dot_general(w, inputs, TN, preferred_element_type=jnp.float32)
    sigma = jax.nn.sigmoid(pre)
    delta = (loss * column(head) * sigma * (1.0 + pre * (1.0 - sigma))).astype(jnp.bfloat16)
    delta_ref[...] = delta
    return lax.dot_general(inputs, delta, NT, preferred_element_type=jnp.float32)


def store_pieces(grad, grad_ref, plus_ref):
    across, down, owners, rows, columns = grad_ref.shape
    for x in range(across):
        for y in range(down):
            for z in range(owners):
                top = (z * down + y) * rows
                piece = grad[top : top + rows, x * columns : (x + 1) * columns]
                grad_ref[x, y, z] = piece if plus_ref is None else piece + plus_ref[x, y, z]


def first_kernel(cores, cache_ref, batch_ref, loss_ref, head_ref, w_ref, grad_ref, delta_ref, inputs_ref):
    rows = cache_ref.shape[0]
    features = batch_ref.shape[0]
    embed = inputs_ref.shape[0] // features

    @pl.when(pl.program_id(0) == 0)
    def _():
        looked = jnp.transpose(cache_ref[...]).astype(jnp.bfloat16)
        for f in range(features):
            pick = onehot(batch_ref[f : f + 1, :], rows)
            inputs_ref[f * embed : (f + 1) * embed, :] = lax.dot_general(
                looked, pick, NN, preferred_element_type=jnp.float32
            ).astype(jnp.bfloat16)

    grad = hidden(inputs_ref[...], loss_ref[...], head_ref[...], w_ref[...], delta_ref)
    store_pieces(grad, grad_ref, None)


def second_kernel(cores, plus_ref, inputs_ref, loss_ref, head_ref, w_ref, grad_ref, delta_ref):
    grad = hidden(inputs_ref[...], loss_ref[...], head_ref[...], w_ref[...], delta_ref)
    store_pieces(grad, grad_ref, plus_ref)


def forward_half(cores, owners, cache, batch_t, partner, inputs, loss, head, w):
    samples = loss.shape[1]
    width = w.shape[0]
    half = width // 2
    steps = 2
    block = half // steps
    here = 0 if inputs is None else 1
    tail_specs = [
        full((1, samples)),
        pl.BlockSpec((1, block), lambda j, c: (0, steps * c[here] + j)),
        pl.BlockSpec((width, block), lambda j, c: (0, steps * c[here] + j)),
    ]
    pieces = (side, side, owners, width // (owners * side), half // side)
    grad = jax.ShapeDtypeStruct(pieces, jnp.float32)
    delta = jax.ShapeDtypeStruct((half, samples), jnp.bfloat16)
    grad_spec = pl.BlockSpec((side // steps,) + pieces[1:], lambda j, c: (j, 0, 0, 0, 0))
    delta_spec = pl.BlockSpec((block, samples), lambda j, c: (j, 0))
    if inputs is None:
        rows = cache.shape[0]
        embed = cache.shape[1] // 3
        return pl.pallas_call(
            first_kernel,
            out_shape=(grad, delta, jax.ShapeDtypeStruct((width, samples), jnp.bfloat16)),
            grid_spec=pltpu.PrefetchScalarGridSpec(
                num_scalar_prefetch=1,
                grid=(steps,),
                in_specs=[pl.BlockSpec((rows, embed), lambda j, c: (0, 0)), full(batch_t.shape)] + tail_specs,
                out_specs=(grad_spec, delta_spec, full((width, samples))),
            ),
            name="forward_first",
        )(cores, cache, batch_t, loss, head, w)
    return pl.pallas_call(
        second_kernel,
        out_shape=(grad, delta),
        grid_spec=pltpu.PrefetchScalarGridSpec(
            num_scalar_prefetch=1,
            grid=(steps,),
            in_specs=[grad_spec, full((width, samples))] + tail_specs,
            out_specs=(grad_spec, delta_spec),
        ),
        name="forward_second",
    )(cores, partner, inputs, loss, head, w)


def backward_kernel(
    cores, asked, leaving, cache_ref, table_ref, batch_ref, delta_a, delta_b, w_a, w_b, sent_ref, acc_ref, upd_ref
):
    rows, width = cache_ref.shape
    embed = width // 3
    owners, capacity = leaving.shape
    step = pl.program_id(0)
    back = lax.dot_general(w_a[...], delta_a[...], NN, preferred_element_type=jnp.float32)
    back += lax.dot_general(w_b[...], delta_b[...], NN, preferred_element_type=jnp.float32)
    total = None
    for k in range(w_a.shape[0] // embed):
        part = back[k * embed : (k + 1) * embed]
        high = part.astype(jnp.bfloat16)
        low = (part - high.astype(jnp.float32)).astype(jnp.bfloat16)
        pick = onehot(batch_ref[pl.ds(step * (w_a.shape[0] // embed) + k, 1), :], rows)
        add = lax.dot_general(jnp.concatenate([high, low], 0), pick, NT, preferred_element_type=jnp.float32)
        total = add if total is None else total + add

    @pl.when(step == 0)
    def _():
        acc_ref[...] = total

        def fetch(i, carry):
            for k in range(capacity):
                row = table_ref[pl.ds(asked[i, k], 1), :]
                for p in range(3):
                    at = p * capacity + k
                    sent_ref[i, at : at + 1, :] = row[:, p * embed : (p + 1) * embed]
            return carry

        lax.fori_loop(0, owners, fetch, 0)

    @pl.when(step > 0)
    def _():
        acc_ref[...] += total

    @pl.when(step == pl.num_programs(0) - 1)
    def _():
        grads = jnp.transpose(acc_ref[:embed, :] + acc_ref[embed:, :])
        value = cache_ref[:, :embed]
        first = cache_ref[:, embed : 2 * embed]
        second = cache_ref[:, 2 * embed :]
        first = beta_one * first + (1.0 - beta_one) * grads
        second = beta_two * second + (1.0 - beta_two) * grads * grads
        upd_ref[:, :embed] = value - learn_rate * (first / bias_one) / (jnp.sqrt(second / bias_two) + epsilon)
        upd_ref[:, embed : 2 * embed] = first
        upd_ref[:, 2 * embed :] = second

        def evict(i, carry):
            for k in range(capacity):
                row = upd_ref[pl.ds(leaving[i, k], 1), :]
                for p in range(3):
                    at = (3 + p) * capacity + k
                    sent_ref[i, at : at + 1, :] = row[:, p * embed : (p + 1) * embed]
            return carry

        lax.fori_loop(0, owners, evict, 0)


def backward(cores, asked, leaving, cache, table, batch_t, delta_a, delta_b, w):
    rows, width3 = cache.shape
    embed = width3 // 3
    features, samples = batch_t.shape
    width = w.shape[0]
    half = width // 2
    steps = features // 2
    owners, capacity = leaving.shape
    fixed = lambda shape: pl.BlockSpec(shape, lambda j, c, a, e: tuple(0 for _ in shape))
    return pl.pallas_call(
        backward_kernel,
        out_shape=jax.ShapeDtypeStruct((owners, 7 * capacity, embed), jnp.float32),
        grid_spec=pltpu.PrefetchScalarGridSpec(
            num_scalar_prefetch=3,
            grid=(steps,),
            in_specs=[
                fixed(cache.shape),
                fixed(table.shape),
                fixed(batch_t.shape),
                fixed((half, samples)),
                fixed((half, samples)),
                pl.BlockSpec((2 * embed, half), lambda j, c, a, e: (j, c[0])),
                pl.BlockSpec((2 * embed, half), lambda j, c, a, e: (j, c[1])),
            ],
            out_specs=fixed((owners, 6 * capacity, embed)),
            scratch_shapes=[pltpu.VMEM((2 * embed, rows), jnp.float32), pltpu.VMEM((rows, width3), jnp.float32)],
        ),
        name="backward",
    )(cores, asked, leaving, cache, table, batch_t, delta_a, delta_b, w, w)


def total_kernel(pieces_ref, sent_ref, out_ref):
    total = pieces_ref[0]
    for i in range(1, pieces_ref.shape[0]):
        total += pieces_ref[i]
    out_ref[...] = total


def add_total(pieces, sent):
    count, owners, rows, columns = pieces.shape
    step = owners // 4
    return pl.pallas_call(
        total_kernel,
        out_shape=jax.ShapeDtypeStruct(sent.shape, sent.dtype),
        grid=(owners // step,),
        in_specs=[
            pl.BlockSpec((count, step, rows, columns), lambda j: (0, j, 0, 0)),
            pl.BlockSpec(memory_space=pl.ANY),
        ],
        out_specs=pl.BlockSpec((step, rows, columns), lambda j: (j, sent.shape[1] // rows - 1, 0)),
        input_output_aliases={1: 0},
        name="total",
    )(pieces, sent)


def swap_pairs():
    return [(d, d ^ 1) for d in range(2 * side * side)]


def planes():
    return [[2 * chip + c for chip in range(side * side)] for c in range(2)]


def local(
    cache_state,
    table_state,
    batch_idx,
    loss_grad,
    w_first,
    head,
    home,
    fetch_rows,
    fetch_counts,
    evict_rows,
    evict_from,
    evict_counts,
):
    group = lax.axis_size("shard")
    devices = lax.axis_size("dp")
    place = lax.axis_index("dp").astype(jnp.uint32)
    core = (place & 1).astype(jnp.int32)
    cache = cache_state[0, 0]
    table = table_state[0, 0]
    batch_t = batch_idx[0, 0].T
    loss = loss_grad[0]
    home_map = home[0]
    wanted = fetch_rows[0, 0]
    gone = evict_rows[0, 0]
    width = cache.shape[1]
    table_rows = table.shape[0]
    capacity = wanted.shape[1]
    samples = loss.shape[1]
    mlp_width = w_first.shape[0]
    within = jnp.arange(capacity, dtype=jnp.int32)[None, :]
    wanted_live = within < fetch_counts[0, 0][:, None]
    gone_live = within < evict_counts[0, 0][:, None]

    slots = jnp.take(home_map, jnp.concatenate([wanted, gone], 1), axis=0) % table_rows
    live = jnp.concatenate([jnp.ones_like(wanted_live), gone_live], 1)
    asked = lax.all_to_all(
        jnp.where(live, slots, table_rows), "shard", split_axis=0, concat_axis=0, tiled=True
    )
    got_slots = asked[:, capacity:]

    cores = jnp.stack([1 - core, core])
    head_row = head[None]
    send, delta_a, inputs = forward_half(cores, group, cache, batch_t, None, None, loss, head_row, w_first)
    partner = lax.ppermute(send, "dp", swap_pairs())
    partner = pltpu.with_memory_space_constraint(partner, pltpu.HBM)
    chip, delta_b = forward_half(cores, group, None, None, partner, inputs, loss, head_row, w_first)
    plane = side * side
    pieces = chip.reshape((plane,) + chip.shape[2:])
    pieces = lax.all_to_all(
        pieces, "dp", split_axis=0, concat_axis=0, axis_index_groups=planes(), tiled=True
    )
    sent = backward(cores, asked, evict_from[0, 0], cache, table, batch_t, delta_a, delta_b, w_first)
    sent = add_total(pltpu.with_memory_space_constraint(pieces, pltpu.HBM), sent)
    got = lax.all_to_all(sent, "shard", split_axis=0, concat_axis=0, tiled=True)
    embed = width // 3
    got = got.reshape(group, 7, capacity, embed)
    mine = jnp.sum(got[:, 6], 0)
    came = got[:, 3:6].transpose(0, 2, 1, 3).reshape(-1, width)
    new_table = table.at[got_slots.reshape(-1)].set(came, mode="drop")
    arrived = got[:, :3].transpose(0, 2, 1, 3).reshape(group, capacity, width)
    fetched = jnp.where(wanted_live[:, :, None], arrived, 0.0)
    scale = 1.0 / math.sqrt(samples * group * devices)
    every = lax.all_to_all(
        jnp.broadcast_to(mine[None], (devices,) + mine.shape), "dp", split_axis=0, concat_axis=0, tiled=True
    )
    every = every.reshape((side, side, 2) + mine.shape).transpose(1, 3, 2, 0, 4)
    grad_first = (every.reshape(mlp_width // group, mlp_width) * scale).astype(jnp.bfloat16)
    return (grad_first, new_table[None, None], fetched[None, None])


def solution(mesh):
    placed = (
        P("dp", "shard", None, None),
        P("dp", "shard", None, None),
        P("dp", "shard", None, None),
        P("dp", "shard", None),
        P(),
        P(),
        P("dp", None),
        P("dp", "shard", None, None),
        P("dp", "shard", None),
        P("dp", "shard", None, None),
        P("dp", "shard", None, None),
        P("dp", "shard", None),
    )

    return jax.shard_map(
        local,
        mesh=mesh,
        in_specs=placed,
        out_specs=(
            P("shard", None),
            P("dp", "shard", None, None),
            P("dp", "shard", None, None, None),
        ),
        check_vma=False,
    )
```

time: 177 us -> 153 us (0.86)
  starting transfers between devices: 98.9 us -> 45.9 us
  waiting for transfers between devices: 33 us -> 61.2 us
  other arithmetic: 8.61 us -> 2.53 us
  Pallas kernels: 24.2 us -> 28.6 us
  local copies, waits for them, and re-layouts: 10.7 us -> 13.3 us
    ppermute x13 -> x1, starting transfers between devices: 47 us -> 8.73 us  [local(): partner = lax.ppermute(send, 'dp', swap_pairs())]
    all_to_all x3 -> x2, waiting for transfers between devices: 24.6 us -> 53.2 us  [the longest x1 38.6 us: local(): got = lax.all_to_all(sent, 'shard', split_axis=0, concat_axis=0, tiled=True)]
    all_to_all x3 -> x2, starting transfers between devices: 27 us -> 18.1 us  [the longest x1 11.4 us: local(): got = lax.all_to_all(sent, 'shard', split_axis=0, concat_axis=0, tiled=True)]
    all_to_all x1, starting transfers between devices: 15.4 us -> 9.46 us  [local(): lax.all_to_all(jnp.broadcast_to(mine[None], (devices,) + mine.shape), 'dp...]
    unnamed x17 -> x25, local copies, waits for them, and re-layouts: 1.2 us -> 6.24 us
    add x5 -> x0, other arithmetic: 4.38 us -> none  [the longest x1 2.07 us: reduce_gradient(): mine = keep + lax.ppermute(send, 'dp', swap_pairs())]
    pallas_call x1 -> x2, Pallas kernels: 10.3 us -> 14.6 us  [the longest x1 11.2 us: backward(): pl.pallas_call(backward_kernel, out_shape=jax.ShapeDtypeStruct((owners, 7...]
    all_to_all x1, waiting for transfers between devices: 0.01 us -> 2.91 us  [local(): lax.all_to_all(jnp.where(live, slots, table_rows), 'shard', split_axis=0,...]
  transfers between devices with their start and end apart: 18 -> 5, of which waited for: 5 -> 4; matrix products, arithmetic and copies ran while one was open for 9% -> 5% of each run, Pallas kernels for 10% -> 12%
where the time goes in v2:
time: 153 us; the launch traced here: 152 us
  waiting for transfers between devices  61.2 us (40%)
  starting transfers between devices  45.9 us (30%)
  Pallas kernels  28.6 us (19%)
  local copies, waits for them, and re-layouts  13.3 us (9%)
  other arithmetic  2.53 us (2%)
    all_to_all x1, waiting for transfers between devices, local(): got = lax.all_to_all(sent, 'shard', split_axis=0, concat_axis=0, tiled=True)  38.6 us
    all_to_all x1, waiting for transfers between devices, local(): lax.all_to_all(pieces, 'dp', split_axis=0, concat_axis=0, axis_index_grou...  14.6 us
    all_to_all x1, starting transfers between devices, local(): got = lax.all_to_all(sent, 'shard', split_axis=0, concat_axis=0, tiled=True)  11.4 us
    pallas_call x1, Pallas kernels, backward(): pl.pallas_call(backward_kernel, out_shape=jax.ShapeDtypeStruct((owners, 7...  11.2 us
    all_to_all x1, starting transfers between devices, local(): lax.all_to_all(jnp.where(live, slots, table_rows), 'shard', split_axis=0,...  9.57 us
    all_to_all x1, starting transfers between devices, local(): lax.all_to_all(jnp.broadcast_to(mine[None], (devices,) + mine.shape), 'dp...  9.46 us
    ppermute x1, starting transfers between devices, local(): partner = lax.ppermute(send, 'dp', swap_pairs())  8.73 us
    pallas_call x1, Pallas kernels, forward_half(): pl.pallas_call(first_kernel, out_shape=(grad, delta, jax.ShapeDtypeStruct...  7.04 us
  transfers between devices with their start and end apart: 5, of which 4 were waited for; matrix products, arithmetic and copies ran while one was open for 5% of the time, Pallas kernels for 12%

profile of v2, /device:TPU:1, one launch (start us, length us, event | category | flops | bytes accessed | tf_op | source)
XLA Modules:
  0.0 152.3 jit_solution(15657729270096313521)
XLA Ops:
  0.6 0.0 copy-start
  0.6 0.0 copy-start.8
  0.7 0.0 copy-start.7
  0.7 2.1 %copy.38 = f32[1,1,512,384]{3,2,1,0:T(8,128)} copy(f32[1,1,512,384]{3,2,1,0:T(8,128)} %param.13) | data formatting | bytes 1572864
  2.7 0.6 pad_add_fusion.cores
  3.3 7.0 %forward_first.1 = (f32[4,4,16,16,128]{4,3,2,1,0:T(8,128)}, bf16[512,1024]{1,0:T(8,128)(2,1)}, bf16[1024,1024]{1,0:T(8,128)(2,1)}) custom-call(s32[2]{0:T(128)} %pad_add_fusion.cores, f32[256,384]{1,0:T(8,128)} %bitcast.46, s32[8,1024]{1,0:T(8,128)} %bitcast.49, f32[1,1024]{1,0:T(1,128)} %bitcast.57, f32[1,1024]{1,0:T(1,128)} %bitcast.59, bf16[1024,1024]{1,0:T(8,128)(2,1)} %w_b.1), custom_call_target="tpu_custom_call" | custom-call | tf_op jit(solution)/shard_map/forward_first/pallas_call | solution.py:98
  10.3 8.7 %collective-permute-start = (f32[4,4,16,16,128]{4,3,2,1,0:T(8,128)}, f32[4,4,16,16,128]{4,3,2,1,0:T(8,128)S(1)}, u32[]{:S(2)}, u32[]{:S(2)}) collective-permute-start(f32[4,4,16,16,128]{4,3,2,1,0:T(8,128)} %get-tuple-element.8), channel_id=1, source_target_pairs={{0,1},{1,0},{2,3},{3,2},{4,5},{5,4},{6,7},{7,6},{8,9},{9,8},{10,11... | collective-permute-start | bytes 6291464 | tf_op jit(solution)/shard_map/ppermute | solution.py:288
  19.1 0.0 copy-done.8
  19.1 0.0 copy-done.7
  19.1 0.1 compare_select_fusion
  19.2 0.1 reshape.199
  19.3 0.0 copy-done
  19.3 0.0 copy-start.9
  19.3 3.1 %gather_fusion = s32[512]{0:T(512)S(1)} fusion(s32[8192]{0:T(1024)S(1)} %bitcast.37, s32[1024]{0:T(1024)S(1)} %pad_clamp_fusion), kind=kCustom, calls=%fused_computation | custom fusion | bytes 6144 | tf_op jit(solution)/shard_map/jit(_take)/gather | solution.py:278
  22.4 0.1 reshape.198
  22.5 0.0 copy-done.9
  22.5 0.1 iota_compare_fusion.1
  22.6 0.7 fusion.4
  23.3 9.6 %all-to-all-start.1 = ((s32[16,1,32]{2,1,0:T(1,128)}), s32[16,1,32]{2,1,0:T(1,128)S(1)}, u32[]{:S(2)}, u32[]{:S(2)}) async-start(s32[16,1,32]{2,1,0:T(1,128)} %bitcast.14), calls=%async_computation.1 | async-start | bytes 16384 | tf_op jit(solution)/shard_map/all_to_all | solution.py:280
  32.9 0.0 collective-permute-done.plus_ref
  32.9 0.0 copy-start.4
  32.9 1.4 copy-done.4
  34.2 7.0 %forward_second.1 = (f32[4,4,16,16,128]{4,3,2,1,0:T(8,128)}, bf16[512,1024]{1,0:T(8,128)(2,1)}) custom-call(s32[2]{0:T(128)} %pad_add_fusion.cores, f32[4,4,16,16,128]{4,3,2,1,0:T(8,128)} %copy-done.4, bf16[1024,1024]{1,0:T(8,128)(2,1)} %get-tuple-element.9.inputs_ref, f32[1,1024]{1,0:T(1,128)} %bitcast.58, f32[1,1024]{1,0:T(1,128)} %bitcast.60, ...), custom_call_target="tpu_custom_call" | custom-call | tf_op jit(solution)/shard_map/forward_second/pallas_call | solution.py:109
  41.2 2.9 %all-to-all-done.1 = s32[16,1,32]{2,1,0:T(1,128)S(1)} async-done(((s32[16,1,32]{2,1,0:T(1,128)}), s32[16,1,32]{2,1,0:T(1,128)S(1)}, u32[]{:S(2)}, u32[]{:S(2)}) %all-to-all-start.1) | async-done | bytes 2080 | tf_op jit(solution)/shard_map/all_to_all | solution.py:280
  44.1 0.0 copy-start.5
  44.1 0.6 copy-done.5
  44.7 6.8 %all-to-all-start = ((f32[16,16,16,128]{3,2,1,0:T(8,128)}), f32[16,16,16,128]{3,2,1,0:T(8,128)S(1)}, u32[]{:S(2)}, u32[]{:S(2)}) async-start(f32[16,16,16,128]{3,2,1,0:T(8,128)} %bitcast.45), calls=%async_computation | async-start | bytes 4194304 | tf_op jit(solution)/shard_map/all_to_all | solution.py:293
  51.5 11.2 %backward.1.sent_ref = f32[16,112,128]{2,1,0:T(8,128)} custom-call(s32[2]{0:T(128)} %pad_add_fusion.cores, s32[16,32]{1,0:T(8,128)} %bitcast.51, s32[16,16]{1,0:T(8,128)} %bitcast.61, f32[256,384]{1,0:T(8,128)} %bitcast.47, f32[512,384]{1,0:T(8,128)} %bitcast.40, s32[8,1024]{1,0:T(8,128)} %bitcast.50, bf16[512,1024]{1,0:T(8,128)(2,1)} %get-tuple-element.11.delta_a, ...), custom_call_target="tpu_custom_call" | custom-call | tf_op jit(solution)/shard_map/backward/pallas_call | solution.py:190
  62.6 0.0 copy-start.10
  62.6 0.0 copy-start.6
  62.6 14.6 %all-to-all-done.pieces_ref = f32[16,16,16,128]{3,2,1,0:T(8,128)S(1)} async-done(((f32[16,16,16,128]{3,2,1,0:T(8,128)}), f32[16,16,16,128]{3,2,1,0:T(8,128)S(1)}, u32[]{:S(2)}, u32[]{:S(2)}) %all-to-all-start) | async-done | bytes 2097184 | tf_op jit(solution)/shard_map/all_to_all | solution.py:293
  77.2 0.0 copy-start.1
  77.2 1.3 copy-done.1
  78.5 3.4 %total.1 = f32[16,112,128]{2,1,0:T(8,128)} custom-call(f32[16,16,16,128]{3,2,1,0:T(8,128)} %copy-done.1, f32[16,112,128]{2,1,0:T(8,128)} %backward.1.sent_ref), custom_call_target="tpu_custom_call", output_to_operand_aliasing={{}: (1, {})} | custom-call | tf_op jit(solution)/shard_map/total/pallas_call | solution.py:222
  82.0 11.4 %all-to-all-start.2 = ((f32[16,112,128]{2,1,0:T(8,128)}), f32[16,112,128]{2,1,0:T(8,128)S(1)}, u32[]{:S(2)}, u32[]{:S(2)}) async-start(f32[16,112,128]{2,1,0:T(8,128)} %total.1), calls=%async_computation.2 | async-start | bytes 1835008 | tf_op jit(solution)/shard_map/all_to_all | solution.py:298
  93.4 0.0 copy-done.10
  93.4 0.1 iota_compare_fusion
  93.4 0.0 copy-done.6
  93.5 0.1 slice.19
  93.5 0.1 reshape.194
  93.6 38.6 %all-to-all-done.2 = f32[16,112,128]{2,1,0:T(8,128)S(1)} async-done(((f32[16,112,128]{2,1,0:T(8,128)}), f32[16,112,128]{2,1,0:T(8,128)S(1)}, u32[]{:S(2)}, u32[]{:S(2)}) %all-to-all-start.2) | async-done | bytes 917536 | tf_op jit(solution)/shard_map/all_to_all | solution.py:298
  132.3 0.7 broadcast_in_dim.39
  133.0 9.5 %all-to-all-start.3 = ((f32[32,16,128]{2,1,0:T(8,128)}), f32[32,16,128]{2,1,0:T(8,128)S(1)}, u32[]{:S(2)}, u32[]{:S(2)}) async-start(f32[32,16,128]{2,1,0:T(8,128)} %broadcast_in_dim.39), calls=%async_computation.3 | async-start | bytes 524288 | tf_op jit(solution)/shard_map/all_to_all | solution.py:307
  142.5 0.0 copy-start.2
  142.5 0.1 fusion.5
  142.5 0.2 copy.26
  142.8 0.2 copy.34
  143.0 0.2 reshape.196
  143.2 0.4 copy-done.2
  143.6 1.7 %scatter_custom_fusion = f32[512,384]{1,0:T(8,128)S(1)} fusion(f32[512,384]{1,0:T(8,128)S(1)} %bitcast.41, s32[256]{0:T(256)S(1)} %bitcast.62, f32[32,8,3,128]{3,2,1,0:T(4,128)S(1)} %bitcast.44), kind=kCustom, calls=%fused_computation.3 | custom fusion | bytes 1310720 | tf_op jit(solution)/shard_map/scatter | solution.py:303
  145.4 0.0 copy-start.3
  145.4 1.0 broadcast_select_fusion
  146.4 5.1 %all-to-all-done.3 = f32[32,16,128]{2,1,0:T(8,128)S(1)} async-done(((f32[32,16,128]{2,1,0:T(8,128)}), f32[32,16,128]{2,1,0:T(8,128)S(1)}, u32[]{:S(2)}, u32[]{:S(2)}) %all-to-all-start.3) | async-done | bytes 262176 | tf_op jit(solution)/shard_map/all_to_all | solution.py:307
  151.5 0.1 copy.23
  151.6 0.7 convert_element_type.23
  152.3 0.0 copy-done.3
  (4 shorter events, 0.1 us)
Async XLA Ops:
  0.6 18.6 %copy-start = (s32[1,8192]{1,0:T(1,128)S(1)}, s32[1,8192]{1,0:T(1,128)}, u32[]{:S(2)}) copy-start(s32[1,8192]{1,0:T(1,128)} %param.18) | copy-start | bytes 98308
  0.6 18.4 %copy-start.8 = (s32[1,1,16,16]{3,2,1,0:T(8,128)S(1)}, s32[1,1,16,16]{3,2,1,0:T(8,128)}, u32[]{:S(2)}) copy-start(s32[1,1,16,16]{3,2,1,0:T(8,128)} %param.19) | copy-start | bytes 3076
  0.7 18.4 %copy-start.7 = (s32[1,1,16,16]{3,2,1,0:T(8,128)S(1)}, s32[1,1,16,16]{3,2,1,0:T(8,128)}, u32[]{:S(2)}) copy-start(s32[1,1,16,16]{3,2,1,0:T(8,128)} %param.21) | copy-start | bytes 3076
  10.3 22.5 %collective-permute-start = (f32[4,4,16,16,128]{4,3,2,1,0:T(8,128)}, f32[4,4,16,16,128]{4,3,2,1,0:T(8,128)S(1)}, u32[]{:S(2)}, u32[]{:S(2)}) collective-permute-start(f32[4,4,16,16,128]{4,3,2,1,0:T(8,128)} %get-tuple-element.8), channel_id=1, source_target_pairs={{0,1},{1,0},{2,3},{3,2},{4,5},{5,4},{6,7},{7,6},{8,9},{9,8},{10,11... | collective-permute-start | bytes 6291464 | tf_op jit(solution)/shard_map/ppermute | solution.py:288
  19.3 3.2 %copy-start.9 = (s32[1,1,16]{2,1,0:T(1,128)S(1)}, s32[1,1,16]{2,1,0:T(1,128)}, u32[]{:S(2)}) copy-start(s32[1,1,16]{2,1,0:T(1,128)} %param.23) | copy-start | bytes 196
  23.3 20.8 %all-to-all-start.1 = ((s32[16,1,32]{2,1,0:T(1,128)}), s32[16,1,32]{2,1,0:T(1,128)S(1)}, u32[]{:S(2)}, u32[]{:S(2)}) async-start(s32[16,1,32]{2,1,0:T(1,128)} %bitcast.14), calls=%async_computation.1 | async-start | bytes 16384 | tf_op jit(solution)/shard_map/all_to_all | solution.py:280
  32.9 1.4 copy-start.4
  44.1 0.6 copy-start.5
  44.7 32.5 %all-to-all-start = ((f32[16,16,16,128]{3,2,1,0:T(8,128)}), f32[16,16,16,128]{3,2,1,0:T(8,128)S(1)}, u32[]{:S(2)}, u32[]{:S(2)}) async-start(f32[16,16,16,128]{3,2,1,0:T(8,128)} %bitcast.45), calls=%async_computation | async-start | bytes 4194304 | tf_op jit(solution)/shard_map/all_to_all | solution.py:293
  62.6 30.7 %copy-start.10 = (s32[1,1,16]{2,1,0:T(1,128)S(1)}, s32[1,1,16]{2,1,0:T(1,128)}, u32[]{:S(2)}) copy-start(s32[1,1,16]{2,1,0:T(1,128)} %param.20) | copy-start | bytes 196
  62.6 30.8 %copy-start.6 = (s32[16,1,32]{2,1,0:T(1,128)S(1)}, s32[16,1,32]{2,1,0:T(1,128)}, u32[]{:S(2)}) copy-start(s32[16,1,32]{2,1,0:T(1,128)} %copy-done.5) | copy-start | bytes 6148
  77.2 1.3 copy-start.1
  82.0 50.3 %all-to-all-start.2 = ((f32[16,112,128]{2,1,0:T(8,128)}), f32[16,112,128]{2,1,0:T(8,128)S(1)}, u32[]{:S(2)}, u32[]{:S(2)}) async-start(f32[16,112,128]{2,1,0:T(8,128)} %total.1), calls=%async_computation.2 | async-start | bytes 1835008 | tf_op jit(solution)/shard_map/all_to_all | solution.py:298
  133.0 18.4 %all-to-all-start.3 = ((f32[32,16,128]{2,1,0:T(8,128)}), f32[32,16,128]{2,1,0:T(8,128)S(1)}, u32[]{:S(2)}, u32[]{:S(2)}) async-start(f32[32,16,128]{2,1,0:T(8,128)} %broadcast_in_dim.39), calls=%async_computation.3 | async-start | bytes 524288 | tf_op jit(solution)/shard_map/all_to_all | solution.py:307
  142.5 1.1 copy-start.2
  145.4 6.9 %copy-start.3 = (f32[512,384]{1,0:T(8,128)}, f32[512,384]{1,0:T(8,128)S(1)}, u32[]{:S(2)}) copy-start(f32[512,384]{1,0:T(8,128)S(1)} %scatter_custom_fusion) | copy-start | bytes 2359300

commit v3 on v2

--- a/solution.py
+++ b/solution.py
@@ -1,3 +1,4 @@
+import functools
 import math
 
 import jax
@@ -70,9 +71,10 @@
     store_pieces(grad, grad_ref, None)
 
 
-def second_kernel(cores, plus_ref, inputs_ref, loss_ref, head_ref, w_ref, grad_ref, delta_ref):
+def second_kernel(cores, plus_all, inputs_ref, loss_ref, head_ref, w_ref, grad_ref, delta_ref):
     grad = hidden(inputs_ref[...], loss_ref[...], head_ref[...], w_ref[...], delta_ref)
-    store_pieces(grad, grad_ref, plus_ref)
+    across = grad_ref.shape[0]
+    store_pieces(grad, grad_ref, plus_all.at[pl.ds(pl.program_id(0) * across, across)])
 
 
 def forward_half(cores, owners, cache, batch_t, partner, inputs, loss, head, w):
@@ -112,7 +114,7 @@
         grid_spec=pltpu.PrefetchScalarGridSpec(
             num_scalar_prefetch=1,
             grid=(steps,),
-            in_specs=[grad_spec, full((width, samples))] + tail_specs,
+            in_specs=[pl.BlockSpec(memory_space=pltpu.VMEM), full((width, samples))] + tail_specs,
             out_specs=(grad_spec, delta_spec),
         ),
         name="forward_second",
@@ -210,27 +212,135 @@
 
 
 def total_kernel(pieces_ref, sent_ref, out_ref):
-    total = pieces_ref[0]
+    owners = out_ref.shape[0]
+    here = pl.ds(pl.program_id(0) * owners, owners)
+    total = pieces_ref[0, here]
     for i in range(1, pieces_ref.shape[0]):
-        total += pieces_ref[i]
+        total += pieces_ref[i, here]
     out_ref[...] = total
 
 
 def add_total(pieces, sent):
-    count, owners, rows, columns = pieces.shape
+    _, owners, rows, columns = pieces.shape
     step = owners // 4
     return pl.pallas_call(
         total_kernel,
         out_shape=jax.ShapeDtypeStruct(sent.shape, sent.dtype),
         grid=(owners // step,),
         in_specs=[
-            pl.BlockSpec((count, step, rows, columns), lambda j: (0, j, 0, 0)),
+            pl.BlockSpec(memory_space=pltpu.VMEM),
             pl.BlockSpec(memory_space=pl.ANY),
         ],
         out_specs=pl.BlockSpec((step, rows, columns), lambda j: (j, sent.shape[1] // rows - 1, 0)),
         input_output_aliases={1: 0},
         name="total",
     )(pieces, sent)
+
+
+def lookup_kernel(home_ref, wanted_ref, gone_ref, counts_ref, out_ref, *, table_rows):
+    owners, capacity = wanted_ref.shape
+
+    def look(i, carry):
+        count = counts_ref[0, i]
+        for k in range(capacity):
+            out_ref[i, k] = home_ref[0, wanted_ref[i, k]] & (table_rows - 1)
+            slot = home_ref[0, gone_ref[i, k]] & (table_rows - 1)
+            out_ref[i, capacity + k] = jnp.where(k < count, slot, table_rows)
+        return carry
+
+    lax.fori_loop(0, owners, look, 0)
+
+
+def lookup(home, wanted, gone, counts, table_rows):
+    owners, capacity = wanted.shape
+    scalar = pl.BlockSpec(memory_space=pltpu.SMEM)
+    return pl.pallas_call(
+        functools.partial(lookup_kernel, table_rows=table_rows),
+        out_shape=jax.ShapeDtypeStruct((owners, 2 * capacity), jnp.int32),
+        in_specs=[scalar] * 4,
+        out_specs=scalar,
+        name="lookup",
+    )(home, wanted, gone, counts)
+
+
+def share_kernel(got_ref, out_ref):
+    rows = out_ref.shape[1]
+    last = pl.ds(got_ref.shape[1] - rows, rows)
+    total = got_ref[0, last]
+    for i in range(1, got_ref.shape[0]):
+        total += got_ref[i, last]
+    for d in range(out_ref.shape[0]):
+        out_ref[d] = total
+
+
+def share_total(got, rows, devices):
+    return pl.pallas_call(
+        share_kernel,
+        out_shape=jax.ShapeDtypeStruct((devices, rows, got.shape[2]), got.dtype),
+        in_specs=[pl.BlockSpec(memory_space=pltpu.VMEM)],
+        name="share_total",
+    )(got)
+
+
+def settle_kernel(asked_ref, counts_ref, got_ref, table_ref, new_ref, fetched_ref, rows_ref):
+    owners, both = asked_ref.shape
+    capacity = both // 2
+    embed = got_ref.shape[2]
+    table_rows = table_ref.shape[0]
+    for p in range(3):
+        rows_ref[p, :table_rows] = table_ref[:, p * embed : (p + 1) * embed]
+
+    def place(i, carry):
+        for k in range(capacity):
+            slot = asked_ref[i, capacity + k]
+            for p in range(3):
+                at = (3 + p) * capacity + k
+                rows_ref[p, pl.ds(slot, 1), :] = got_ref[i, at : at + 1, :]
+        live = lax.broadcasted_iota(jnp.int32, (capacity, embed), 0) < counts_ref[0, i]
+        for p in range(3):
+            block = got_ref[i, p * capacity : (p + 1) * capacity, :]
+            fetched_ref[i, :, p * embed : (p + 1) * embed] = jnp.where(live, block, 0.0)
+        return carry
+
+    lax.fori_loop(0, owners, place, 0)
+    for p in range(3):
+        new_ref[:, p * embed : (p + 1) * embed] = rows_ref[p, :table_rows]
+
+
+def settle(asked, counts, got, table):
+    owners, both = asked.shape
+    table_rows, width = table.shape
+    scalar = pl.BlockSpec(memory_space=pltpu.SMEM)
+    whole = pl.BlockSpec(memory_space=pltpu.VMEM)
+    return pl.pallas_call(
+        settle_kernel,
+        out_shape=(
+            jax.ShapeDtypeStruct(table.shape, table.dtype),
+            jax.ShapeDtypeStruct((owners, both // 2, width), table.dtype),
+        ),
+        in_specs=[scalar, scalar, whole, pl.BlockSpec(table.shape)],
+        out_specs=(pl.BlockSpec(table.shape), pl.BlockSpec((owners, both // 2, width))),
+        scratch_shapes=[pltpu.VMEM((3, table_rows + 8, width // 3), table.dtype)],
+        name="settle",
+    )(asked, counts, got, table)
+
+
+def finish_kernel(every_ref, out_ref, *, scale):
+    devices, rows, columns = every_ref.shape
+    for d in range(devices):
+        x, y, c = d // (2 * side), (d // 2) % side, d % 2
+        left = (c * side + x) * columns
+        out_ref[y * rows : (y + 1) * rows, left : left + columns] = (every_ref[d] * scale).astype(out_ref.dtype)
+
+
+def finish(every, scale):
+    _, rows, columns = every.shape
+    return pl.pallas_call(
+        functools.partial(finish_kernel, scale=scale),
+        out_shape=jax.ShapeDtypeStruct((side * rows, 2 * side * columns), jnp.bfloat16),
+        in_specs=[pl.BlockSpec(memory_space=pltpu.VMEM)],
+        name="finish",
+    )(every)
 
 
 def swap_pairs():
@@ -263,30 +373,20 @@
     table = table_state[0, 0]
     batch_t = batch_idx[0, 0].T
     loss = loss_grad[0]
-    home_map = home[0]
     wanted = fetch_rows[0, 0]
     gone = evict_rows[0, 0]
-    width = cache.shape[1]
     table_rows = table.shape[0]
-    capacity = wanted.shape[1]
     samples = loss.shape[1]
     mlp_width = w_first.shape[0]
-    within = jnp.arange(capacity, dtype=jnp.int32)[None, :]
-    wanted_live = within < fetch_counts[0, 0][:, None]
-    gone_live = within < evict_counts[0, 0][:, None]
-
-    slots = jnp.take(home_map, jnp.concatenate([wanted, gone], 1), axis=0) % table_rows
-    live = jnp.concatenate([jnp.ones_like(wanted_live), gone_live], 1)
-    asked = lax.all_to_all(
-        jnp.where(live, slots, table_rows), "shard", split_axis=0, concat_axis=0, tiled=True
-    )
-    got_slots = asked[:, capacity:]
+
+    slots = lookup(home, wanted, gone, evict_counts[0], table_rows)
+    asked = lax.all_to_all(slots, "shard", split_axis=0, concat_axis=0, tiled=True)
 
     cores = jnp.stack([1 - core, core])
     head_row = head[None]
     send, delta_a, inputs = forward_half(cores, group, cache, batch_t, None, None, loss, head_row, w_first)
     partner = lax.ppermute(send, "dp", swap_pairs())
-    partner = pltpu.with_memory_space_constraint(partner, pltpu.HBM)
+    partner = pltpu.with_memory_space_constraint(partner, pltpu.VMEM)
     chip, delta_b = forward_half(cores, group, None, None, partner, inputs, loss, head_row, w_first)
     plane = side * side
     pieces = chip.reshape((plane,) + chip.shape[2:])
@@ -294,21 +394,14 @@
         pieces, "dp", split_axis=0, concat_axis=0, axis_index_groups=planes(), tiled=True
     )
     sent = backward(cores, asked, evict_from[0, 0], cache, table, batch_t, delta_a, delta_b, w_first)
-    sent = add_total(pltpu.with_memory_space_constraint(pieces, pltpu.HBM), sent)
+    sent = add_total(pltpu.with_memory_space_constraint(pieces, pltpu.VMEM), sent)
     got = lax.all_to_all(sent, "shard", split_axis=0, concat_axis=0, tiled=True)
-    embed = width // 3
-    got = got.reshape(group, 7, capacity, embed)
-    mine = jnp.sum(got[:, 6], 0)
-    came = got[:, 3:6].transpose(0, 2, 1, 3).reshape(-1, width)
-    new_table = table.at[got_slots.reshape(-1)].set(came, mode="drop")
-    arrived = got[:, :3].transpose(0, 2, 1, 3).reshape(group, capacity, width)
-    fetched = jnp.where(wanted_live[:, :, None], arrived, 0.0)
     scale = 1.0 / math.sqrt(samples * group * devices)
-    every = lax.all_to_all(
-        jnp.broadcast_to(mine[None], (devices,) + mine.shape), "dp", split_axis=0, concat_axis=0, tiled=True
-    )
-    every = every.reshape((side, side, 2) + mine.shape).transpose(1, 3, 2, 0, 4)
-    grad_first = (every.reshape(mlp_width // group, mlp_width) * scale).astype(jnp.bfloat16)
+    got = pltpu.with_memory_space_constraint(got, pltpu.VMEM)
+    every = share_total(got, mlp_width // (group * side), devices)
+    every = lax.all_to_all(every, "dp", split_axis=0, concat_axis=0, tiled=True)
+    new_table, fetched = settle(asked, fetch_counts[0], got, table)
+    grad_first = finish(pltpu.with_memory_space_constraint(every, pltpu.VMEM), scale)
     return (grad_first, new_table[None, None], fetched[None, None])
 
 

time: 153 us -> 147 us (0.961)
  blocking collectives: 0 us -> 47.9 us
  waiting for transfers between devices: 61.2 us -> 25.5 us
  local copies, waits for them, and re-layouts: 13.3 us -> 0.6 us
  starting transfers between devices: 45.9 us -> 37.8 us
  Pallas kernels: 28.6 us -> 33.3 us
  other arithmetic: 2.53 us -> 0.59 us
    all_to_all x0 -> x1, blocking collectives: none -> 47.9 us  [local(): got = lax.all_to_all(sent, 'shard', split_axis=0, concat_axis=0, tiled=True)]
    all_to_all x3 -> x2, waiting for transfers between devices: 46.6 us -> 10.9 us  [the longest x1 6.33 us: local(): every = lax.all_to_all(every, 'dp', split_axis=0, concat_axis=0, tiled=True)]
    all_to_all x3 -> x2, starting transfers between devices: 30.4 us -> 22.3 us  [the longest x1 12.8 us: local(): every = lax.all_to_all(every, 'dp', split_axis=0, concat_axis=0, tiled=True)]
    pallas_call x0 -> x4, Pallas kernels: none -> 7.1 us  [the longest x1 3.05 us: lookup(): pl.pallas_call(functools.partial(lookup_kernel, table_rows=table_rows), o...]
    unnamed x25 -> x2, local copies, waits for them, and re-layouts: 6.24 us -> 0.6 us
    gather x2 -> x0, local copies, waits for them, and re-layouts: 3.22 us -> none  [local(): jnp.take(home_map, jnp.concatenate([wanted, gone], 1), axis=0) % table_rows]
    pallas_call x1, Pallas kernels: 3.43 us -> 1.34 us  [add_total(): pl.pallas_call(total_kernel, out_shape=jax.ShapeDtypeStruct(sent.shape, s...]
    select_n x4 -> x0, other arithmetic: 1.77 us -> none  [the longest x1 1 us: local(): fetched = jnp.where(wanted_live[:, :, None], arrived, 0.0)]
  transfers between devices with their start and end apart: 5 -> 4, of which waited for: 4 -> 3; matrix products, arithmetic and copies ran while one was open for 5% -> 0% of each run, Pallas kernels for 12% -> 16%
where the time goes in v3:
time: 147 us; the launch traced here: 146 us
  blocking collectives  47.9 us (33%)
  starting transfers between devices  37.8 us (26%)
  Pallas kernels  33.3 us (23%)
  waiting for transfers between devices  25.5 us (17%)
    all_to_all x1, blocking collectives, local(): got = lax.all_to_all(sent, 'shard', split_axis=0, concat_axis=0, tiled=True)  47.9 us
    all_to_all x1, waiting for transfers between devices, local(): lax.all_to_all(pieces, 'dp', split_axis=0, concat_axis=0, axis_index_grou...  14.6 us
    all_to_all x1, starting transfers between devices, local(): every = lax.all_to_all(every, 'dp', split_axis=0, concat_axis=0, tiled=True)  12.8 us
    pallas_call x1, Pallas kernels, backward(): pl.pallas_call(backward_kernel, out_shape=jax.ShapeDtypeStruct((owners, 7...  11.2 us
    all_to_all x1, starting transfers between devices, local(): lax.all_to_all(slots, 'shard', split_axis=0, concat_axis=0, tiled=True)  9.58 us
    ppermute x1, starting transfers between devices, local(): partner = lax.ppermute(send, 'dp', swap_pairs())  8.73 us
    pallas_call x1, Pallas kernels, forward_half(): pl.pallas_call(first_kernel, out_shape=(grad, delta, jax.ShapeDtypeStruct...  7.02 us
    all_to_all x1, starting transfers between devices, local(): lax.all_to_all(pieces, 'dp', split_axis=0, concat_axis=0, axis_index_grou...  6.76 us
  transfers between devices with their start and end apart: 4, of which 3 were waited for; matrix products, arithmetic and copies ran while one was open for 0% of the time, Pallas kernels for 16%

profile of v3, /device:TPU:1, one launch (start us, length us, event | category | flops | bytes accessed | tf_op | source)
XLA Modules:
  0.0 146.4 jit_solution(14764342716810825957)
XLA Ops:
  0.6 0.6 pad_add_fusion.cores
  1.2 7.0 %forward_first.1 = (f32[4,4,16,16,128]{4,3,2,1,0:T(8,128)}, bf16[512,1024]{1,0:T(8,128)(2,1)}, bf16[1024,1024]{1,0:T(8,128)(2,1)}) custom-call(s32[2]{0:T(128)} %pad_add_fusion.cores, f32[256,384]{1,0:T(8,128)} %bitcast.24, s32[8,1024]{1,0:T(8,128)} %bitcast.26, f32[1,1024]{1,0:T(1,128)} %bitcast.31, f32[1,1024]{1,0:T(1,128)} %bitcast.33, bf16[1024,1024]{1,0:T(8,128)(2,1)} %w_b.1), custom_call_target="tpu_custom_call" | custom-call | tf_op jit(solution)/shard_map/forward_first/pallas_call | solution.py:100
  8.2 8.7 %collective-permute-start = (f32[4,4,16,16,128]{4,3,2,1,0:T(8,128)}, f32[4,4,16,16,128]{4,3,2,1,0:T(8,128)S(1)}, u32[]{:S(2)}, u32[]{:S(2)}) collective-permute-start(f32[4,4,16,16,128]{4,3,2,1,0:T(8,128)} %get-tuple-element.10), channel_id=1, source_target_pairs={{0,1},{1,0},{2,3},{3,2},{4,5},{5,4},{6,7},{7,6},{8,9},{9,8},{10,11... | collective-permute-start | bytes 6291464 | tf_op jit(solution)/shard_map/ppermute | solution.py:388
  17.0 3.0 %lookup.1 = s32[16,32]{1,0:T(8,128)} custom-call(s32[1,8192]{1,0:T(1,128)} %home_ref.1, s32[16,16]{1,0:T(8,128)} %bitcast.35, s32[16,16]{1,0:T(8,128)} %bitcast.36, s32[1,16]{1,0:T(1,128)} %bitcast.39), custom_call_target="tpu_custom_call" | custom-call | tf_op jit(solution)/shard_map/lookup/pallas_call | solution.py:257
  20.0 9.6 %all-to-all-start.1 = ((s32[16,1,32]{2,1,0:T(1,128)}), s32[16,1,32]{2,1,0:T(1,128)S(1)}, u32[]{:S(2)}, u32[]{:S(2)}) async-start(s32[16,1,32]{2,1,0:T(1,128)} %bitcast.30), calls=%async_computation.1 | async-start | bytes 16384 | tf_op jit(solution)/shard_map/all_to_all | solution.py:383
  29.6 0.0 collective-permute-done.plus_all
  29.6 6.6 %forward_second.1 = (f32[4,4,16,16,128]{4,3,2,1,0:T(8,128)}, bf16[512,1024]{1,0:T(8,128)(2,1)}) custom-call(s32[2]{0:T(128)} %pad_add_fusion.cores, f32[4,4,16,16,128]{4,3,2,1,0:T(8,128)S(1)} %collective-permute-done.plus_all, bf16[1024,1024]{1,0:T(8,128)(2,1)} %get-tuple-element.11.inputs_ref, f32[1,1024]{1,0:T(1,128)} %bitcast.32, f32[1,1024]{1,0:T(1,128)} %bitcast.34, ...), custom_call_target="tpu_custom_call" | custom-call | tf_op jit(solution)/shard_map/forward_second/pallas_call | solution.py:111
  36.3 4.6 %all-to-all-done.1 = s32[16,1,32]{2,1,0:T(1,128)S(1)} async-done(((s32[16,1,32]{2,1,0:T(1,128)}), s32[16,1,32]{2,1,0:T(1,128)S(1)}, u32[]{:S(2)}, u32[]{:S(2)}) %all-to-all-start.1) | async-done | bytes 2080 | tf_op jit(solution)/shard_map/all_to_all | solution.py:383
  40.9 0.0 copy-start
  40.9 0.6 copy-done
  41.5 6.8 %all-to-all-start = ((f32[16,16,16,128]{3,2,1,0:T(8,128)}), f32[16,16,16,128]{3,2,1,0:T(8,128)S(1)}, u32[]{:S(2)}, u32[]{:S(2)}) async-start(f32[16,16,16,128]{3,2,1,0:T(8,128)} %bitcast.23), calls=%async_computation | async-start | bytes 4194304 | tf_op jit(solution)/shard_map/all_to_all | solution.py:393
  48.3 11.2 %backward.1.sent_ref = f32[16,112,128]{2,1,0:T(8,128)} custom-call(s32[2]{0:T(128)} %pad_add_fusion.cores, s32[16,32]{1,0:T(8,128)} %bitcast.28, s32[16,16]{1,0:T(8,128)} %bitcast.37, f32[256,384]{1,0:T(8,128)} %bitcast.25, f32[512,384]{1,0:T(8,128)} %bitcast.21, s32[8,1024]{1,0:T(8,128)} %bitcast.27, bf16[512,1024]{1,0:T(8,128)(2,1)} %get-tuple-element.13.delta_a, ...), custom_call_target="tpu_custom_call" | custom-call | tf_op jit(solution)/shard_map/backward/pallas_call | solution.py:192
  59.4 14.6 %all-to-all-done.pieces_ref = f32[16,16,16,128]{3,2,1,0:T(8,128)S(1)} async-done(((f32[16,16,16,128]{3,2,1,0:T(8,128)}), f32[16,16,16,128]{3,2,1,0:T(8,128)S(1)}, u32[]{:S(2)}, u32[]{:S(2)}) %all-to-all-start) | async-done | bytes 2097184 | tf_op jit(solution)/shard_map/all_to_all | solution.py:393
  74.0 1.3 total.1
  75.3 47.9 %all_to_all.26.got_ref = f32[16,112,128]{2,1,0:T(8,128)S(1)} all-to-all(f32[16,112,128]{2,1,0:T(8,128)} %total.1), channel_id=1, replica_groups=mesh['shard'=16,'dp'=32] {'shard'}, dimensions={0} | all-to-all | bytes 1835008 | tf_op jit(solution)/shard_map/all_to_all | solution.py:398
  123.2 0.7 share_total.1
  124.0 12.8 %all-to-all-start.3 = ((f32[32,16,128]{2,1,0:T(8,128)}), f32[32,16,128]{2,1,0:T(8,128)S(1)}, u32[]{:S(2)}, u32[]{:S(2)}) async-start(f32[32,16,128]{2,1,0:T(8,128)} %share_total.1), calls=%async_computation.3 | async-start | bytes 524288 | tf_op jit(solution)/shard_map/all_to_all | solution.py:402
  136.7 2.6 %settle.1 = (f32[512,384]{1,0:T(8,128)}, f32[16,16,384]{2,1,0:T(8,128)}) custom-call(s32[16,32]{1,0:T(8,128)} %bitcast.29, s32[1,16]{1,0:T(1,128)} %bitcast.38, f32[16,112,128]{2,1,0:T(8,128)S(1)} %all_to_all.26.got_ref, f32[512,384]{1,0:T(8,128)} %bitcast.22), custom_call_target="tpu_custom_call" | custom-call | tf_op jit(solution)/shard_map/settle/pallas_call | solution.py:315
  139.3 6.3 %all-to-all-done.3.every_ref = f32[32,16,128]{2,1,0:T(8,128)S(1)} async-done(((f32[32,16,128]{2,1,0:T(8,128)}), f32[32,16,128]{2,1,0:T(8,128)S(1)}, u32[]{:S(2)}, u32[]{:S(2)}) %all-to-all-start.3) | async-done | bytes 262176 | tf_op jit(solution)/shard_map/all_to_all | solution.py:402
  145.7 0.7 finish.1
Async XLA Ops:
  8.2 21.4 %collective-permute-start = (f32[4,4,16,16,128]{4,3,2,1,0:T(8,128)}, f32[4,4,16,16,128]{4,3,2,1,0:T(8,128)S(1)}, u32[]{:S(2)}, u32[]{:S(2)}) collective-permute-start(f32[4,4,16,16,128]{4,3,2,1,0:T(8,128)} %get-tuple-element.10), channel_id=1, source_target_pairs={{0,1},{1,0},{2,3},{3,2},{4,5},{5,4},{6,7},{7,6},{8,9},{9,8},{10,11... | collective-permute-start | bytes 6291464 | tf_op jit(solution)/shard_map/ppermute | solution.py:388
  20.0 20.8 %all-to-all-start.1 = ((s32[16,1,32]{2,1,0:T(1,128)}), s32[16,1,32]{2,1,0:T(1,128)S(1)}, u32[]{:S(2)}, u32[]{:S(2)}) async-start(s32[16,1,32]{2,1,0:T(1,128)} %bitcast.30), calls=%async_computation.1 | async-start | bytes 16384 | tf_op jit(solution)/shard_map/all_to_all | solution.py:383
  40.9 0.6 copy-start
  41.5 32.5 %all-to-all-start = ((f32[16,16,16,128]{3,2,1,0:T(8,128)}), f32[16,16,16,128]{3,2,1,0:T(8,128)S(1)}, u32[]{:S(2)}, u32[]{:S(2)}) async-start(f32[16,16,16,128]{3,2,1,0:T(8,128)} %bitcast.23), calls=%async_computation | async-start | bytes 4194304 | tf_op jit(solution)/shard_map/all_to_all | solution.py:393
  124.0 21.7 %all-to-all-start.3 = ((f32[32,16,128]{2,1,0:T(8,128)}), f32[32,16,128]{2,1,0:T(8,128)S(1)}, u32[]{:S(2)}, u32[]{:S(2)}) async-start(f32[32,16,128]{2,1,0:T(8,128)} %share_total.1), calls=%async_computation.3 | async-start | bytes 524288 | tf_op jit(solution)/shard_map/all_to_all | solution.py:402

commit v4 on v3

v4 whole, which is shorter than its diff:
```python
import functools
import math

import jax
import jax.numpy as jnp
from jax import lax
from jax.experimental import pallas as pl
from jax.experimental.pallas import tpu as pltpu
from jax.sharding import PartitionSpec as P


beta_one = 0.9
beta_two = 0.999
learn_rate = 0.05
epsilon = 1e-08
bias_one = 1.0 - 0.9**10
bias_two = 1.0 - 0.999**10
NN = (((1,), (0,)), ((), ()))
NT = (((1,), (1,)), ((), ()))
TN = (((0,), (0,)), ((), ()))
side = 4


def full(shape):
    return pl.BlockSpec(shape, lambda j, o: tuple(0 for _ in shape))


def column(row):
    return jnp.transpose(jnp.broadcast_to(row, (8, row.shape[1])))[:, :1]


def onehot(batch_row, rows):
    shape = (rows, batch_row.shape[1])
    hit = lax.broadcasted_iota(jnp.int32, shape, 0) == batch_row
    return hit.astype(jnp.float32).astype(jnp.bfloat16)


def turn(outer, inner):
    return (3 * outer) ^ inner


def hidden(j, info, inputs, loss, head, w, delta_ref):
    width = delta_ref.shape[1]
    pre = lax.dot_general(w, inputs, TN, preferred_element_type=jnp.float32)
    sigma = jax.nn.sigmoid(pre)
    delta = (loss * column(head) * sigma * (1.0 + pre * (1.0 - sigma))).astype(jnp.bfloat16)
    for u in range(2):
        delta_ref[turn(j, u) ^ info[2]] = delta[u * width : (u + 1) * width]
    return lax.dot_general(inputs, delta, NT, preferred_element_type=jnp.float32)


def store_pieces(j, info, grad_ref, outs, plus_ref):
    owners, rows, columns = outs[0].shape[-3:]
    deep = 2 * side * rows
    for v in range(2):
        for o in range(2):
            y = turn(o, v) ^ info[3]
            for u in range(2):
                left = slice(u * columns, (u + 1) * columns)
                for z in range(owners):
                    even = grad_ref[pl.ds(pl.multiple_of(z * deep + y * rows, rows), rows), left]
                    odd = grad_ref[pl.ds(pl.multiple_of(z * deep + side * rows + y * rows, rows), rows), left]
                    if plus_ref is not None:
                        even += plus_ref[u, j, v, o, z]
                        odd += plus_ref[2 + v, o, u, j, z]
                    outs[u][j, v, o, z] = even
                    outs[2 + v][o, u, j, z] = odd


def first_kernel(
    info, cache_ref, batch_ref, loss_ref, head_a, head_b, w_a, w_b, grad_out, delta_ref, inputs_ref, grad_ref
):
    rows = cache_ref.shape[0]
    features = batch_ref.shape[0]
    embed = inputs_ref.shape[0] // features
    j = pl.program_id(0)

    @pl.when(j == 0)
    def _():
        looked = jnp.transpose(cache_ref[...]).astype(jnp.bfloat16)
        for f in range(features):
            pick = onehot(batch_ref[f : f + 1, :], rows)
            inputs_ref[f * embed : (f + 1) * embed, :] = lax.dot_general(
                looked, pick, NN, preferred_element_type=jnp.float32
            ).astype(jnp.bfloat16)

    head = jnp.concatenate([head_a[...], head_b[...]], 1)
    w = jnp.concatenate([w_a[...], w_b[...]], 1)
    grad_ref[...] = hidden(j, info, inputs_ref[...], loss_ref[...], head, w, delta_ref)
    store_pieces(j, info, grad_ref, [grad_out.at[i] for i in range(4)], None)


def second_kernel(
    info, plus_ref, inputs_ref, loss_ref, head_a, head_b, w_a, w_b, out_a, out_b, out_c, out_d, delta_ref, grad_ref
):
    j = pl.program_id(0)
    head = jnp.concatenate([head_a[...], head_b[...]], 1)
    w = jnp.concatenate([w_a[...], w_b[...]], 1)
    grad_ref[...] = hidden(j, info, inputs_ref[...], loss_ref[...], head, w, delta_ref)
    store_pieces(j, info, grad_ref, [out_a, out_b, out_c, out_d], plus_ref)


def forward_half(info, owners, cache, batch_t, partner, inputs, loss, head, w):
    samples = loss.shape[1]
    width = w.shape[0]
    half = width // 2
    block = half // side
    here = 0 if inputs is None else 1
    whole = pl.BlockSpec(memory_space=pltpu.VMEM)
    part = lambda u: lambda j, c: (0, side * c[here] + (turn(j, u) ^ c[2]))
    tail_specs = [full((1, samples))]
    tail_specs += [pl.BlockSpec((1, block), part(u)) for u in range(2)]
    tail_specs += [pl.BlockSpec((width, block), part(u)) for u in range(2)]
    piece = (2, 2, 2, owners, width // (owners * 2 * side), block)
    delta = jax.ShapeDtypeStruct((side, block, samples), jnp.bfloat16)
    scratch = [pltpu.VMEM((width, 2 * block), jnp.float32)]
    if inputs is None:
        rows = cache.shape[0]
        embed = cache.shape[1] // 3
        return pl.pallas_call(
            first_kernel,
            out_shape=(
                jax.ShapeDtypeStruct((4,) + piece, jnp.float32),
                delta,
                jax.ShapeDtypeStruct((width, samples), jnp.bfloat16),
            ),
            grid_spec=pltpu.PrefetchScalarGridSpec(
                num_scalar_prefetch=1,
                grid=(2,),
                in_specs=[pl.BlockSpec((rows, embed), lambda j, c: (0, 0)), full(batch_t.shape)] + tail_specs,
                out_specs=(whole, whole, whole),
                scratch_shapes=scratch,
            ),
            name="forward_first",
        )(info, cache, batch_t, loss, head, head, w, w)
    return pl.pallas_call(
        second_kernel,
        out_shape=tuple(jax.ShapeDtypeStruct(piece, jnp.float32) for _ in range(4)) + (delta,),
        grid_spec=pltpu.PrefetchScalarGridSpec(
            num_scalar_prefetch=1,
            grid=(2,),
            in_specs=[whole, whole] + tail_specs,
            out_specs=(whole,) * 5,
            scratch_shapes=scratch,
        ),
        name="forward_second",
    )(info, partner, inputs, loss, head, head, w, w)


def backward_kernel(
    info, leaving, cache_ref, ids_ref, batch_ref, delta_a, delta_b, w_a, w_b, sent_ref, acc_ref, upd_ref
):
    rows, width = cache_ref.shape
    embed = width // 3
    owners, capacity = leaving.shape
    step = pl.program_id(0)
    half = w_a.shape[1]
    back = lax.dot_general(w_a[...], delta_a[...].reshape(half, -1), NN, preferred_element_type=jnp.float32)
    back += lax.dot_general(w_b[...], delta_b[...].reshape(half, -1), NN, preferred_element_type=jnp.float32)
    total = None
    for k in range(w_a.shape[0] // embed):
        part = back[k * embed : (k + 1) * embed]
        high = part.astype(jnp.bfloat16)
        low = (part - high.astype(jnp.float32)).astype(jnp.bfloat16)
        pick = onehot(batch_ref[pl.ds(step * (w_a.shape[0] // embed) + k, 1), :], rows)
        add = lax.dot_general(jnp.concatenate([high, low], 0), pick, NT, preferred_element_type=jnp.float32)
        total = add if total is None else total + add

    @pl.when(step == 0)
    def _():
        acc_ref[...] = total
        sent_ref[:, 3 * capacity :, :] = ids_ref[...]

    @pl.when(step > 0)
    def _():
        acc_ref[...] += total

    @pl.when(step == pl.num_programs(0) - 1)
    def _():
        grads = jnp.transpose(acc_ref[:embed, :] + acc_ref[embed:, :])
        value = cache_ref[:, :embed]
        first = cache_ref[:, embed : 2 * embed]
        second = cache_ref[:, 2 * embed :]
        first = beta_one * first + (1.0 - beta_one) * grads
        second = beta_two * second + (1.0 - beta_two) * grads * grads
        upd_ref[:, :embed] = value - learn_rate * (first / bias_one) / (jnp.sqrt(second / bias_two) + epsilon)
        upd_ref[:, embed : 2 * embed] = first
        upd_ref[:, 2 * embed :] = second

        def evict(i, carry):
            for k in range(capacity):
                row = upd_ref[pl.ds(leaving[i, k], 1), :]
                for p in range(3):
                    at = p * capacity + k
                    sent_ref[i, at : at + 1, :] = row[:, p * embed : (p + 1) * embed]
            return carry

        lax.fori_loop(0, owners, evict, 0)


def backward(info, leaving, cache, ids, batch_t, delta_a, delta_b, w):
    rows, width3 = cache.shape
    embed = width3 // 3
    features, _ = batch_t.shape
    width = w.shape[0]
    half = width // 2
    steps = features // 2
    owners, capacity = leaving.shape
    fixed = lambda shape: pl.BlockSpec(shape, lambda j, c, e: tuple(0 for _ in shape))
    whole = pl.BlockSpec(memory_space=pltpu.VMEM)
    sent = (owners, 3 * capacity + ids.shape[1], embed)
    return pl.pallas_call(
        backward_kernel,
        out_shape=jax.ShapeDtypeStruct(sent, jnp.float32),
        grid_spec=pltpu.PrefetchScalarGridSpec(
            num_scalar_prefetch=2,
            grid=(steps,),
            in_specs=[
                fixed(cache.shape),
                fixed(ids.shape),
                fixed(batch_t.shape),
                whole,
                whole,
                pl.BlockSpec((2 * embed, half), lambda j, c, e: (j, c[0])),
                pl.BlockSpec((2 * embed, half), lambda j, c, e: (j, c[1])),
            ],
            out_specs=fixed(sent),
            scratch_shapes=[pltpu.VMEM((2 * embed, rows), jnp.float32), pltpu.VMEM((rows, width3), jnp.float32)],
        ),
        name="backward",
    )(info, leaving, cache, ids, batch_t, delta_a, delta_b, w, w)


def serve_kernel(asked_ref, table_ref, even_a, even_b, odd_a, odd_b, out_ref):
    owners, both = asked_ref.shape
    capacity = both // 2
    embed = out_ref.shape[2]
    rows = even_a.shape[1]

    def fetch(i, carry):
        for k in range(capacity):
            row = table_ref[pl.ds(asked_ref[i, k], 1), :]
            for p in range(3):
                at = p * capacity + k
                out_ref[i, at : at + 1, :] = row[:, p * embed : (p + 1) * embed]
        return carry

    lax.fori_loop(0, owners, fetch, 0)
    out_ref[:, 3 * capacity : 3 * capacity + rows, :] = even_a[...] + even_b[...]
    out_ref[:, 3 * capacity + rows :, :] = odd_a[...] + odd_b[...]


def serve(asked, table, even, odd):
    owners, both = asked.shape
    _, rows, embed = even[0].shape
    whole = pl.BlockSpec(memory_space=pltpu.VMEM)
    return pl.pallas_call(
        serve_kernel,
        out_shape=jax.ShapeDtypeStruct((owners, 3 * both // 2 + 2 * rows, embed), jnp.float32),
        in_specs=[pl.BlockSpec(memory_space=pltpu.SMEM), pl.BlockSpec(table.shape)] + [whole] * 4,
        name="serve",
    )(asked, table, *even, *odd)


def lookup_kernel(home_ref, wanted_ref, gone_ref, counts_ref, out_ref, *, table_rows):
    owners, capacity = wanted_ref.shape

    def look(i, carry):
        count = counts_ref[0, i]
        for k in range(capacity):
            out_ref[i, k] = home_ref[0, wanted_ref[i, k]] & (table_rows - 1)
            slot = home_ref[0, gone_ref[i, k]] & (table_rows - 1)
            out_ref[i, capacity + k] = jnp.where(k < count, slot, table_rows)
        return carry

    lax.fori_loop(0, owners, look, 0)


def lookup(home, wanted, gone, counts, table_rows):
    owners, capacity = wanted.shape
    scalar = pl.BlockSpec(memory_space=pltpu.SMEM)
    return pl.pallas_call(
        functools.partial(lookup_kernel, table_rows=table_rows),
        out_shape=jax.ShapeDtypeStruct((owners, 2 * capacity), jnp.int32),
        in_specs=[scalar] * 4,
        out_specs=scalar,
        name="lookup",
    )(home, wanted, gone, counts)


def share_kernel(got_ref, out_ref):
    rows = out_ref.shape[1]
    last = pl.ds(got_ref.shape[1] - rows, rows)
    total = got_ref[0, last]
    for i in range(1, got_ref.shape[0]):
        total += got_ref[i, last]
    for d in range(out_ref.shape[0]):
        out_ref[d] = total


def share_total(got, rows, devices):
    return pl.pallas_call(
        share_kernel,
        out_shape=jax.ShapeDtypeStruct((devices, rows, got.shape[2]), got.dtype),
        in_specs=[pl.BlockSpec(memory_space=pltpu.VMEM)],
        name="share_total",
    )(got)


def settle_kernel(asked_ref, got_ref, table_ref, new_ref, rows_ref):
    owners, both = asked_ref.shape
    capacity = both // 2
    embed = got_ref.shape[2]
    table_rows = table_ref.shape[0]
    for p in range(3):
        rows_ref[p, :table_rows] = table_ref[:, p * embed : (p + 1) * embed]

    def place(i, carry):
        for k in range(capacity):
            slot = asked_ref[i, capacity + k]
            for p in range(3):
                at = p * capacity + k
                rows_ref[p, pl.ds(slot, 1), :] = got_ref[i, at : at + 1, :]
        return carry

    lax.fori_loop(0, owners, place, 0)
    for p in range(3):
        new_ref[:, p * embed : (p + 1) * embed] = rows_ref[p, :table_rows]


def settle(asked, got, table):
    table_rows, width = table.shape
    return pl.pallas_call(
        settle_kernel,
        out_shape=jax.ShapeDtypeStruct(table.shape, table.dtype),
        in_specs=[
            pl.BlockSpec(memory_space=pltpu.SMEM),
            pl.BlockSpec(memory_space=pltpu.VMEM),
            pl.BlockSpec(table.shape),
        ],
        out_specs=pl.BlockSpec(table.shape),
        scratch_shapes=[pltpu.VMEM((3, table_rows + 8, width // 3), table.dtype)],
        name="settle",
    )(asked, got, table)


def mask_kernel(counts_ref, got_ref, fetched_ref):
    owners, capacity, width = fetched_ref.shape
    embed = width // 3
    for i in range(owners):
        live = lax.broadcasted_iota(jnp.int32, (capacity, embed), 0) < counts_ref[0, i]
        for p in range(3):
            block = got_ref[i, p * capacity : (p + 1) * capacity, :]
            fetched_ref[i, :, p * embed : (p + 1) * embed] = jnp.where(live, block, 0.0)


def mask_rows(counts, got, capacity):
    return pl.pallas_call(
        mask_kernel,
        out_shape=jax.ShapeDtypeStruct((got.shape[0], capacity, 3 * got.shape[2]), got.dtype),
        in_specs=[pl.BlockSpec(memory_space=pltpu.SMEM), pl.BlockSpec(memory_space=pltpu.VMEM)],
        name="mask_rows",
    )(counts, got)


def finish_kernel(every_ref, out_ref, *, scale):
    _, both, columns = every_ref.shape
    rows = both // 2
    for x in range(side):
        for c in range(2):
            left = (c * side + x) * columns
            for k in range(2):
                for y in range(0, side, 2):
                    pair = [every_ref[(x * side + y + i) * 2 + c, k * rows : (k + 1) * rows] for i in range(2)]
                    top = (k * side + y) * rows
                    out_ref[top : top + both, left : left + columns] = (
                        jnp.concatenate(pair, 0) * scale
                    ).astype(out_ref.dtype)


def finish(every, scale):
    _, rows, columns = every.shape
    return pl.pallas_call(
        functools.partial(finish_kernel, scale=scale),
        out_shape=jax.ShapeDtypeStruct((side * rows, 2 * side * columns), jnp.bfloat16),
        in_specs=[pl.BlockSpec(memory_space=pltpu.VMEM)],
        name="finish",
    )(every)


def pairs(core, x, y):
    bits = (x * side + y) * 2 + core
    return [(d, d ^ bits) for d in range(2 * side * side)]


def send_to(a, x, y):
    return lax.ppermute(a, "dp", pairs(0, x, y))


def on_chip(a):
    return pltpu.with_memory_space_constraint(a, pltpu.VMEM)


def local(
    cache_state,
    table_state,
    batch_idx,
    loss_grad,
    w_first,
    head,
    home,
    fetch_rows,
    fetch_counts,
    evict_rows,
    evict_from,
    evict_counts,
):
    group = lax.axis_size("shard")
    devices = lax.axis_size("dp")
    place = lax.axis_index("dp").astype(jnp.uint32)
    core = (place & 1).astype(jnp.int32)
    cache = cache_state[0, 0]
    table = table_state[0, 0]
    batch_t = batch_idx[0, 0].T
    loss = loss_grad[0]
    wanted = fetch_rows[0, 0]
    gone = evict_rows[0, 0]
    table_rows = table.shape[0]
    capacity = wanted.shape[1]
    samples = loss.shape[1]
    mlp_width = w_first.shape[0]

    info = jnp.stack([1 - core, core, (place >> 3).astype(jnp.int32), ((place >> 1) & 3).astype(jnp.int32)])
    head_row = head[None]
    send, delta_a, inputs = forward_half(info, group, cache, batch_t, None, None, loss, head_row, w_first)
    partner = on_chip(lax.ppermute(send, "dp", pairs(1, 0, 0)))
    slots = lookup(home, wanted, gone, evict_counts[0], table_rows)
    lanes = cache.shape[1] // 3
    ids = jnp.pad(slots.astype(jnp.float32), ((0, 0), (0, lanes - slots.shape[1])))
    ids = jnp.broadcast_to(ids[:, None, :], (group, 8, lanes))
    even, even_out, odd, odd_out, delta_b = forward_half(
        info, group, None, None, partner, inputs, loss, head_row, w_first
    )
    even += send_to(even_out, 1, 0)
    odd += send_to(odd_out, 0, 1)
    sent = backward(info, evict_from[0, 0], cache, ids, batch_t, delta_a, delta_b, w_first)
    even = even[0] + send_to(even[1], 3, 0)
    odd = odd[0] + send_to(odd[1], 0, 3)
    got = lax.all_to_all(sent, "shard", split_axis=0, concat_axis=0, tiled=True)
    even = even[0] + send_to(even[1], 0, 1)
    odd = odd[0] + send_to(odd[1], 1, 0)
    even = (even[0], on_chip(send_to(even[1], 0, 3)))
    odd = (odd[0], on_chip(send_to(odd[1], 3, 0)))
    asked = got[:, 3 * capacity, : 2 * capacity].astype(jnp.int32)
    served = serve(asked, table, even, odd)
    came = on_chip(lax.all_to_all(served, "shard", split_axis=0, concat_axis=0, tiled=True))
    new_table = settle(asked, on_chip(got), table)
    scale = 1.0 / math.sqrt(samples * group * devices)
    every = share_total(came, mlp_width // (group * side), devices)
    every = on_chip(lax.all_to_all(every, "dp", split_axis=0, concat_axis=0, tiled=True))
    fetched = mask_rows(fetch_counts[0], came, capacity)
    grad_first = finish(every, scale)
    return (grad_first, new_table[None, None], fetched[None, None])


def solution(mesh):
    placed = (
        P("dp", "shard", None, None),
        P("dp", "shard", None, None),
        P("dp", "shard", None, None),
        P("dp", "shard", None),
        P(),
        P(),
        P("dp", None),
        P("dp", "shard", None, None),
        P("dp", "shard", None),
        P("dp", "shard", None, None),
        P("dp", "shard", None, None),
        P("dp", "shard", None),
    )

    return jax.shard_map(
        local,
        mesh=mesh,
        in_specs=placed,
        out_specs=(
            P("shard", None),
            P("dp", "shard", None, None),
            P("dp", "shard", None, None, None),
        ),
        check_vma=False,
    )
```

time: 147 us -> 160 us (1.088)
  starting transfers between devices: 37.8 us -> 55.5 us
  blocking collectives: 47.9 us -> 30.8 us
  local copies, waits for them, and re-layouts: 0.6 us -> 4.89 us
  Pallas kernels: 33.3 us -> 37.4 us
  other arithmetic: 0.59 us -> 3.2 us
    ppermute x1 -> x9, starting transfers between devices: 8.73 us -> 29.6 us  [the longest x8 20.9 us: send_to(): return lax.ppermute(a, 'dp', pairs(0, x, y))]
    ppermute x1 -> x9, waiting for transfers between devices: 0.01 us -> 20.5 us  [the longest x8 16.5 us: send_to(): return lax.ppermute(a, 'dp', pairs(0, x, y))]
    all_to_all x3 -> x2, waiting for transfers between devices: 25.5 us -> 6.04 us  [the longest x1 5.08 us: local(): lax.all_to_all(every, 'dp', split_axis=0, concat_axis=0, tiled=True)]
    all_to_all x1, blocking collectives: 47.9 us -> 30.8 us  [local(): lax.all_to_all(served, 'shard', split_axis=0, concat_axis=0, tiled=True)]
    pallas_call x5 -> x6, Pallas kernels: 28.8 us -> 32.9 us  [the longest x1 10.2 us: backward(): pl.pallas_call(backward_kernel, out_shape=jax.ShapeDtypeStruct(sent, jnp....]
    all_to_all x3 -> x2, starting transfers between devices: 29.1 us -> 25.9 us  [the longest x1 13.6 us: local(): lax.all_to_all(every, 'dp', split_axis=0, concat_axis=0, tiled=True)]
    unnamed x2 -> x6, local copies, waits for them, and re-layouts: 0.6 us -> 2.91 us
  transfers between devices with their start and end apart: 4 -> 11, of which waited for: 3 -> 6; matrix products, arithmetic and copies ran while one was open for 0% -> 3% of each run, Pallas kernels for 16% -> 11%
where the time goes in v4:
time: 160 us; the launch traced here: 159 us
  starting transfers between devices  55.5 us (35%)
  Pallas kernels  37.4 us (23%)
  blocking collectives  30.8 us (19%)
  waiting for transfers between devices  26.6 us (17%)
  local copies, waits for them, and re-layouts  4.89 us (3%)
  other arithmetic  3.2 us (2%)
    all_to_all x1, blocking collectives, local(): lax.all_to_all(served, 'shard', split_axis=0, concat_axis=0, tiled=True)  30.8 us
    ppermute x8, starting transfers between devices, send_to(): return lax.ppermute(a, 'dp', pairs(0, x, y))  20.9 us
    ppermute x8, waiting for transfers between devices, send_to(): return lax.ppermute(a, 'dp', pairs(0, x, y))  16.5 us
    all_to_all x1, starting transfers between devices, local(): lax.all_to_all(every, 'dp', split_axis=0, concat_axis=0, tiled=True)  13.6 us
    all_to_all x1, starting transfers between devices, local(): got = lax.all_to_all(sent, 'shard', split_axis=0, concat_axis=0, tiled=True)  12.3 us
    pallas_call x1, Pallas kernels, backward(): pl.pallas_call(backward_kernel, out_shape=jax.ShapeDtypeStruct(sent, jnp....  10.2 us
    ppermute x1, starting transfers between devices, local(): partner = on_chip(lax.ppermute(send, 'dp', pairs(1, 0, 0)))  8.73 us
    pallas_call x1, Pallas kernels, forward_half(): pl.pallas_call(first_kernel, out_shape=(jax.ShapeDtypeStruct((4,) + piece...  8.44 us
  transfers between devices with their start and end apart: 11, of which 6 were waited for; matrix products, arithmetic and copies ran while one was open for 3% of the time, Pallas kernels for 11%

profile of v4, /device:TPU:1, one launch (start us, length us, event | category | flops | bytes accessed | tf_op | source)
XLA Modules:
  0.0 159.1 jit_solution(15494407259759671236)
XLA Ops:
  0.6 0.6 pad_add_fusion.info
  1.2 8.4 %forward_first.1 = (f32[4,2,2,2,16,8,128]{6,5,4,3,2,1,0:T(8,128)}, bf16[4,128,1024]{2,1,0:T(8,128)(2,1)}, bf16[1024,1024]{1,0:T(8,128)(2,1)}) custom-call(s32[4]{0:T(128)} %pad_add_fusion.info, f32[256,384]{1,0:T(8,128)} %bitcast.53, s32[8,1024]{1,0:T(8,128)} %bitcast.57, f32[1,1024]{1,0:T(1,128)} %bitcast.65, f32[1,1024]{1,0:T(1,128)} %bitcast.61, ...), custom_call_target="tpu_custom_call" | custom-call | tf_op jit(solution)/shard_map/forward_first/pallas_call | solution.py:120
  9.7 8.7 %collective-permute-start = (f32[4,2,2,2,16,8,128]{6,5,4,3,2,1,0:T(8,128)}, f32[4,2,2,2,16,8,128]{6,5,4,3,2,1,0:T(8,128)S(1)}, u32[]{:S(2)}, u32[]{:S(2)}) collective-permute-start(f32[4,2,2,2,16,8,128]{6,5,4,3,2,1,0:T(8,128)} %get-tuple-element.12), channel_id=1, source_target_pairs={{0,1},{1,0},{2,3},{3,2},{4,5},{5,4},{6,7},{7,6},{8,9},{9,8},{10,11... | collective-permute-start | bytes 6291464 | tf_op jit(solution)/shard_map/ppermute | solution.py:436
  18.4 4.0 %collective-permute-done.plus_ref = f32[4,2,2,2,16,8,128]{6,5,4,3,2,1,0:T(8,128)S(1)} collective-permute-done((f32[4,2,2,2,16,8,128]{6,5,4,3,2,1,0:T(8,128)}, f32[4,2,2,2,16,8,128]{6,5,4,3,2,1,0:T(8,128)S(1)}, u32[]{:S(2)}, u32[]{:S(2)}) %collective-permute-start) | collective-permute-done | bytes 2097184 | tf_op jit(solution)/shard_map/ppermute | solution.py:436
  22.4 0.0 copy-start
  22.4 1.3 copy-done
  23.7 0.0 copy-start.1
  23.7 1.6 copy-done.1
  25.3 7.7 %forward_second.1 = (f32[2,2,2,16,8,128]{5,4,3,2,1,0:T(8,128)}, f32[2,2,2,16,8,128]{5,4,3,2,1,0:T(8,128)}, f32[2,2,2,16,8,128]{5,4,3,2,1,0:T(8,128)}, f32[2,2,2,...) custom-call(s32[4]{0:T(128)} %pad_add_fusion.info, f32[4,2,2,2,16,8,128]{6,5,4,3,2,1,0:T(8,128)S(1)} %copy-done.1, ...), custom_call_target="tpu_custom_call" | custom-call | tf_op jit(solution)/shard_map/forward_second/pallas_call | solution.py:136
  33.0 1.9 %collective-permute-start.5 = (f32[2,2,2,16,8,128]{5,4,3,2,1,0:T(8,128)}, f32[2,2,2,16,8,128]{5,4,3,2,1,0:T(8,128)S(1)}, u32[]{:S(2)}, u32[]{:S(2)}) collective-permute-start(f32[2,2,2,16,8,128]{5,4,3,2,1,0:T(8,128)} %get-tuple-element.18), channel_id=1, source_target_pairs={{0,2},{1,3},{2,0},{3,1},{4,6},{5,7},{6,4},{7,5},{8,10},{9,11},{10,... | collective-permute-start | bytes 1572872 | tf_op jit(solution)/shard_map/ppermute | solution.py:397
  34.9 1.9 %collective-permute-start.1 = (f32[2,2,2,16,8,128]{5,4,3,2,1,0:T(8,128)}, f32[2,2,2,16,8,128]{5,4,3,2,1,0:T(8,128)S(1)}, u32[]{:S(2)}, u32[]{:S(2)}) collective-permute-start(f32[2,2,2,16,8,128]{5,4,3,2,1,0:T(8,128)} %get-tuple-element.16), channel_id=1, source_target_pairs={{0,8},{1,9},{2,10},{3,11},{4,12},{5,13},{6,14},{7,15},{8,0},{9,1},... | collective-permute-start | bytes 1572872 | tf_op jit(solution)/shard_map/ppermute | solution.py:397
  36.8 11.4 %collective-permute-done.5 = f32[2,2,2,16,8,128]{5,4,3,2,1,0:T(8,128)S(1)} collective-permute-done((f32[2,2,2,16,8,128]{5,4,3,2,1,0:T(8,128)}, f32[2,2,2,16,8,128]{5,4,3,2,1,0:T(8,128)S(1)}, u32[]{:S(2)}, u32[]{:S(2)}) %collective-permute-start.5) | collective-permute-done | bytes 524320 | tf_op jit(solution)/shard_map/ppermute | solution.py:397
  48.2 1.1 add.23
  49.3 1.9 %collective-permute-start.6 = (f32[2,2,16,8,128]{4,3,2,1,0:T(8,128)S(1)}, f32[2,2,16,8,128]{4,3,2,1,0:T(8,128)S(1)}, u32[]{:S(2)}, u32[]{:S(2)}) collective-permute-start(f32[2,2,16,8,128]{4,3,2,1,0:T(8,128)S(1)} %slice_bitcast_fusion), channel_id=1, source_target_pairs={{0,6},{1,7},{2,4},{3,5},{4,2},{5,3},{6,0},{7,1},{8,14},{9,15},{10,... | collective-permute-start | bytes 786440 | tf_op jit(solution)/shard_map/ppermute | solution.py:397
  51.3 3.0 %lookup.1 = s32[16,32]{1,0:T(8,128)} custom-call(s32[1,8192]{1,0:T(1,128)} %home_ref.1, s32[16,16]{1,0:T(8,128)} %bitcast.67, s32[16,16]{1,0:T(8,128)} %bitcast.68, s32[1,16]{1,0:T(1,128)} %bitcast.70), custom_call_target="tpu_custom_call" | custom-call | tf_op jit(solution)/shard_map/lookup/pallas_call | solution.py:282
  54.3 0.7 convert_element_type.26
  55.0 0.6 broadcast_in_dim.15.ids_ref
  55.7 0.0 copy-start.2
  55.7 10.2 %backward.1 = f32[16,56,128]{2,1,0:T(8,128)} custom-call(s32[4]{0:T(128)} %pad_add_fusion.info, s32[16,16]{1,0:T(8,128)} %bitcast.69, f32[256,384]{1,0:T(8,128)} %bitcast.54, f32[16,8,128]{2,1,0:T(8,128)} %broadcast_in_dim.15.ids_ref, s32[8,1024]{1,0:T(8,128)} %bitcast.58, bf16[4,128,1024]{2,1,0:T(8,128)(2,1)} %get-tuple-element.11.delta_a, ...), custom_call_target="tpu_custom_call" | custom-call | tf_op jit(solution)/shard_map/backward/pallas_call | solution.py:212
  65.9 12.3 %all-to-all-start = ((f32[16,56,128]{2,1,0:T(8,128)}), f32[16,56,128]{2,1,0:T(8,128)S(1)}, u32[]{:S(2)}, u32[]{:S(2)}) async-start(f32[16,56,128]{2,1,0:T(8,128)} %backward.1), calls=%async_computation | async-start | bytes 917504 | tf_op jit(solution)/shard_map/all_to_all | solution.py:449
  78.2 0.0 collective-permute-done.1
  78.2 0.0 copy-done.2
  78.2 0.1 add.20
  78.3 4.4 %collective-permute-start.2 = (f32[2,2,16,8,128]{4,3,2,1,0:T(8,128)S(1)}, f32[2,2,16,8,128]{4,3,2,1,0:T(8,128)S(1)}, u32[]{:S(2)}, u32[]{:S(2)}) collective-permute-start(f32[2,2,16,8,128]{4,3,2,1,0:T(8,128)S(1)} %slice_bitcast_fusion.2), channel_id=1, source_target_pairs={{0,24},{1,25},{2,26},{3,27},{4,28},{5,29},{6,30},{7,31},{8,16},{9,... | collective-permute-start | bytes 786440 | tf_op jit(solution)/shard_map/ppermute | solution.py:397
  82.7 0.0 collective-permute-done.6
  82.8 1.9 %collective-permute-start.7 = (f32[2,16,8,128]{3,2,1,0:T(8,128)S(1)}, f32[2,16,8,128]{3,2,1,0:T(8,128)S(1)}, u32[]{:S(2)}, u32[]{:S(2)}) collective-permute-start(f32[2,16,8,128]{3,2,1,0:T(8,128)S(1)} %slice_bitcast_fusion.4), channel_id=1, source_target_pairs={{0,8},{1,9},{2,10},{3,11},{4,12},{5,13},{6,14},{7,15},{8,0},{9,1},... | collective-permute-start | bytes 393224 | tf_op jit(solution)/shard_map/ppermute | solution.py:397
  84.7 2.8 %collective-permute-done.2 = f32[2,2,16,8,128]{4,3,2,1,0:T(8,128)S(1)} collective-permute-done((f32[2,2,16,8,128]{4,3,2,1,0:T(8,128)S(1)}, f32[2,2,16,8,128]{4,3,2,1,0:T(8,128)S(1)}, u32[]{:S(2)}, u32[]{:S(2)}) %collective-permute-start.2) | collective-permute-done | bytes 262176 | tf_op jit(solution)/shard_map/ppermute | solution.py:397
  87.5 1.9 %collective-permute-start.3 = (f32[2,16,8,128]{3,2,1,0:T(8,128)S(1)}, f32[2,16,8,128]{3,2,1,0:T(8,128)S(1)}, u32[]{:S(2)}, u32[]{:S(2)}) collective-permute-start(f32[2,16,8,128]{3,2,1,0:T(8,128)S(1)} %slice_bitcast_fusion.6), channel_id=1, source_target_pairs={{0,2},{1,3},{2,0},{3,1},{4,6},{5,7},{6,4},{7,5},{8,10},{9,11},{10,... | collective-permute-start | bytes 393224 | tf_op jit(solution)/shard_map/ppermute | solution.py:397
  89.5 0.0 collective-permute-done.7
  89.5 0.6 slice_bitcast_fusion.8
  90.1 4.4 %collective-permute-start.8 = (f32[16,8,128]{2,1,0:T(8,128)S(1)}, f32[16,8,128]{2,1,0:T(8,128)S(1)}, u32[]{:S(2)}, u32[]{:S(2)}) collective-permute-start(f32[16,8,128]{2,1,0:T(8,128)S(1)} %get-tuple-element.19), channel_id=1, source_target_pairs={{0,24},{1,25},{2,26},{3,27},{4,28},{5,29},{6,30},{7,31},{8,16},{9,... | collective-permute-start | bytes 196616 | tf_op jit(solution)/shard_map/ppermute | solution.py:397
  94.5 0.0 collective-permute-done.3
  94.6 0.6 slice_bitcast_fusion.10
  95.2 2.5 %collective-permute-start.4 = (f32[16,8,128]{2,1,0:T(8,128)S(1)}, f32[16,8,128]{2,1,0:T(8,128)S(1)}, u32[]{:S(2)}, u32[]{:S(2)}) collective-permute-start(f32[16,8,128]{2,1,0:T(8,128)S(1)} %get-tuple-element.21), channel_id=1, source_target_pairs={{0,6},{1,7},{2,4},{3,5},{4,2},{5,3},{6,0},{7,1},{8,14},{9,15},{10,... | collective-permute-start | bytes 196616 | tf_op jit(solution)/shard_map/ppermute | solution.py:397
  97.7 1.0 all-to-all-done.got_ref
  98.7 0.6 slice_convert_fusion
  99.3 0.0 collective-permute-done.8.odd_b
  99.3 2.4 %collective-permute-done.4.even_b = f32[16,8,128]{2,1,0:T(8,128)S(1)} collective-permute-done((f32[16,8,128]{2,1,0:T(8,128)S(1)}, f32[16,8,128]{2,1,0:T(8,128)S(1)}, u32[]{:S(2)}, u32[]{:S(2)}) %collective-permute-start.4) | collective-permute-done | bytes 65568 | tf_op jit(solution)/shard_map/ppermute | solution.py:397
  101.7 2.6 %serve.1 = f32[16,64,128]{2,1,0:T(8,128)} custom-call(s32[16,32]{1,0:T(8,128)} %bitcast.59, f32[512,384]{1,0:T(8,128)} %bitcast.51, f32[16,8,128]{2,1,0:T(8,128)} %get-tuple-element.22.even_a, f32[16,8,128]{2,1,0:T(8,128)S(1)} %collective-permute-done.4.even_b, f32[16,8,128]{2,1,0:T(8,128)} %get-tuple-element.20.odd_a, ...), custom_call_target="tpu_custom_call" | custom-call | tf_op jit(solution)/shard_map/serve/pallas_call | solution.py:257
  104.3 30.8 %all_to_all.15.got_ref = f32[16,64,128]{2,1,0:T(8,128)S(1)} all-to-all(f32[16,64,128]{2,1,0:T(8,128)} %serve.1), channel_id=1, replica_groups=mesh['shard'=16,'dp'=32] {'shard'}, dimensions={0} | all-to-all | bytes 1048576 | tf_op jit(solution)/shard_map/all_to_all | solution.py:456
  135.1 0.7 share_total.1
  135.8 13.6 %all-to-all-start.2 = ((f32[32,16,128]{2,1,0:T(8,128)}), f32[32,16,128]{2,1,0:T(8,128)S(1)}, u32[]{:S(2)}, u32[]{:S(2)}) async-start(f32[32,16,128]{2,1,0:T(8,128)} %share_total.1), calls=%async_computation.2 | async-start | bytes 524288 | tf_op jit(solution)/shard_map/all_to_all | solution.py:460
  149.4 2.5 %settle.1 = f32[512,384]{1,0:T(8,128)} custom-call(s32[16,32]{1,0:T(8,128)} %bitcast.60, f32[16,56,128]{2,1,0:T(8,128)S(1)} %all-to-all-done.got_ref, f32[512,384]{1,0:T(8,128)} %bitcast.52), custom_call_target="tpu_custom_call" | custom-call | tf_op jit(solution)/shard_map/settle/pallas_call | solution.py:333
  151.9 1.4 mask_rows.1
  153.4 5.1 %all-to-all-done.2.every_ref = f32[32,16,128]{2,1,0:T(8,128)S(1)} async-done(((f32[32,16,128]{2,1,0:T(8,128)}), f32[32,16,128]{2,1,0:T(8,128)S(1)}, u32[]{:S(2)}, u32[]{:S(2)}) %all-to-all-start.2) | async-done | bytes 262176 | tf_op jit(solution)/shard_map/all_to_all | solution.py:460
  158.5 0.7 finish.1
  (9 shorter events, 0.2 us)
Async XLA Ops:
  9.7 12.7 %collective-permute-start = (f32[4,2,2,2,16,8,128]{6,5,4,3,2,1,0:T(8,128)}, f32[4,2,2,2,16,8,128]{6,5,4,3,2,1,0:T(8,128)S(1)}, u32[]{:S(2)}, u32[]{:S(2)}) collective-permute-start(f32[4,2,2,2,16,8,128]{6,5,4,3,2,1,0:T(8,128)} %get-tuple-element.12), channel_id=1, source_target_pairs={{0,1},{1,0},{2,3},{3,2},{4,5},{5,4},{6,7},{7,6},{8,9},{9,8},{10,11... | collective-permute-start | bytes 6291464 | tf_op jit(solution)/shard_map/ppermute | solution.py:436
  22.4 1.3 copy-start
  23.7 1.6 copy-start.1
  33.0 15.2 %collective-permute-start.5 = (f32[2,2,2,16,8,128]{5,4,3,2,1,0:T(8,128)}, f32[2,2,2,16,8,128]{5,4,3,2,1,0:T(8,128)S(1)}, u32[]{:S(2)}, u32[]{:S(2)}) collective-permute-start(f32[2,2,2,16,8,128]{5,4,3,2,1,0:T(8,128)} %get-tuple-element.18), channel_id=1, source_target_pairs={{0,2},{1,3},{2,0},{3,1},{4,6},{5,7},{6,4},{7,5},{8,10},{9,11},{10,... | collective-permute-start | bytes 1572872 | tf_op jit(solution)/shard_map/ppermute | solution.py:397
  34.9 43.3 %collective-permute-start.1 = (f32[2,2,2,16,8,128]{5,4,3,2,1,0:T(8,128)}, f32[2,2,2,16,8,128]{5,4,3,2,1,0:T(8,128)S(1)}, u32[]{:S(2)}, u32[]{:S(2)}) collective-permute-start(f32[2,2,2,16,8,128]{5,4,3,2,1,0:T(8,128)} %get-tuple-element.16), channel_id=1, source_target_pairs={{0,8},{1,9},{2,10},{3,11},{4,12},{5,13},{6,14},{7,15},{8,0},{9,1},... | collective-permute-start | bytes 1572872 | tf_op jit(solution)/shard_map/ppermute | solution.py:397
  49.3 33.4 %collective-permute-start.6 = (f32[2,2,16,8,128]{4,3,2,1,0:T(8,128)S(1)}, f32[2,2,16,8,128]{4,3,2,1,0:T(8,128)S(1)}, u32[]{:S(2)}, u32[]{:S(2)}) collective-permute-start(f32[2,2,16,8,128]{4,3,2,1,0:T(8,128)S(1)} %slice_bitcast_fusion), channel_id=1, source_target_pairs={{0,6},{1,7},{2,4},{3,5},{4,2},{5,3},{6,0},{7,1},{8,14},{9,15},{10,... | collective-permute-start | bytes 786440 | tf_op jit(solution)/shard_map/ppermute | solution.py:397
  55.7 22.5 %copy-start.2 = (f32[2,2,2,16,8,128]{5,4,3,2,1,0:T(8,128)S(1)}, f32[2,2,2,16,8,128]{5,4,3,2,1,0:T(8,128)}, u32[]{:S(2)}) copy-start(f32[2,2,2,16,8,128]{5,4,3,2,1,0:T(8,128)} %get-tuple-element.15) | copy-start | bytes 1572868
  65.9 32.8 %all-to-all-start = ((f32[16,56,128]{2,1,0:T(8,128)}), f32[16,56,128]{2,1,0:T(8,128)S(1)}, u32[]{:S(2)}, u32[]{:S(2)}) async-start(f32[16,56,128]{2,1,0:T(8,128)} %backward.1), calls=%async_computation | async-start | bytes 917504 | tf_op jit(solution)/shard_map/all_to_all | solution.py:449
  78.3 9.2 %collective-permute-start.2 = (f32[2,2,16,8,128]{4,3,2,1,0:T(8,128)S(1)}, f32[2,2,16,8,128]{4,3,2,1,0:T(8,128)S(1)}, u32[]{:S(2)}, u32[]{:S(2)}) collective-permute-start(f32[2,2,16,8,128]{4,3,2,1,0:T(8,128)S(1)} %slice_bitcast_fusion.2), channel_id=1, source_target_pairs={{0,24},{1,25},{2,26},{3,27},{4,28},{5,29},{6,30},{7,31},{8,16},{9,... | collective-permute-start | bytes 786440 | tf_op jit(solution)/shard_map/ppermute | solution.py:397
  82.8 6.7 %collective-permute-start.7 = (f32[2,16,8,128]{3,2,1,0:T(8,128)S(1)}, f32[2,16,8,128]{3,2,1,0:T(8,128)S(1)}, u32[]{:S(2)}, u32[]{:S(2)}) collective-permute-start(f32[2,16,8,128]{3,2,1,0:T(8,128)S(1)} %slice_bitcast_fusion.4), channel_id=1, source_target_pairs={{0,8},{1,9},{2,10},{3,11},{4,12},{5,13},{6,14},{7,15},{8,0},{9,1},... | collective-permute-start | bytes 393224 | tf_op jit(solution)/shard_map/ppermute | solution.py:397
  87.5 7.0 %collective-permute-start.3 = (f32[2,16,8,128]{3,2,1,0:T(8,128)S(1)}, f32[2,16,8,128]{3,2,1,0:T(8,128)S(1)}, u32[]{:S(2)}, u32[]{:S(2)}) collective-permute-start(f32[2,16,8,128]{3,2,1,0:T(8,128)S(1)} %slice_bitcast_fusion.6), channel_id=1, source_target_pairs={{0,2},{1,3},{2,0},{3,1},{4,6},{5,7},{6,4},{7,5},{8,10},{9,11},{10,... | collective-permute-start | bytes 393224 | tf_op jit(solution)/shard_map/ppermute | solution.py:397
  90.1 9.2 %collective-permute-start.8 = (f32[16,8,128]{2,1,0:T(8,128)S(1)}, f32[16,8,128]{2,1,0:T(8,128)S(1)}, u32[]{:S(2)}, u32[]{:S(2)}) collective-permute-start(f32[16,8,128]{2,1,0:T(8,128)S(1)} %get-tuple-element.19), channel_id=1, source_target_pairs={{0,24},{1,25},{2,26},{3,27},{4,28},{5,29},{6,30},{7,31},{8,16},{9,... | collective-permute-start | bytes 196616 | tf_op jit(solution)/shard_map/ppermute | solution.py:397
  95.2 6.5 %collective-permute-start.4 = (f32[16,8,128]{2,1,0:T(8,128)S(1)}, f32[16,8,128]{2,1,0:T(8,128)S(1)}, u32[]{:S(2)}, u32[]{:S(2)}) collective-permute-start(f32[16,8,128]{2,1,0:T(8,128)S(1)} %get-tuple-element.21), channel_id=1, source_target_pairs={{0,6},{1,7},{2,4},{3,5},{4,2},{5,3},{6,0},{7,1},{8,14},{9,15},{10,... | collective-permute-start | bytes 196616 | tf_op jit(solution)/shard_map/ppermute | solution.py:397
  135.8 22.7 %all-to-all-start.2 = ((f32[32,16,128]{2,1,0:T(8,128)}), f32[32,16,128]{2,1,0:T(8,128)S(1)}, u32[]{:S(2)}, u32[]{:S(2)}) async-start(f32[32,16,128]{2,1,0:T(8,128)} %share_total.1), calls=%async_computation.2 | async-start | bytes 524288 | tf_op jit(solution)/shard_map/all_to_all | solution.py:460

commit v5 on v4

--- a/solution.py
+++ b/solution.py
@@ -40,12 +40,11 @@
 
 
 def hidden(j, info, inputs, loss, head, w, delta_ref):
-    width = delta_ref.shape[1]
     pre = lax.dot_general(w, inputs, TN, preferred_element_type=jnp.float32)
     sigma = jax.nn.sigmoid(pre)
     delta = (loss * column(head) * sigma * (1.0 + pre * (1.0 - sigma))).astype(jnp.bfloat16)
     for u in range(2):
-        delta_ref[turn(j, u) ^ info[2]] = delta[u * width : (u + 1) * width]
+        delta_ref[(turn(j, u) ^ info[2]) & 1] = delta[u * (delta.shape[0] // 2) : (u + 1) * (delta.shape[0] // 2)]
     return lax.dot_general(inputs, delta, NT, preferred_element_type=jnp.float32)
 
 
@@ -62,20 +61,20 @@
                     odd = grad_ref[pl.ds(pl.multiple_of(z * deep + side * rows + y * rows, rows), rows), left]
                     if plus_ref is not None:
                         even += plus_ref[u, j, v, o, z]
-                        odd += plus_ref[2 + v, o, u, j, z]
-                    outs[u][j, v, o, z] = even
-                    outs[2 + v][o, u, j, z] = odd
-
-
-def first_kernel(
-    info, cache_ref, batch_ref, loss_ref, head_a, head_b, w_a, w_b, grad_out, delta_ref, inputs_ref, grad_ref
-):
+                        odd += plus_ref[2 + v, j, o, u, z]
+                    outs[u][0, v, o, z] = even
+                    if plus_ref is None:
+                        outs[2 + v][0, o, u, z] = odd
+                    else:
+                        outs[2 + v][o, u, 0, z] = odd
+
+
+def gather(cache_ref, batch_ref, inputs_ref):
     rows = cache_ref.shape[0]
     features = batch_ref.shape[0]
     embed = inputs_ref.shape[0] // features
-    j = pl.program_id(0)
-
-    @pl.when(j == 0)
+
+    @pl.when(pl.program_id(0) == 0)
     def _():
         looked = jnp.transpose(cache_ref[...]).astype(jnp.bfloat16)
         for f in range(features):
@@ -84,6 +83,12 @@
                 looked, pick, NN, preferred_element_type=jnp.float32
             ).astype(jnp.bfloat16)
 
+
+def first_kernel(
+    info, cache_ref, batch_ref, loss_ref, head_a, head_b, w_a, w_b, grad_out, delta_ref, inputs_ref, grad_ref
+):
+    j = pl.program_id(0)
+    gather(cache_ref, batch_ref, inputs_ref)
     head = jnp.concatenate([head_a[...], head_b[...]], 1)
     w = jnp.concatenate([w_a[...], w_b[...]], 1)
     grad_ref[...] = hidden(j, info, inputs_ref[...], loss_ref[...], head, w, delta_ref)
@@ -91,60 +96,74 @@
 
 
 def second_kernel(
-    info, plus_ref, inputs_ref, loss_ref, head_a, head_b, w_a, w_b, out_a, out_b, out_c, out_d, delta_ref, grad_ref
+    info,
+    plus_ref,
+    cache_ref,
+    batch_ref,
+    loss_ref,
+    head_a,
+    head_b,
+    w_a,
+    w_b,
+    out_a,
+    out_b,
+    out_c,
+    out_d,
+    delta_ref,
+    inputs_ref,
+    grad_ref,
 ):
     j = pl.program_id(0)
+    gather(cache_ref, batch_ref, inputs_ref)
     head = jnp.concatenate([head_a[...], head_b[...]], 1)
     w = jnp.concatenate([w_a[...], w_b[...]], 1)
     grad_ref[...] = hidden(j, info, inputs_ref[...], loss_ref[...], head, w, delta_ref)
     store_pieces(j, info, grad_ref, [out_a, out_b, out_c, out_d], plus_ref)
 
 
-def forward_half(info, owners, cache, batch_t, partner, inputs, loss, head, w):
+def forward_half(info, owners, cache, batch_t, partner, loss, head, w):
     samples = loss.shape[1]
     width = w.shape[0]
     half = width // 2
     block = half // side
-    here = 0 if inputs is None else 1
-    whole = pl.BlockSpec(memory_space=pltpu.VMEM)
+    here = 0 if partner is None else 1
+    rows = cache.shape[0]
+    embed = cache.shape[1] // 3
     part = lambda u: lambda j, c: (0, side * c[here] + (turn(j, u) ^ c[2]))
-    tail_specs = [full((1, samples))]
-    tail_specs += [pl.BlockSpec((1, block), part(u)) for u in range(2)]
-    tail_specs += [pl.BlockSpec((width, block), part(u)) for u in range(2)]
+    specs = [pl.BlockSpec((rows, embed), lambda j, c: (0, 0)), full(batch_t.shape), full((1, samples))]
+    specs += [pl.BlockSpec((1, block), part(u)) for u in range(2)]
+    specs += [pl.BlockSpec((width, block), part(u)) for u in range(2)]
     piece = (2, 2, 2, owners, width // (owners * 2 * side), block)
     delta = jax.ShapeDtypeStruct((side, block, samples), jnp.bfloat16)
-    scratch = [pltpu.VMEM((width, 2 * block), jnp.float32)]
-    if inputs is None:
-        rows = cache.shape[0]
-        embed = cache.shape[1] // 3
+    delta_spec = pl.BlockSpec((2, block, samples), lambda j, c: (j ^ (c[2] >> 1), 0, 0))
+    scratch = [pltpu.VMEM((width, samples), jnp.bfloat16), pltpu.VMEM((width, 2 * block), jnp.float32)]
+    if partner is None:
         return pl.pallas_call(
             first_kernel,
-            out_shape=(
-                jax.ShapeDtypeStruct((4,) + piece, jnp.float32),
-                delta,
-                jax.ShapeDtypeStruct((width, samples), jnp.bfloat16),
-            ),
+            out_shape=(jax.ShapeDtypeStruct((4,) + piece, jnp.float32), delta),
             grid_spec=pltpu.PrefetchScalarGridSpec(
                 num_scalar_prefetch=1,
                 grid=(2,),
-                in_specs=[pl.BlockSpec((rows, embed), lambda j, c: (0, 0)), full(batch_t.shape)] + tail_specs,
-                out_specs=(whole, whole, whole),
+                in_specs=specs,
+                out_specs=(pl.BlockSpec((4, 1) + piece[1:], lambda j, c: (0, j, 0, 0, 0, 0, 0)), delta_spec),
                 scratch_shapes=scratch,
             ),
             name="forward_first",
         )(info, cache, batch_t, loss, head, head, w, w)
+    even_spec = pl.BlockSpec((1,) + piece[1:], lambda j, c: (j, 0, 0, 0, 0, 0))
+    odd_spec = pl.BlockSpec((2, 2, 1) + piece[3:], lambda j, c: (0, 0, j, 0, 0, 0))
     return pl.pallas_call(
         second_kernel,
         out_shape=tuple(jax.ShapeDtypeStruct(piece, jnp.float32) for _ in range(4)) + (delta,),
         grid_spec=pltpu.PrefetchScalarGridSpec(
             num_scalar_prefetch=1,
             grid=(2,),
-            in_specs=[whole, whole] + tail_specs,
-            out_specs=(whole,) * 5,
+            in_specs=[pl.BlockSpec(memory_space=pltpu.VMEM)] + specs,
+            out_specs=(even_spec, even_spec, odd_spec, odd_spec, delta_spec),
             scratch_shapes=scratch,
         ),
         name="forward_second",
-    )(info, partner, inputs, loss, head, head, w, w)
+    )(info, partner, cache, batch_t, loss, head, head, w, w)
 
 
 def backward_kernel(
@@ -432,18 +451,18 @@
 
     info = jnp.stack([1 - core, core, (place >> 3).astype(jnp.int32), ((place >> 1) & 3).astype(jnp.int32)])
     head_row = head[None]
-    send, delta_a, inputs = forward_half(info, group, cache, batch_t, None, None, loss, head_row, w_first)
+    send, delta_a = forward_half(info, group, cache, batch_t, None, loss, head_row, w_first)
     partner = on_chip(lax.ppermute(send, "dp", pairs(1, 0, 0)))
     slots = lookup(home, wanted, gone, evict_counts[0], table_rows)
     lanes = cache.shape[1] // 3
     ids = jnp.pad(slots.astype(jnp.float32), ((0, 0), (0, lanes - slots.shape[1])))
     ids = jnp.broadcast_to(ids[:, None, :], (group, 8, lanes))
-    even, even_out, odd, odd_out, delta_b = forward_half(
-        info, group, None, None, partner, inputs, loss, head_row, w_first
-    )
+    even, even_out, odd, odd_out, delta_b = forward_half(info, group, cache, batch_t, partner, loss, head_row, w_first)
     even += send_to(even_out, 1, 0)
     odd += send_to(odd_out, 0, 1)
-    sent = backward(info, evict_from[0, 0], cache, ids, batch_t, delta_a, delta_b, w_first)
+    sent = backward(
+        info, evict_from[0, 0], cache, ids, batch_t, on_chip(delta_a), on_chip(delta_b), w_first
+    )
     even = even[0] + send_to(even[1], 3, 0)
     odd = odd[0] + send_to(odd[1], 0, 3)
     got = lax.all_to_all(sent, "shard", split_axis=0, concat_axis=0, tiled=True)

time: 160 us -> 161 us (level)
  Pallas kernels: 37.4 us -> 35.6 us
  transfers between devices with their start and end apart: 11 -> 11, of which waited for: 6 -> 5; matrix products, arithmetic and copies ran while one was open for 3% -> 4% of each run, Pallas kernels for 11% -> 10%
where the time goes in v5:
time: 161 us; the launch traced here: 160 us
  starting transfers between devices  55.4 us (34%)
  Pallas kernels  35.6 us (22%)
  blocking collectives  31.1 us (19%)
  waiting for transfers between devices  26.8 us (17%)
  local copies, waits for them, and re-layouts  5.62 us (3%)
  other arithmetic  4.43 us (3%)
    all_to_all x1, blocking collectives, local(): lax.all_to_all(served, 'shard', split_axis=0, concat_axis=0, tiled=True)  31.1 us
    ppermute x8, starting transfers between devices, send_to(): return lax.ppermute(a, 'dp', pairs(0, x, y))  21 us
    ppermute x8, waiting for transfers between devices, send_to(): return lax.ppermute(a, 'dp', pairs(0, x, y))  17.7 us
    all_to_all x1, starting transfers between devices, local(): lax.all_to_all(every, 'dp', split_axis=0, concat_axis=0, tiled=True)  13.4 us
    all_to_all x1, starting transfers between devices, local(): got = lax.all_to_all(sent, 'shard', split_axis=0, concat_axis=0, tiled=True)  12.3 us
    pallas_call x1, Pallas kernels, backward(): pl.pallas_call(backward_kernel, out_shape=jax.ShapeDtypeStruct(sent, jnp....  9.38 us
    ppermute x1, starting transfers between devices, local(): partner = on_chip(lax.ppermute(send, 'dp', pairs(1, 0, 0)))  8.73 us
    pallas_call x1, Pallas kernels, forward_half(): pl.pallas_call(second_kernel, out_shape=tuple((jax.ShapeDtypeStruct(piece...  7.62 us
  transfers between devices with their start and end apart: 11, of which 5 were waited for; matrix products, arithmetic and copies ran while one was open for 4% of the time, Pallas kernels for 10%

profile of v5, /device:TPU:1, one launch (start us, length us, event | category | flops | bytes accessed | tf_op | source)
XLA Modules:
  0.0 159.8 jit_solution(9389072243108202247)
XLA Ops:
  0.6 0.7 pad_add_fusion.info
  1.3 7.5 %forward_first.1 = (f32[4,2,2,2,16,8,128]{6,5,4,3,2,1,0:T(8,128)}, bf16[4,128,1024]{2,1,0:T(8,128)(2,1)}) custom-call(s32[4]{0:T(128)} %pad_add_fusion.info, f32[256,384]{1,0:T(8,128)} %bitcast.51, s32[8,1024]{1,0:T(8,128)} %bitcast.58, f32[1,1024]{1,0:T(1,128)} %bitcast.67, f32[1,1024]{1,0:T(1,128)} %bitcast.63, f32[1,1024]{1,0:T(1,128)} %bitcast.64, ...), custom_call_target="tpu_custom_call" | custom-call | tf_op jit(solution)/shard_map/forward_first/pallas_call | solution.py:141
  8.8 8.7 %collective-permute-start = (f32[4,2,2,2,16,8,128]{6,5,4,3,2,1,0:T(8,128)}, f32[4,2,2,2,16,8,128]{6,5,4,3,2,1,0:T(8,128)S(1)}, u32[]{:S(2)}, u32[]{:S(2)}) collective-permute-start(f32[4,2,2,2,16,8,128]{6,5,4,3,2,1,0:T(8,128)} %get-tuple-element.11), channel_id=1, source_target_pairs={{0,1},{1,0},{2,3},{3,2},{4,5},{5,4},{6,7},{7,6},{8,9},{9,8},{10,11... | collective-permute-start | bytes 6291464 | tf_op jit(solution)/shard_map/ppermute | solution.py:455
  17.6 4.0 %collective-permute-done.plus_ref = f32[4,2,2,2,16,8,128]{6,5,4,3,2,1,0:T(8,128)S(1)} collective-permute-done((f32[4,2,2,2,16,8,128]{6,5,4,3,2,1,0:T(8,128)}, f32[4,2,2,2,16,8,128]{6,5,4,3,2,1,0:T(8,128)S(1)}, u32[]{:S(2)}, u32[]{:S(2)}) %collective-permute-start) | collective-permute-done | bytes 2097184 | tf_op jit(solution)/shard_map/ppermute | solution.py:455
  21.6 0.0 copy-start
  21.6 1.3 copy-done
  22.9 0.0 copy-start.1
  22.9 1.6 copy-done.1
  24.5 7.6 %forward_second.1 = (f32[2,2,2,16,8,128]{5,4,3,2,1,0:T(8,128)}, f32[2,2,2,16,8,128]{5,4,3,2,1,0:T(8,128)}, f32[2,2,2,16,8,128]{5,4,3,2,1,0:T(8,128)}, f32[2,2,2,...) custom-call(s32[4]{0:T(128)} %pad_add_fusion.info, f32[4,2,2,2,16,8,128]{6,5,4,3,2,1,0:T(8,128)S(1)} %copy-done.1, ...), custom_call_target="tpu_custom_call" | custom-call | tf_op jit(solution)/shard_map/forward_second/pallas_call | solution.py:155
  32.1 0.0 copy-start.2
  32.1 0.0 copy-start.3
  32.1 2.1 %collective-permute-start.5 = (f32[2,2,2,16,8,128]{5,4,3,2,1,0:T(8,128)}, f32[2,2,2,16,8,128]{5,4,3,2,1,0:T(8,128)S(1)}, u32[]{:S(2)}, u32[]{:S(2)}) collective-permute-start(f32[2,2,2,16,8,128]{5,4,3,2,1,0:T(8,128)} %get-tuple-element.16), channel_id=1, source_target_pairs={{0,2},{1,3},{2,0},{3,1},{4,6},{5,7},{6,4},{7,5},{8,10},{9,11},{10,... | collective-permute-start | bytes 1572872 | tf_op jit(solution)/shard_map/ppermute | solution.py:416
  34.2 1.9 %collective-permute-start.1 = (f32[2,2,2,16,8,128]{5,4,3,2,1,0:T(8,128)}, f32[2,2,2,16,8,128]{5,4,3,2,1,0:T(8,128)}, u32[]{:S(2)}, u32[]{:S(2)}) collective-permute-start(f32[2,2,2,16,8,128]{5,4,3,2,1,0:T(8,128)} %get-tuple-element.14), channel_id=1, source_target_pairs={{0,8},{1,9},{2,10},{3,11},{4,12},{5,13},{6,14},{7,15},{8,0},{9,1},... | collective-permute-start | bytes 1572872 | tf_op jit(solution)/shard_map/ppermute | solution.py:416
  36.1 11.5 %collective-permute-done.5 = f32[2,2,2,16,8,128]{5,4,3,2,1,0:T(8,128)S(1)} collective-permute-done((f32[2,2,2,16,8,128]{5,4,3,2,1,0:T(8,128)}, f32[2,2,2,16,8,128]{5,4,3,2,1,0:T(8,128)S(1)}, u32[]{:S(2)}, u32[]{:S(2)}) %collective-permute-start.5) | collective-permute-done | bytes 524320 | tf_op jit(solution)/shard_map/ppermute | solution.py:416
  47.6 1.1 add.23
  48.7 0.7 slice_bitcast_fusion
  49.4 1.9 %collective-permute-start.6 = (f32[2,2,16,8,128]{4,3,2,1,0:T(8,128)}, f32[2,2,16,8,128]{4,3,2,1,0:T(8,128)S(1)}, u32[]{:S(2)}, u32[]{:S(2)}) collective-permute-start(f32[2,2,16,8,128]{4,3,2,1,0:T(8,128)} %slice_bitcast_fusion), channel_id=1, source_target_pairs={{0,6},{1,7},{2,4},{3,5},{4,2},{5,3},{6,0},{7,1},{8,14},{9,15},{10,... | collective-permute-start | bytes 786440 | tf_op jit(solution)/shard_map/ppermute | solution.py:416
  51.3 3.0 %lookup.1 = s32[16,32]{1,0:T(8,128)} custom-call(s32[1,8192]{1,0:T(1,128)} %home_ref.1, s32[16,16]{1,0:T(8,128)} %bitcast.69, s32[16,16]{1,0:T(8,128)} %bitcast.70, s32[1,16]{1,0:T(1,128)} %bitcast.72), custom_call_target="tpu_custom_call" | custom-call | tf_op jit(solution)/shard_map/lookup/pallas_call | solution.py:301
  54.4 0.7 convert_element_type.26
  55.1 0.6 broadcast_in_dim.15.ids_ref
  55.7 0.0 copy-done.2
  55.7 0.0 copy-done.3
  55.7 9.4 %backward.1 = f32[16,56,128]{2,1,0:T(8,128)} custom-call(s32[4]{0:T(128)} %pad_add_fusion.info, s32[16,16]{1,0:T(8,128)} %bitcast.71, f32[256,384]{1,0:T(8,128)} %bitcast.53, f32[16,8,128]{2,1,0:T(8,128)} %broadcast_in_dim.15.ids_ref, s32[8,1024]{1,0:T(8,128)} %bitcast.60, bf16[4,128,1024]{2,1,0:T(8,128)(2,1)S(1)} %copy-done.2, ...), custom_call_target="tpu_custom_call" | custom-call | tf_op jit(solution)/shard_map/backward/pallas_call | solution.py:231
  65.1 12.3 %all-to-all-start = ((f32[16,56,128]{2,1,0:T(8,128)}), f32[16,56,128]{2,1,0:T(8,128)S(1)}, u32[]{:S(2)}, u32[]{:S(2)}) async-start(f32[16,56,128]{2,1,0:T(8,128)} %backward.1), calls=%async_computation | async-start | bytes 917504 | tf_op jit(solution)/shard_map/all_to_all | solution.py:468
  77.4 0.0 collective-permute-done.1
  77.4 1.3 add.20
  78.7 4.4 %collective-permute-start.2 = (f32[2,2,16,8,128]{4,3,2,1,0:T(8,128)S(1)}, f32[2,2,16,8,128]{4,3,2,1,0:T(8,128)S(1)}, u32[]{:S(2)}, u32[]{:S(2)}) collective-permute-start(f32[2,2,16,8,128]{4,3,2,1,0:T(8,128)S(1)} %slice_bitcast_fusion.2), channel_id=1, source_target_pairs={{0,24},{1,25},{2,26},{3,27},{4,28},{5,29},{6,30},{7,31},{8,16},{9,... | collective-permute-start | bytes 786440 | tf_op jit(solution)/shard_map/ppermute | solution.py:416
  83.1 0.0 collective-permute-done.6
  83.2 1.9 %collective-permute-start.7 = (f32[2,16,8,128]{3,2,1,0:T(8,128)S(1)}, f32[2,16,8,128]{3,2,1,0:T(8,128)S(1)}, u32[]{:S(2)}, u32[]{:S(2)}) collective-permute-start(f32[2,16,8,128]{3,2,1,0:T(8,128)S(1)} %slice_bitcast_fusion.4), channel_id=1, source_target_pairs={{0,8},{1,9},{2,10},{3,11},{4,12},{5,13},{6,14},{7,15},{8,0},{9,1},... | collective-permute-start | bytes 393224 | tf_op jit(solution)/shard_map/ppermute | solution.py:416
  85.1 2.9 %collective-permute-done.2 = f32[2,2,16,8,128]{4,3,2,1,0:T(8,128)S(1)} collective-permute-done((f32[2,2,16,8,128]{4,3,2,1,0:T(8,128)S(1)}, f32[2,2,16,8,128]{4,3,2,1,0:T(8,128)S(1)}, u32[]{:S(2)}, u32[]{:S(2)}) %collective-permute-start.2) | collective-permute-done | bytes 262176 | tf_op jit(solution)/shard_map/ppermute | solution.py:416
  88.1 1.9 %collective-permute-start.3 = (f32[2,16,8,128]{3,2,1,0:T(8,128)S(1)}, f32[2,16,8,128]{3,2,1,0:T(8,128)S(1)}, u32[]{:S(2)}, u32[]{:S(2)}) collective-permute-start(f32[2,16,8,128]{3,2,1,0:T(8,128)S(1)} %slice_bitcast_fusion.6), channel_id=1, source_target_pairs={{0,2},{1,3},{2,0},{3,1},{4,6},{5,7},{6,4},{7,5},{8,10},{9,11},{10,... | collective-permute-start | bytes 393224 | tf_op jit(solution)/shard_map/ppermute | solution.py:416
  90.0 0.0 collective-permute-done.7
  90.0 0.6 slice_bitcast_fusion.8
  90.7 4.4 %collective-permute-start.8 = (f32[16,8,128]{2,1,0:T(8,128)S(1)}, f32[16,8,128]{2,1,0:T(8,128)S(1)}, u32[]{:S(2)}, u32[]{:S(2)}) collective-permute-start(f32[16,8,128]{2,1,0:T(8,128)S(1)} %get-tuple-element.17), channel_id=1, source_target_pairs={{0,24},{1,25},{2,26},{3,27},{4,28},{5,29},{6,30},{7,31},{8,16},{9,... | collective-permute-start | bytes 196616 | tf_op jit(solution)/shard_map/ppermute | solution.py:416
  95.0 0.0 collective-permute-done.3
  95.1 0.6 slice_bitcast_fusion.10
  95.7 2.5 %collective-permute-start.4 = (f32[16,8,128]{2,1,0:T(8,128)S(1)}, f32[16,8,128]{2,1,0:T(8,128)S(1)}, u32[]{:S(2)}, u32[]{:S(2)}) collective-permute-start(f32[16,8,128]{2,1,0:T(8,128)S(1)} %get-tuple-element.19), channel_id=1, source_target_pairs={{0,6},{1,7},{2,4},{3,5},{4,2},{5,3},{6,0},{7,1},{8,14},{9,15},{10,... | collective-permute-start | bytes 196616 | tf_op jit(solution)/shard_map/ppermute | solution.py:416
  98.3 0.0 all-to-all-done.got_ref
  98.3 0.6 slice_convert_fusion
  98.9 0.0 collective-permute-done.8.odd_b
  98.9 3.3 %collective-permute-done.4.even_b = f32[16,8,128]{2,1,0:T(8,128)S(1)} collective-permute-done((f32[16,8,128]{2,1,0:T(8,128)S(1)}, f32[16,8,128]{2,1,0:T(8,128)S(1)}, u32[]{:S(2)}, u32[]{:S(2)}) %collective-permute-start.4) | collective-permute-done | bytes 65568 | tf_op jit(solution)/shard_map/ppermute | solution.py:416
  102.2 2.6 %serve.1 = f32[16,64,128]{2,1,0:T(8,128)} custom-call(s32[16,32]{1,0:T(8,128)} %bitcast.61, f32[512,384]{1,0:T(8,128)} %bitcast.54, f32[16,8,128]{2,1,0:T(8,128)} %get-tuple-element.20.even_a, f32[16,8,128]{2,1,0:T(8,128)S(1)} %collective-permute-done.4.even_b, f32[16,8,128]{2,1,0:T(8,128)} %get-tuple-element.18.odd_a, ...), custom_call_target="tpu_custom_call" | custom-call | tf_op jit(solution)/shard_map/serve/pallas_call | solution.py:276
  104.8 31.1 %all_to_all.15.got_ref = f32[16,64,128]{2,1,0:T(8,128)S(1)} all-to-all(f32[16,64,128]{2,1,0:T(8,128)} %serve.1), channel_id=1, replica_groups=mesh['shard'=16,'dp'=32] {'shard'}, dimensions={0} | all-to-all | bytes 1048576 | tf_op jit(solution)/shard_map/all_to_all | solution.py:475
  135.9 0.7 share_total.1
  136.6 13.4 %all-to-all-start.2 = ((f32[32,16,128]{2,1,0:T(8,128)}), f32[32,16,128]{2,1,0:T(8,128)S(1)}, u32[]{:S(2)}, u32[]{:S(2)}) async-start(f32[32,16,128]{2,1,0:T(8,128)} %share_total.1), calls=%async_computation.2 | async-start | bytes 524288 | tf_op jit(solution)/shard_map/all_to_all | solution.py:479
  150.0 2.5 %settle.1 = f32[512,384]{1,0:T(8,128)} custom-call(s32[16,32]{1,0:T(8,128)} %bitcast.62, f32[16,56,128]{2,1,0:T(8,128)S(1)} %all-to-all-done.got_ref, f32[512,384]{1,0:T(8,128)} %bitcast.55), custom_call_target="tpu_custom_call" | custom-call | tf_op jit(solution)/shard_map/settle/pallas_call | solution.py:352
  152.5 1.4 mask_rows.1
  154.0 5.1 %all-to-all-done.2.every_ref = f32[32,16,128]{2,1,0:T(8,128)S(1)} async-done(((f32[32,16,128]{2,1,0:T(8,128)}), f32[32,16,128]{2,1,0:T(8,128)S(1)}, u32[]{:S(2)}, u32[]{:S(2)}) %all-to-all-start.2) | async-done | bytes 262176 | tf_op jit(solution)/shard_map/all_to_all | solution.py:479
  159.1 0.7 finish.1
  (8 shorter events, 0.1 us)
Async XLA Ops:
  8.8 12.7 %collective-permute-start = (f32[4,2,2,2,16,8,128]{6,5,4,3,2,1,0:T(8,128)}, f32[4,2,2,2,16,8,128]{6,5,4,3,2,1,0:T(8,128)S(1)}, u32[]{:S(2)}, u32[]{:S(2)}) collective-permute-start(f32[4,2,2,2,16,8,128]{6,5,4,3,2,1,0:T(8,128)} %get-tuple-element.11), channel_id=1, source_target_pairs={{0,1},{1,0},{2,3},{3,2},{4,5},{5,4},{6,7},{7,6},{8,9},{9,8},{10,11... | collective-permute-start | bytes 6291464 | tf_op jit(solution)/shard_map/ppermute | solution.py:455
  21.6 1.3 copy-start
  22.9 1.6 copy-start.1
  32.1 23.6 %copy-start.2 = (bf16[4,128,1024]{2,1,0:T(8,128)(2,1)S(1)}, bf16[4,128,1024]{2,1,0:T(8,128)(2,1)}, u32[]{:S(2)}) copy-start(bf16[4,128,1024]{2,1,0:T(8,128)(2,1)} %get-tuple-element.10.delta_a) | copy-start | bytes 3145732
  32.1 23.6 %copy-start.3 = (bf16[4,128,1024]{2,1,0:T(8,128)(2,1)S(1)}, bf16[4,128,1024]{2,1,0:T(8,128)(2,1)}, u32[]{:S(2)}) copy-start(bf16[4,128,1024]{2,1,0:T(8,128)(2,1)} %get-tuple-element.12.delta_b) | copy-start | bytes 3145732
  32.1 15.5 %collective-permute-start.5 = (f32[2,2,2,16,8,128]{5,4,3,2,1,0:T(8,128)}, f32[2,2,2,16,8,128]{5,4,3,2,1,0:T(8,128)S(1)}, u32[]{:S(2)}, u32[]{:S(2)}) collective-permute-start(f32[2,2,2,16,8,128]{5,4,3,2,1,0:T(8,128)} %get-tuple-element.16), channel_id=1, source_target_pairs={{0,2},{1,3},{2,0},{3,1},{4,6},{5,7},{6,4},{7,5},{8,10},{9,11},{10,... | collective-permute-start | bytes 1572872 | tf_op jit(solution)/shard_map/ppermute | solution.py:416
  34.2 43.2 %collective-permute-start.1 = (f32[2,2,2,16,8,128]{5,4,3,2,1,0:T(8,128)}, f32[2,2,2,16,8,128]{5,4,3,2,1,0:T(8,128)}, u32[]{:S(2)}, u32[]{:S(2)}) collective-permute-start(f32[2,2,2,16,8,128]{5,4,3,2,1,0:T(8,128)} %get-tuple-element.14), channel_id=1, source_target_pairs={{0,8},{1,9},{2,10},{3,11},{4,12},{5,13},{6,14},{7,15},{8,0},{9,1},... | collective-permute-start | bytes 1572872 | tf_op jit(solution)/shard_map/ppermute | solution.py:416
  49.4 33.7 %collective-permute-start.6 = (f32[2,2,16,8,128]{4,3,2,1,0:T(8,128)}, f32[2,2,16,8,128]{4,3,2,1,0:T(8,128)S(1)}, u32[]{:S(2)}, u32[]{:S(2)}) collective-permute-start(f32[2,2,16,8,128]{4,3,2,1,0:T(8,128)} %slice_bitcast_fusion), channel_id=1, source_target_pairs={{0,6},{1,7},{2,4},{3,5},{4,2},{5,3},{6,0},{7,1},{8,14},{9,15},{10,... | collective-permute-start | bytes 786440 | tf_op jit(solution)/shard_map/ppermute | solution.py:416
  65.1 33.2 %all-to-all-start = ((f32[16,56,128]{2,1,0:T(8,128)}), f32[16,56,128]{2,1,0:T(8,128)S(1)}, u32[]{:S(2)}, u32[]{:S(2)}) async-start(f32[16,56,128]{2,1,0:T(8,128)} %backward.1), calls=%async_computation | async-start | bytes 917504 | tf_op jit(solution)/shard_map/all_to_all | solution.py:468
  78.7 9.3 %collective-permute-start.2 = (f32[2,2,16,8,128]{4,3,2,1,0:T(8,128)S(1)}, f32[2,2,16,8,128]{4,3,2,1,0:T(8,128)S(1)}, u32[]{:S(2)}, u32[]{:S(2)}) collective-permute-start(f32[2,2,16,8,128]{4,3,2,1,0:T(8,128)S(1)} %slice_bitcast_fusion.2), channel_id=1, source_target_pairs={{0,24},{1,25},{2,26},{3,27},{4,28},{5,29},{6,30},{7,31},{8,16},{9,... | collective-permute-start | bytes 786440 | tf_op jit(solution)/shard_map/ppermute | solution.py:416
  83.2 6.8 %collective-permute-start.7 = (f32[2,16,8,128]{3,2,1,0:T(8,128)S(1)}, f32[2,16,8,128]{3,2,1,0:T(8,128)S(1)}, u32[]{:S(2)}, u32[]{:S(2)}) collective-permute-start(f32[2,16,8,128]{3,2,1,0:T(8,128)S(1)} %slice_bitcast_fusion.4), channel_id=1, source_target_pairs={{0,8},{1,9},{2,10},{3,11},{4,12},{5,13},{6,14},{7,15},{8,0},{9,1},... | collective-permute-start | bytes 393224 | tf_op jit(solution)/shard_map/ppermute | solution.py:416
  88.1 7.0 %collective-permute-start.3 = (f32[2,16,8,128]{3,2,1,0:T(8,128)S(1)}, f32[2,16,8,128]{3,2,1,0:T(8,128)S(1)}, u32[]{:S(2)}, u32[]{:S(2)}) collective-permute-start(f32[2,16,8,128]{3,2,1,0:T(8,128)S(1)} %slice_bitcast_fusion.6), channel_id=1, source_target_pairs={{0,2},{1,3},{2,0},{3,1},{4,6},{5,7},{6,4},{7,5},{8,10},{9,11},{10,... | collective-permute-start | bytes 393224 | tf_op jit(solution)/shard_map/ppermute | solution.py:416
  90.7 8.2 %collective-permute-start.8 = (f32[16,8,128]{2,1,0:T(8,128)S(1)}, f32[16,8,128]{2,1,0:T(8,128)S(1)}, u32[]{:S(2)}, u32[]{:S(2)}) collective-permute-start(f32[16,8,128]{2,1,0:T(8,128)S(1)} %get-tuple-element.17), channel_id=1, source_target_pairs={{0,24},{1,25},{2,26},{3,27},{4,28},{5,29},{6,30},{7,31},{8,16},{9,... | collective-permute-start | bytes 196616 | tf_op jit(solution)/shard_map/ppermute | solution.py:416
  95.7 6.5 %collective-permute-start.4 = (f32[16,8,128]{2,1,0:T(8,128)S(1)}, f32[16,8,128]{2,1,0:T(8,128)S(1)}, u32[]{:S(2)}, u32[]{:S(2)}) collective-permute-start(f32[16,8,128]{2,1,0:T(8,128)S(1)} %get-tuple-element.19), channel_id=1, source_target_pairs={{0,6},{1,7},{2,4},{3,5},{4,2},{5,3},{6,0},{7,1},{8,14},{9,15},{10,... | collective-permute-start | bytes 196616 | tf_op jit(solution)/shard_map/ppermute | solution.py:416
  136.6 22.5 %all-to-all-start.2 = ((f32[32,16,128]{2,1,0:T(8,128)}), f32[32,16,128]{2,1,0:T(8,128)S(1)}, u32[]{:S(2)}, u32[]{:S(2)}) async-start(f32[32,16,128]{2,1,0:T(8,128)} %share_total.1), calls=%async_computation.2 | async-start | bytes 524288 | tf_op jit(solution)/shard_map/all_to_all | solution.py:479

commit v6 on v5

--- a/solution.py
+++ b/solution.py
@@ -62,11 +62,12 @@
                     if plus_ref is not None:
                         even += plus_ref[u, j, v, o, z]
                         odd += plus_ref[2 + v, j, o, u, z]
-                    outs[u][0, v, o, z] = even
                     if plus_ref is None:
+                        outs[u][0, v, o, z] = even
                         outs[2 + v][0, o, u, z] = odd
                     else:
-                        outs[2 + v][o, u, 0, z] = odd
+                        outs[u][v, 0, o, z] = even
+                        outs[2 + v][u, 0, o, z] = odd
 
 
 def gather(cache_ref, batch_ref, inputs_ref):
@@ -150,8 +151,7 @@
             ),
             name="forward_first",
         )(info, cache, batch_t, loss, head, head, w, w)
-    even_spec = pl.BlockSpec((1,) + piece[1:], lambda j, c: (j, 0, 0, 0, 0, 0))
-    odd_spec = pl.BlockSpec((2, 2, 1) + piece[3:], lambda j, c: (0, 0, j, 0, 0, 0))
+    out_spec = pl.BlockSpec((2, 1, 2) + piece[3:], lambda j, c: (0, j, 0, 0, 0, 0))
     return pl.pallas_call(
         second_kernel,
         out_shape=tuple(jax.ShapeDtypeStruct(piece, jnp.float32) for _ in range(4)) + (delta,),
@@ -159,7 +159,7 @@
             num_scalar_prefetch=1,
             grid=(2,),
             in_specs=[pl.BlockSpec(memory_space=pltpu.VMEM)] + specs,
-            out_specs=(even_spec, even_spec, odd_spec, odd_spec, delta_spec),
+            out_specs=(out_spec,) * 4 + (delta_spec,),
             scratch_shapes=scratch,
         ),
         name="forward_second",
@@ -167,14 +167,38 @@
 
 
 def backward_kernel(
-    info, leaving, cache_ref, ids_ref, batch_ref, delta_a, delta_b, w_a, w_b, sent_ref, acc_ref, upd_ref
+    info,
+    leaving,
+    cache_ref,
+    ids_ref,
+    batch_ref,
+    delta_a,
+    delta_hbm,
+    w_a,
+    w_b,
+    sent_ref,
+    acc_ref,
+    upd_ref,
+    delta_b,
+    arrived,
 ):
     rows, width = cache_ref.shape
     embed = width // 3
     owners, capacity = leaving.shape
     step = pl.program_id(0)
     half = w_a.shape[1]
+    copy = pltpu.make_async_copy(delta_hbm, delta_b, arrived)
+
+    @pl.when(step == 0)
+    def _():
+        copy.start()
+
     back = lax.dot_general(w_a[...], delta_a[...].reshape(half, -1), NN, preferred_element_type=jnp.float32)
+
+    @pl.when(step == 0)
+    def _():
+        copy.wait()
+
     back += lax.dot_general(w_b[...], delta_b[...].reshape(half, -1), NN, preferred_element_type=jnp.float32)
     total = None
     for k in range(w_a.shape[0] // embed):
@@ -239,22 +263,27 @@
                 fixed(ids.shape),
                 fixed(batch_t.shape),
                 whole,
-                whole,
+                pl.BlockSpec(memory_space=pl.ANY),
                 pl.BlockSpec((2 * embed, half), lambda j, c, e: (j, c[0])),
                 pl.BlockSpec((2 * embed, half), lambda j, c, e: (j, c[1])),
             ],
             out_specs=fixed(sent),
-            scratch_shapes=[pltpu.VMEM((2 * embed, rows), jnp.float32), pltpu.VMEM((rows, width3), jnp.float32)],
+            scratch_shapes=[
+                pltpu.VMEM((2 * embed, rows), jnp.float32),
+                pltpu.VMEM((rows, width3), jnp.float32),
+                pltpu.VMEM(delta_b.shape, delta_b.dtype),
+                pltpu.SemaphoreType.DMA(()),
+            ],
         ),
         name="backward",
     )(info, leaving, cache, ids, batch_t, delta_a, delta_b, w, w)
 
 
-def serve_kernel(asked_ref, table_ref, even_a, even_b, odd_a, odd_b, out_ref):
+def serve_kernel(asked_ref, table_ref, out_ref):
     owners, both = asked_ref.shape
     capacity = both // 2
     embed = out_ref.shape[2]
-    rows = even_a.shape[1]
+    out_ref[:, 3 * capacity :, :] = jnp.zeros((owners, out_ref.shape[1] - 3 * capacity, embed), out_ref.dtype)
 
     def fetch(i, carry):
         for k in range(capacity):
@@ -265,20 +294,37 @@
         return carry
 
     lax.fori_loop(0, owners, fetch, 0)
-    out_ref[:, 3 * capacity : 3 * capacity + rows, :] = even_a[...] + even_b[...]
-    out_ref[:, 3 * capacity + rows :, :] = odd_a[...] + odd_b[...]
-
-
-def serve(asked, table, even, odd):
+
+
+def serve(asked, table, rows):
     owners, both = asked.shape
-    _, rows, embed = even[0].shape
+    return pl.pallas_call(
+        serve_kernel,
+        out_shape=jax.ShapeDtypeStruct((owners, 3 * both // 2 + rows, table.shape[1] // 3), jnp.float32),
+        in_specs=[pl.BlockSpec(memory_space=pltpu.SMEM), pl.BlockSpec(table.shape)],
+        name="serve",
+    )(asked, table)
+
+
+def block_kernel(mine_ref, other_ref, served_ref, out_ref):
+    rows = mine_ref.shape[2]
+    for k in range(2):
+        out_ref[:, k * rows : (k + 1) * rows, :] = mine_ref[k] + other_ref[k]
+
+
+def add_block(mine, other, served):
+    colours, owners, rows, embed = other.shape
     whole = pl.BlockSpec(memory_space=pltpu.VMEM)
-    return pl.pallas_call(
-        serve_kernel,
-        out_shape=jax.ShapeDtypeStruct((owners, 3 * both // 2 + 2 * rows, embed), jnp.float32),
-        in_specs=[pl.BlockSpec(memory_space=pltpu.SMEM), pl.BlockSpec(table.shape)] + [whole] * 4,
-        name="serve",
-    )(asked, table, *even, *odd)
+    block = colours * rows
+    return pl.pallas_call(
+        block_kernel,
+        out_shape=jax.ShapeDtypeStruct(served.shape, served.dtype),
+        grid=(1,),
+        in_specs=[whole, whole, pl.BlockSpec(memory_space=pl.ANY)],
+        out_specs=pl.BlockSpec((owners, block, embed), lambda j: (0, served.shape[1] // block - 1, 0)),
+        input_output_aliases={2: 0},
+        name="add_block",
+    )(mine, other, served)
 
 
 def lookup_kernel(home_ref, wanted_ref, gone_ref, counts_ref, out_ref, *, table_rows):
@@ -457,21 +503,19 @@
     lanes = cache.shape[1] // 3
     ids = jnp.pad(slots.astype(jnp.float32), ((0, 0), (0, lanes - slots.shape[1])))
     ids = jnp.broadcast_to(ids[:, None, :], (group, 8, lanes))
+    loss, ids = lax.optimization_barrier((loss, ids))
     even, even_out, odd, odd_out, delta_b = forward_half(info, group, cache, batch_t, partner, loss, head_row, w_first)
-    even += send_to(even_out, 1, 0)
-    odd += send_to(odd_out, 0, 1)
-    sent = backward(
-        info, evict_from[0, 0], cache, ids, batch_t, on_chip(delta_a), on_chip(delta_b), w_first
-    )
-    even = even[0] + send_to(even[1], 3, 0)
-    odd = odd[0] + send_to(odd[1], 0, 3)
+    even_in = send_to(even_out, 1, 0)
+    odd_in = send_to(odd_out, 0, 1)
+    sent = backward(info, evict_from[0, 0], cache, ids, batch_t, on_chip(delta_a), delta_b, w_first)
     got = lax.all_to_all(sent, "shard", split_axis=0, concat_axis=0, tiled=True)
-    even = even[0] + send_to(even[1], 0, 1)
-    odd = odd[0] + send_to(odd[1], 1, 0)
-    even = (even[0], on_chip(send_to(even[1], 0, 3)))
-    odd = (odd[0], on_chip(send_to(odd[1], 3, 0)))
+    even = even[0] + even_in[0] + send_to(even[1] + even_in[1], 0, 1)
+    odd = odd[0] + odd_in[0] + send_to(odd[1] + odd_in[1], 1, 0)
+    mine = jnp.stack([even[0], odd[0]], 1) + send_to(jnp.stack([even[1], odd[1]], 1), 3, 0)
+    other = send_to(mine[1], 0, 3)
     asked = got[:, 3 * capacity, : 2 * capacity].astype(jnp.int32)
-    served = serve(asked, table, even, odd)
+    served = serve(asked, table, 2 * mine.shape[3])
+    served = add_block(on_chip(mine[0]), on_chip(other), served)
     came = on_chip(lax.all_to_all(served, "shard", split_axis=0, concat_axis=0, tiled=True))
     new_table = settle(asked, on_chip(got), table)
     scale = 1.0 / math.sqrt(samples * group * devices)

time: 161 us -> 154 us (0.957)
  local copies, waits for them, and re-layouts: 5.62 us -> 0.72 us
  starting transfers between devices: 55.4 us -> 52.6 us
  Pallas kernels: 35.6 us -> 38 us
    ppermute x1, waiting for transfers between devices: 3.97 us -> 0.01 us  [local(): partner = on_chip(lax.ppermute(send, 'dp', pairs(1, 0, 0)))]
    ppermute x8 -> x6, starting transfers between devices: 21 us -> 17.1 us  [send_to(): return lax.ppermute(a, 'dp', pairs(0, x, y))]
    unnamed x8 -> x6, local copies, waits for them, and re-layouts: 2.94 us -> 0.01 us
    ppermute x8 -> x6, waiting for transfers between devices: 17.7 us -> 20.4 us  [send_to(): return lax.ppermute(a, 'dp', pairs(0, x, y))]
    all_to_all x1, starting transfers between devices: 13.4 us -> 15.9 us  [local(): lax.all_to_all(every, 'dp', split_axis=0, concat_axis=0, tiled=True)]
    squeeze x6 -> x1, local copies, waits for them, and re-layouts: 2.04 us -> 0.02 us  [local(): other = send_to(mine[1], 0, 3)]
    pallas_call x1, Pallas kernels: 9.38 us -> 11 us  [backward(): pl.pallas_call(backward_kernel, out_shape=jax.ShapeDtypeStruct(sent, jnp....]
  transfers between devices with their start and end apart: 11 -> 9, of which waited for: 5 -> 5; matrix products, arithmetic and copies ran while one was open for 4% -> 3% of each run, Pallas kernels for 10% -> 13%
where the time goes in v6:
time: 154 us; the launch traced here: 153 us
  starting transfers between devices  52.6 us (34%)
  Pallas kernels  38 us (25%)
  blocking collectives  31.3 us (20%)
  waiting for transfers between devices  25.4 us (16%)
  other arithmetic  4.06 us (3%)
    all_to_all x1, blocking collectives, local(): lax.all_to_all(served, 'shard', split_axis=0, concat_axis=0, tiled=True)  31.3 us
    ppermute x6, waiting for transfers between devices, send_to(): return lax.ppermute(a, 'dp', pairs(0, x, y))  20.4 us
    ppermute x6, starting transfers between devices, send_to(): return lax.ppermute(a, 'dp', pairs(0, x, y))  17.1 us
    all_to_all x1, starting transfers between devices, local(): lax.all_to_all(every, 'dp', split_axis=0, concat_axis=0, tiled=True)  15.9 us
    pallas_call x1, Pallas kernels, backward(): pl.pallas_call(backward_kernel, out_shape=jax.ShapeDtypeStruct(sent, jnp....  11 us
    all_to_all x1, starting transfers between devices, local(): got = lax.all_to_all(sent, 'shard', split_axis=0, concat_axis=0, tiled=True)  10.9 us
    ppermute x1, starting transfers between devices, local(): partner = on_chip(lax.ppermute(send, 'dp', pairs(1, 0, 0)))  8.73 us
    pallas_call x1, Pallas kernels, forward_half(): pl.pallas_call(second_kernel, out_shape=tuple((jax.ShapeDtypeStruct(piece...  7.76 us
  transfers between devices with their start and end apart: 9, of which 5 were waited for; matrix products, arithmetic and copies ran while one was open for 3% of the time, Pallas kernels for 13%

profile of v6, /device:TPU:1, one launch (start us, length us, event | category | flops | bytes accessed | tf_op | source)
XLA Modules:
  0.0 152.9 jit_solution(6828728536143553763)
XLA Ops:
  0.6 0.6 pad_add_fusion.info
  1.3 7.6 %forward_first.1 = (f32[4,2,2,2,16,8,128]{6,5,4,3,2,1,0:T(8,128)}, bf16[4,128,1024]{2,1,0:T(8,128)(2,1)}) custom-call(s32[4]{0:T(128)} %pad_add_fusion.info, f32[256,384]{1,0:T(8,128)} %bitcast.45, s32[8,1024]{1,0:T(8,128)} %bitcast.52, f32[1,1024]{1,0:T(1,128)} %bitcast.61, f32[1,1024]{1,0:T(1,128)} %bitcast.57, f32[1,1024]{1,0:T(1,128)} %bitcast.58, ...), custom_call_target="tpu_custom_call" | custom-call | tf_op jit(solution)/shard_map/forward_first/pallas_call | solution.py:142
  8.8 8.7 %collective-permute-start = (f32[4,2,2,2,16,8,128]{6,5,4,3,2,1,0:T(8,128)}, f32[4,2,2,2,16,8,128]{6,5,4,3,2,1,0:T(8,128)S(1)}, u32[]{:S(2)}, u32[]{:S(2)}) collective-permute-start(f32[4,2,2,2,16,8,128]{6,5,4,3,2,1,0:T(8,128)} %get-tuple-element.12), channel_id=1, source_target_pairs={{0,1},{1,0},{2,3},{3,2},{4,5},{5,4},{6,7},{7,6},{8,9},{9,8},{10,11... | collective-permute-start | bytes 6291464 | tf_op jit(solution)/shard_map/ppermute | solution.py:501
  17.6 3.0 %lookup.1 = s32[16,32]{1,0:T(8,128)} custom-call(s32[1,8192]{1,0:T(1,128)} %home_ref.1, s32[16,16]{1,0:T(8,128)} %bitcast.63, s32[16,16]{1,0:T(8,128)} %bitcast.64, s32[1,16]{1,0:T(1,128)} %bitcast.66), custom_call_target="tpu_custom_call" | custom-call | tf_op jit(solution)/shard_map/lookup/pallas_call | solution.py:347
  20.6 0.7 convert_element_type.26
  21.3 0.6 broadcast_in_dim.16.ids_ref
  22.0 0.0 copy-start
  22.0 0.0 collective-permute-done.plus_ref
  22.0 7.8 %forward_second.1 = (f32[2,2,2,16,8,128]{5,4,3,2,1,0:T(8,128)}, f32[2,2,2,16,8,128]{5,4,3,2,1,0:T(8,128)}, f32[2,2,2,16,8,128]{5,4,3,2,1,0:T(8,128)}, f32[2,2,2,...) custom-call(s32[4]{0:T(128)} %pad_add_fusion.info, f32[4,2,2,2,16,8,128]{6,5,4,3,2,1,0:T(8,128)S(1)} %collective-permute-done.plus_ref, ...), custom_call_target="tpu_custom_call" | custom-call | tf_op jit(solution)/shard_map/forward_second/pallas_call | solution.py:155
  29.7 1.9 %collective-permute-start.1 = (f32[2,2,2,16,8,128]{5,4,3,2,1,0:T(8,128)}, f32[2,2,2,16,8,128]{5,4,3,2,1,0:T(8,128)S(1)}, u32[]{:S(2)}, u32[]{:S(2)}) collective-permute-start(f32[2,2,2,16,8,128]{5,4,3,2,1,0:T(8,128)} %get-tuple-element.15), channel_id=1, source_target_pairs={{0,8},{1,9},{2,10},{3,11},{4,12},{5,13},{6,14},{7,15},{8,0},{9,1},... | collective-permute-start | bytes 1572872 | tf_op jit(solution)/shard_map/ppermute | solution.py:462
  31.6 1.9 %collective-permute-start.3 = (f32[2,2,2,16,8,128]{5,4,3,2,1,0:T(8,128)}, f32[2,2,2,16,8,128]{5,4,3,2,1,0:T(8,128)S(1)}, u32[]{:S(2)}, u32[]{:S(2)}) collective-permute-start(f32[2,2,2,16,8,128]{5,4,3,2,1,0:T(8,128)} %get-tuple-element.17), channel_id=1, source_target_pairs={{0,2},{1,3},{2,0},{3,1},{4,6},{5,7},{6,4},{7,5},{8,10},{9,11},{10,... | collective-permute-start | bytes 1572872 | tf_op jit(solution)/shard_map/ppermute | solution.py:462
  33.6 11.7 %collective-permute-done.1 = f32[2,2,2,16,8,128]{5,4,3,2,1,0:T(8,128)S(1)} collective-permute-done((f32[2,2,2,16,8,128]{5,4,3,2,1,0:T(8,128)}, f32[2,2,2,16,8,128]{5,4,3,2,1,0:T(8,128)S(1)}, u32[]{:S(2)}, u32[]{:S(2)}) %collective-permute-start.1) | collective-permute-done | bytes 524320 | tf_op jit(solution)/shard_map/ppermute | solution.py:462
  45.3 1.0 fusion.3
  46.3 1.9 %collective-permute-start.2 = (f32[2,2,16,8,128]{4,3,2,1,0:T(8,128)S(1)}, f32[2,2,16,8,128]{4,3,2,1,0:T(8,128)}, u32[]{:S(2)}, u32[]{:S(2)}) collective-permute-start(f32[2,2,16,8,128]{4,3,2,1,0:T(8,128)S(1)} %fusion.3), channel_id=1, source_target_pairs={{0,2},{1,3},{2,0},{3,1},{4,6},{5,7},{6,4},{7,5},{8,10},{9,11},{10,... | collective-permute-start | bytes 786440 | tf_op jit(solution)/shard_map/ppermute | solution.py:462
  48.2 0.0 copy-done
  48.2 0.0 copy-start.1
  48.2 0.0 copy-start.2
  48.2 11.0 %backward.1 = f32[16,56,128]{2,1,0:T(8,128)} custom-call(s32[4]{0:T(128)} %pad_add_fusion.info, s32[16,16]{1,0:T(8,128)} %bitcast.65, f32[256,384]{1,0:T(8,128)} %bitcast.47, f32[16,8,128]{2,1,0:T(8,128)} %broadcast_in_dim.16.ids_ref, s32[8,1024]{1,0:T(8,128)} %bitcast.54, bf16[4,128,1024]{2,1,0:T(8,128)(2,1)S(1)} %copy-done, ...), custom_call_target="tpu_custom_call" | custom-call | tf_op jit(solution)/shard_map/backward/pallas_call | solution.py:255
  59.3 10.9 %all-to-all-start = ((f32[16,56,128]{2,1,0:T(8,128)}), f32[16,56,128]{2,1,0:T(8,128)S(1)}, u32[]{:S(2)}, u32[]{:S(2)}) async-start(f32[16,56,128]{2,1,0:T(8,128)} %backward.1), calls=%async_computation | async-start | bytes 917504 | tf_op jit(solution)/shard_map/all_to_all | solution.py:511
  70.1 0.0 collective-permute-done.3
  70.1 0.0 copy-done.1
  70.2 3.2 %collective-permute-start.4 = (f32[2,2,16,8,128]{4,3,2,1,0:T(8,128)S(1)}, f32[2,2,16,8,128]{4,3,2,1,0:T(8,128)S(1)}, u32[]{:S(2)}, u32[]{:S(2)}) collective-permute-start(f32[2,2,16,8,128]{4,3,2,1,0:T(8,128)S(1)} %fusion), channel_id=1, source_target_pairs={{0,8},{1,9},{2,10},{3,11},{4,12},{5,13},{6,14},{7,15},{8,0},{9,1},... | collective-permute-start | bytes 786440 | tf_op jit(solution)/shard_map/ppermute | solution.py:462
  73.4 0.0 collective-permute-done.2
  73.4 0.0 copy-done.2
  73.4 1.0 fusion.5
  74.4 4.1 %collective-permute-done.4 = f32[2,2,16,8,128]{4,3,2,1,0:T(8,128)S(1)} collective-permute-done((f32[2,2,16,8,128]{4,3,2,1,0:T(8,128)S(1)}, f32[2,2,16,8,128]{4,3,2,1,0:T(8,128)S(1)}, u32[]{:S(2)}, u32[]{:S(2)}) %collective-permute-start.4) | collective-permute-done | bytes 262176 | tf_op jit(solution)/shard_map/ppermute | solution.py:462
  78.5 0.1 fusion.2
  78.6 4.4 %collective-permute-start.5 = (f32[2,2,16,8,128]{4,3,2,1,0:T(8,128)S(1)}, f32[2,2,16,8,128]{4,3,2,1,0:T(8,128)S(1)}, u32[]{:S(2)}, u32[]{:S(2)}) collective-permute-start(f32[2,2,16,8,128]{4,3,2,1,0:T(8,128)S(1)} %pad_maximum_fusion.1), channel_id=1, source_target_pairs={{0,24},{1,25},{2,26},{3,27},{4,28},{5,29},{6,30},{7,31},{8,16},{9,... | collective-permute-start | bytes 786440 | tf_op jit(solution)/shard_map/ppermute | solution.py:462
  83.0 4.3 %collective-permute-done.5 = f32[2,2,16,8,128]{4,3,2,1,0:T(8,128)S(1)} collective-permute-done((f32[2,2,16,8,128]{4,3,2,1,0:T(8,128)S(1)}, f32[2,2,16,8,128]{4,3,2,1,0:T(8,128)S(1)}, u32[]{:S(2)}, u32[]{:S(2)}) %collective-permute-start.5) | collective-permute-done | bytes 262176 | tf_op jit(solution)/shard_map/ppermute | solution.py:462
  87.4 3.8 %collective-permute-start.6 = (f32[2,16,8,128]{3,2,1,0:T(8,128)S(1)}, f32[2,16,8,128]{3,2,1,0:T(8,128)S(1)}, u32[]{:S(2)}, u32[]{:S(2)}) collective-permute-start(f32[2,16,8,128]{3,2,1,0:T(8,128)S(1)} %get-tuple-element.21), channel_id=1, source_target_pairs={{0,6},{1,7},{2,4},{3,5},{4,2},{5,3},{6,0},{7,1},{8,14},{9,15},{10,... | collective-permute-start | bytes 393224 | tf_op jit(solution)/shard_map/ppermute | solution.py:462
  91.2 0.0 all-to-all-done.got_ref
  91.2 0.6 slice_convert_fusion
  91.8 2.5 %serve.1.served_ref = f32[16,64,128]{2,1,0:T(8,128)} custom-call(s32[16,32]{1,0:T(8,128)} %bitcast.55, f32[512,384]{1,0:T(8,128)} %bitcast.48), custom_call_target="tpu_custom_call" | custom-call | tf_op jit(solution)/shard_map/serve/pallas_call | solution.py:301
  94.4 0.2 collective-permute-done.6.other_ref
  94.6 0.7 add_block.1
  95.3 31.3 %all_to_all.15.got_ref = f32[16,64,128]{2,1,0:T(8,128)S(1)} all-to-all(f32[16,64,128]{2,1,0:T(8,128)} %add_block.1), channel_id=1, replica_groups=mesh['shard'=16,'dp'=32] {'shard'}, dimensions={0} | all-to-all | bytes 1048576 | tf_op jit(solution)/shard_map/all_to_all | solution.py:519
  126.6 0.7 share_total.1
  127.3 15.9 %all-to-all-start.2 = ((f32[32,16,128]{2,1,0:T(8,128)}), f32[32,16,128]{2,1,0:T(8,128)S(1)}, u32[]{:S(2)}, u32[]{:S(2)}) async-start(f32[32,16,128]{2,1,0:T(8,128)} %share_total.1), calls=%async_computation.2 | async-start | bytes 524288 | tf_op jit(solution)/shard_map/all_to_all | solution.py:523
  143.2 2.6 %settle.1 = f32[512,384]{1,0:T(8,128)} custom-call(s32[16,32]{1,0:T(8,128)} %bitcast.56, f32[16,56,128]{2,1,0:T(8,128)S(1)} %all-to-all-done.got_ref, f32[512,384]{1,0:T(8,128)} %bitcast.49), custom_call_target="tpu_custom_call" | custom-call | tf_op jit(solution)/shard_map/settle/pallas_call | solution.py:398
  145.8 1.4 mask_rows.1
  147.2 5.0 %all-to-all-done.2.every_ref = f32[32,16,128]{2,1,0:T(8,128)S(1)} async-done(((f32[32,16,128]{2,1,0:T(8,128)}), f32[32,16,128]{2,1,0:T(8,128)S(1)}, u32[]{:S(2)}, u32[]{:S(2)}) %all-to-all-start.2) | async-done | bytes 262176 | tf_op jit(solution)/shard_map/all_to_all | solution.py:523
  152.2 0.7 finish.1
  (7 shorter events, 0.2 us)
Async XLA Ops:
  8.8 13.1 %collective-permute-start = (f32[4,2,2,2,16,8,128]{6,5,4,3,2,1,0:T(8,128)}, f32[4,2,2,2,16,8,128]{6,5,4,3,2,1,0:T(8,128)S(1)}, u32[]{:S(2)}, u32[]{:S(2)}) collective-permute-start(f32[4,2,2,2,16,8,128]{6,5,4,3,2,1,0:T(8,128)} %get-tuple-element.12), channel_id=1, source_target_pairs={{0,1},{1,0},{2,3},{3,2},{4,5},{5,4},{6,7},{7,6},{8,9},{9,8},{10,11... | collective-permute-start | bytes 6291464 | tf_op jit(solution)/shard_map/ppermute | solution.py:501
  22.0 26.2 %copy-start = (bf16[4,128,1024]{2,1,0:T(8,128)(2,1)S(1)}, bf16[4,128,1024]{2,1,0:T(8,128)(2,1)}, u32[]{:S(2)}) copy-start(bf16[4,128,1024]{2,1,0:T(8,128)(2,1)} %get-tuple-element.19.delta_a) | copy-start | bytes 3145732
  29.7 15.6 %collective-permute-start.1 = (f32[2,2,2,16,8,128]{5,4,3,2,1,0:T(8,128)}, f32[2,2,2,16,8,128]{5,4,3,2,1,0:T(8,128)S(1)}, u32[]{:S(2)}, u32[]{:S(2)}) collective-permute-start(f32[2,2,2,16,8,128]{5,4,3,2,1,0:T(8,128)} %get-tuple-element.15), channel_id=1, source_target_pairs={{0,8},{1,9},{2,10},{3,11},{4,12},{5,13},{6,14},{7,15},{8,0},{9,1},... | collective-permute-start | bytes 1572872 | tf_op jit(solution)/shard_map/ppermute | solution.py:462
  31.6 38.5 %collective-permute-start.3 = (f32[2,2,2,16,8,128]{5,4,3,2,1,0:T(8,128)}, f32[2,2,2,16,8,128]{5,4,3,2,1,0:T(8,128)S(1)}, u32[]{:S(2)}, u32[]{:S(2)}) collective-permute-start(f32[2,2,2,16,8,128]{5,4,3,2,1,0:T(8,128)} %get-tuple-element.17), channel_id=1, source_target_pairs={{0,2},{1,3},{2,0},{3,1},{4,6},{5,7},{6,4},{7,5},{8,10},{9,11},{10,... | collective-permute-start | bytes 1572872 | tf_op jit(solution)/shard_map/ppermute | solution.py:462
  46.3 27.1 %collective-permute-start.2 = (f32[2,2,16,8,128]{4,3,2,1,0:T(8,128)S(1)}, f32[2,2,16,8,128]{4,3,2,1,0:T(8,128)}, u32[]{:S(2)}, u32[]{:S(2)}) collective-permute-start(f32[2,2,16,8,128]{4,3,2,1,0:T(8,128)S(1)} %fusion.3), channel_id=1, source_target_pairs={{0,2},{1,3},{2,0},{3,1},{4,6},{5,7},{6,4},{7,5},{8,10},{9,11},{10,... | collective-permute-start | bytes 786440 | tf_op jit(solution)/shard_map/ppermute | solution.py:462
  48.2 21.9 %copy-start.1 = (f32[2,2,2,16,8,128]{5,4,3,2,1,0:T(8,128)S(1)}, f32[2,2,2,16,8,128]{5,4,3,2,1,0:T(8,128)}, u32[]{:S(2)}) copy-start(f32[2,2,2,16,8,128]{5,4,3,2,1,0:T(8,128)} %get-tuple-element.16) | copy-start | bytes 1572868
  48.2 25.1 %copy-start.2 = (f32[2,2,2,16,8,128]{5,4,3,2,1,0:T(8,128)S(1)}, f32[2,2,2,16,8,128]{5,4,3,2,1,0:T(8,128)}, u32[]{:S(2)}) copy-start(f32[2,2,2,16,8,128]{5,4,3,2,1,0:T(8,128)} %get-tuple-element.14) | copy-start | bytes 1572868
  59.3 31.9 %all-to-all-start = ((f32[16,56,128]{2,1,0:T(8,128)}), f32[16,56,128]{2,1,0:T(8,128)S(1)}, u32[]{:S(2)}, u32[]{:S(2)}) async-start(f32[16,56,128]{2,1,0:T(8,128)} %backward.1), calls=%async_computation | async-start | bytes 917504 | tf_op jit(solution)/shard_map/all_to_all | solution.py:511
  70.2 8.3 %collective-permute-start.4 = (f32[2,2,16,8,128]{4,3,2,1,0:T(8,128)S(1)}, f32[2,2,16,8,128]{4,3,2,1,0:T(8,128)S(1)}, u32[]{:S(2)}, u32[]{:S(2)}) collective-permute-start(f32[2,2,16,8,128]{4,3,2,1,0:T(8,128)S(1)} %fusion), channel_id=1, source_target_pairs={{0,8},{1,9},{2,10},{3,11},{4,12},{5,13},{6,14},{7,15},{8,0},{9,1},... | collective-permute-start | bytes 786440 | tf_op jit(solution)/shard_map/ppermute | solution.py:462
  78.6 8.7 %collective-permute-start.5 = (f32[2,2,16,8,128]{4,3,2,1,0:T(8,128)S(1)}, f32[2,2,16,8,128]{4,3,2,1,0:T(8,128)S(1)}, u32[]{:S(2)}, u32[]{:S(2)}) collective-permute-start(f32[2,2,16,8,128]{4,3,2,1,0:T(8,128)S(1)} %pad_maximum_fusion.1), channel_id=1, source_target_pairs={{0,24},{1,25},{2,26},{3,27},{4,28},{5,29},{6,30},{7,31},{8,16},{9,... | collective-permute-start | bytes 786440 | tf_op jit(solution)/shard_map/ppermute | solution.py:462
  87.4 7.2 %collective-permute-start.6 = (f32[2,16,8,128]{3,2,1,0:T(8,128)S(1)}, f32[2,16,8,128]{3,2,1,0:T(8,128)S(1)}, u32[]{:S(2)}, u32[]{:S(2)}) collective-permute-start(f32[2,16,8,128]{3,2,1,0:T(8,128)S(1)} %get-tuple-element.21), channel_id=1, source_target_pairs={{0,6},{1,7},{2,4},{3,5},{4,2},{5,3},{6,0},{7,1},{8,14},{9,15},{10,... | collective-permute-start | bytes 393224 | tf_op jit(solution)/shard_map/ppermute | solution.py:462
  127.3 24.8 %all-to-all-start.2 = ((f32[32,16,128]{2,1,0:T(8,128)}), f32[32,16,128]{2,1,0:T(8,128)S(1)}, u32[]{:S(2)}, u32[]{:S(2)}) async-start(f32[32,16,128]{2,1,0:T(8,128)} %share_total.1), calls=%async_computation.2 | async-start | bytes 524288 | tf_op jit(solution)/shard_map/all_to_all | solution.py:523

commit v7 on v6

--- a/solution.py
+++ b/solution.py
@@ -31,8 +31,9 @@
 
 def onehot(batch_row, rows):
     shape = (rows, batch_row.shape[1])
-    hit = lax.broadcasted_iota(jnp.int32, shape, 0) == batch_row
-    return hit.astype(jnp.float32).astype(jnp.bfloat16)
+    row = lax.broadcasted_iota(jnp.int32, shape, 0).astype(jnp.float32).astype(jnp.bfloat16)
+    hit = row == batch_row.astype(jnp.float32).astype(jnp.bfloat16)
+    return jnp.where(hit, jnp.ones((), jnp.bfloat16), jnp.zeros((), jnp.bfloat16))
 
 
 def turn(outer, inner):
@@ -48,8 +49,8 @@
     return lax.dot_general(inputs, delta, NT, preferred_element_type=jnp.float32)
 
 
-def store_pieces(j, info, grad_ref, outs, plus_ref):
-    owners, rows, columns = outs[0].shape[-3:]
+def store_pieces(info, grad_ref, out_ref):
+    owners, rows, columns = out_ref.shape[-3:]
     deep = 2 * side * rows
     for v in range(2):
         for o in range(2):
@@ -57,48 +58,14 @@
             for u in range(2):
                 left = slice(u * columns, (u + 1) * columns)
                 for z in range(owners):
-                    even = grad_ref[pl.ds(pl.multiple_of(z * deep + y * rows, rows), rows), left]
-                    odd = grad_ref[pl.ds(pl.multiple_of(z * deep + side * rows + y * rows, rows), rows), left]
-                    if plus_ref is not None:
-                        even += plus_ref[u, j, v, o, z]
-                        odd += plus_ref[2 + v, j, o, u, z]
-                    if plus_ref is None:
-                        outs[u][0, v, o, z] = even
-                        outs[2 + v][0, o, u, z] = odd
-                    else:
-                        outs[u][v, 0, o, z] = even
-                        outs[2 + v][u, 0, o, z] = odd
-
-
-def gather(cache_ref, batch_ref, inputs_ref):
-    rows = cache_ref.shape[0]
-    features = batch_ref.shape[0]
-    embed = inputs_ref.shape[0] // features
-
-    @pl.when(pl.program_id(0) == 0)
-    def _():
-        looked = jnp.transpose(cache_ref[...]).astype(jnp.bfloat16)
-        for f in range(features):
-            pick = onehot(batch_ref[f : f + 1, :], rows)
-            inputs_ref[f * embed : (f + 1) * embed, :] = lax.dot_general(
-                looked, pick, NN, preferred_element_type=jnp.float32
-            ).astype(jnp.bfloat16)
-
-
-def first_kernel(
-    info, cache_ref, batch_ref, loss_ref, head_a, head_b, w_a, w_b, grad_out, delta_ref, inputs_ref, grad_ref
-):
-    j = pl.program_id(0)
-    gather(cache_ref, batch_ref, inputs_ref)
-    head = jnp.concatenate([head_a[...], head_b[...]], 1)
-    w = jnp.concatenate([w_a[...], w_b[...]], 1)
-    grad_ref[...] = hidden(j, info, inputs_ref[...], loss_ref[...], head, w, delta_ref)
-    store_pieces(j, info, grad_ref, [grad_out.at[i] for i in range(4)], None)
-
-
-def second_kernel(
+                    even = pl.multiple_of(z * deep + y * rows, rows)
+                    odd = pl.multiple_of(z * deep + side * rows + y * rows, rows)
+                    out_ref[u, v, 0, o, z] = grad_ref[pl.ds(even, rows), left]
+                    out_ref[2 + v, u, 0, o, z] = grad_ref[pl.ds(odd, rows), left]
+
+
+def forward_kernel(
     info,
-    plus_ref,
     cache_ref,
     batch_ref,
     loss_ref,
@@ -106,64 +73,72 @@
     head_b,
     w_a,
     w_b,
-    out_a,
-    out_b,
-    out_c,
-    out_d,
-    delta_ref,
+    send_ref,
+    keep_ref,
+    delta_a,
+    delta_b,
     inputs_ref,
     grad_ref,
 ):
-    j = pl.program_id(0)
-    gather(cache_ref, batch_ref, inputs_ref)
+    rows = cache_ref.shape[0]
+    features = batch_ref.shape[0]
+    embed = inputs_ref.shape[0] // features
+    step = pl.program_id(0)
+    j = step & 1
+
+    @pl.when(step == 0)
+    def _():
+        looked = jnp.transpose(cache_ref[...]).astype(jnp.bfloat16)
+        for f in range(features):
+            pick = onehot(batch_ref[f : f + 1, :], rows)
+            inputs_ref[f * embed : (f + 1) * embed, :] = lax.dot_general(
+                looked, pick, NN, preferred_element_type=jnp.float32
+            ).astype(jnp.bfloat16)
+
     head = jnp.concatenate([head_a[...], head_b[...]], 1)
     w = jnp.concatenate([w_a[...], w_b[...]], 1)
-    grad_ref[...] = hidden(j, info, inputs_ref[...], loss_ref[...], head, w, delta_ref)
-    store_pieces(j, info, grad_ref, [out_a, out_b, out_c, out_d], plus_ref)
-
-
-def forward_half(info, owners, cache, batch_t, partner, loss, head, w):
+
+    @pl.when(step < 2)
+    def _():
+        grad_ref[...] = hidden(j, info, inputs_ref[...], loss_ref[...], head, w, delta_a)
+        store_pieces(info, grad_ref, send_ref)
+
+    @pl.when(step >= 2)
+    def _():
+        grad_ref[...] = hidden(j, info, inputs_ref[...], loss_ref[...], head, w, delta_b)
+        store_pieces(info, grad_ref, keep_ref)
+
+
+def forward(info, owners, cache, batch_t, loss, head, w):
     samples = loss.shape[1]
     width = w.shape[0]
     half = width // 2
     block = half // side
-    here = 0 if partner is None else 1
     rows = cache.shape[0]
     embed = cache.shape[1] // 3
-    part = lambda u: lambda j, c: (0, side * c[here] + (turn(j, u) ^ c[2]))
-    specs = [pl.BlockSpec((rows, embed), lambda j, c: (0, 0)), full(batch_t.shape), full((1, samples))]
+    part = lambda u: lambda i, c: (0, side * c[i >> 1] + (turn(i & 1, u) ^ c[2]))
+    specs = [pl.BlockSpec((rows, embed), lambda i, c: (0, 0)), full(batch_t.shape), full((1, samples))]
     specs += [pl.BlockSpec((1, block), part(u)) for u in range(2)]
     specs += [pl.BlockSpec((width, block), part(u)) for u in range(2)]
-    piece = (2, 2, 2, owners, width // (owners * 2 * side), block)
+    piece = (4, 2, 2, 2, owners, width // (owners * 2 * side), block)
+    grad = jax.ShapeDtypeStruct(piece, jnp.float32)
     delta = jax.ShapeDtypeStruct((side, block, samples), jnp.bfloat16)
-    delta_spec = pl.BlockSpec((2, block, samples), lambda j, c: (j ^ (c[2] >> 1), 0, 0))
-    scratch = [pltpu.VMEM((width, samples), jnp.bfloat16), pltpu.VMEM((width, 2 * block), jnp.float32)]
-    if partner is None:
-        return pl.pallas_call(
-            first_kernel,
-            out_shape=(jax.ShapeDtypeStruct((4,) + piece, jnp.float32), delta),
-            grid_spec=pltpu.PrefetchScalarGridSpec(
-                num_scalar_prefetch=1,
-                grid=(2,),
-                in_specs=specs,
-                out_specs=(pl.BlockSpec((4, 1) + piece[1:], lambda j, c: (0, j, 0, 0, 0, 0, 0)), delta_spec),
-                scratch_shapes=scratch,
-            ),
-            name="forward_first",
-        )(info, cache, batch_t, loss, head, head, w, w)
-    out_spec = pl.BlockSpec((2, 1, 2) + piece[3:], lambda j, c: (0, j, 0, 0, 0, 0))
-    return pl.pallas_call(
-        second_kernel,
-        out_shape=tuple(jax.ShapeDtypeStruct(piece, jnp.float32) for _ in range(4)) + (delta,),
+    early = lambda i: jnp.minimum(i, 1)
+    late = lambda i: jnp.maximum(i - 2, 0)
+    grad_spec = lambda at: pl.BlockSpec((4, 2, 1) + piece[3:], lambda i, c: (0, 0, at(i), 0, 0, 0, 0))
+    delta_spec = lambda at: pl.BlockSpec((2, block, samples), lambda i, c: (at(i) ^ (c[2] >> 1), 0, 0))
+    return pl.pallas_call(
+        forward_kernel,
+        out_shape=(grad, grad, delta, delta),
         grid_spec=pltpu.PrefetchScalarGridSpec(
             num_scalar_prefetch=1,
-            grid=(2,),
-            in_specs=[pl.BlockSpec(memory_space=pltpu.VMEM)] + specs,
-            out_specs=(out_spec,) * 4 + (delta_spec,),
-            scratch_shapes=scratch,
+            grid=(4,),
+            in_specs=specs,
+            out_specs=(grad_spec(early), grad_spec(late), delta_spec(early), delta_spec(late)),
+            scratch_shapes=[pltpu.VMEM((width, samples), jnp.bfloat16), pltpu.VMEM((width, 2 * block), jnp.float32)],
         ),
-        name="forward_second",
-    )(info, partner, cache, batch_t, loss, head, head, w, w)
+        name="forward",
+    )(info, cache, batch_t, loss, head, head, w, w)
 
 
 def backward_kernel(
@@ -497,20 +472,21 @@
 
     info = jnp.stack([1 - core, core, (place >> 3).astype(jnp.int32), ((place >> 1) & 3).astype(jnp.int32)])
     head_row = head[None]
-    send, delta_a = forward_half(info, group, cache, batch_t, None, loss, head_row, w_first)
-    partner = on_chip(lax.ppermute(send, "dp", pairs(1, 0, 0)))
+    send, keep, delta_a, delta_b = forward(info, group, cache, batch_t, loss, head_row, w_first)
+    partner = lax.ppermute(send, "dp", pairs(1, 0, 0))
     slots = lookup(home, wanted, gone, evict_counts[0], table_rows)
     lanes = cache.shape[1] // 3
     ids = jnp.pad(slots.astype(jnp.float32), ((0, 0), (0, lanes - slots.shape[1])))
     ids = jnp.broadcast_to(ids[:, None, :], (group, 8, lanes))
-    loss, ids = lax.optimization_barrier((loss, ids))
-    even, even_out, odd, odd_out, delta_b = forward_half(info, group, cache, batch_t, partner, loss, head_row, w_first)
-    even_in = send_to(even_out, 1, 0)
-    odd_in = send_to(odd_out, 0, 1)
+    partner, ids = lax.optimization_barrier((partner, ids))
+    even_in = send_to(keep[1] + partner[1], 1, 0)
+    odd_in = send_to(keep[3] + partner[3], 0, 1)
     sent = backward(info, evict_from[0, 0], cache, ids, batch_t, on_chip(delta_a), delta_b, w_first)
     got = lax.all_to_all(sent, "shard", split_axis=0, concat_axis=0, tiled=True)
-    even = even[0] + even_in[0] + send_to(even[1] + even_in[1], 0, 1)
-    odd = odd[0] + odd_in[0] + send_to(odd[1] + odd_in[1], 1, 0)
+    even = keep[0] + partner[0] + even_in
+    odd = keep[2] + partner[2] + odd_in
+    even = even[0] + send_to(even[1], 0, 1)
+    odd = odd[0] + send_to(odd[1], 1, 0)
     mine = jnp.stack([even[0], odd[0]], 1) + send_to(jnp.stack([even[1], odd[1]], 1), 3, 0)
     other = send_to(mine[1], 0, 3)
     asked = got[:, 3 * capacity, : 2 * capacity].astype(jnp.int32)

time: 154 us -> 155 us (level)
  waiting for transfers between devices: 25.4 us -> 29 us
  Pallas kernels: 38 us -> 34.5 us
  other arithmetic: 4.06 us -> 5.93 us
    pallas_call x2 -> x1, Pallas kernels: 15.3 us -> 11.7 us  [forward(): pl.pallas_call(forward_kernel, out_shape=(grad, grad, delta, delta), grid...]
    ppermute x6, waiting for transfers between devices: 20.4 us -> 23.7 us  [send_to(): return lax.ppermute(a, 'dp', pairs(0, x, y))]
    add x4, other arithmetic: 2.06 us -> 3.9 us  [the longest x1 2.2 us: local(): even = keep[0] + partner[0] + even_in]
  transfers between devices with their start and end apart: 9 -> 9, of which waited for: 5 -> 7; matrix products, arithmetic and copies ran while one was open for 3% -> 1% of each run, Pallas kernels for 13% -> 13%
where the time goes in v7:
time: 155 us; the launch traced here: 154 us
  starting transfers between devices  51.7 us (33%)
  Pallas kernels  34.5 us (22%)
  blocking collectives  31.4 us (20%)
  waiting for transfers between devices  29 us (19%)
  other arithmetic  5.93 us (4%)
    all_to_all x1, blocking collectives, local(): lax.all_to_all(served, 'shard', split_axis=0, concat_axis=0, tiled=True)  31.4 us
    ppermute x6, waiting for transfers between devices, send_to(): return lax.ppermute(a, 'dp', pairs(0, x, y))  23.7 us
    ppermute x6, starting transfers between devices, send_to(): return lax.ppermute(a, 'dp', pairs(0, x, y))  15.8 us
    all_to_all x1, starting transfers between devices, local(): lax.all_to_all(every, 'dp', split_axis=0, concat_axis=0, tiled=True)  15.5 us
    pallas_call x1, Pallas kernels, forward(): pl.pallas_call(forward_kernel, out_shape=(grad, grad, delta, delta), grid...  11.7 us
    all_to_all x1, starting transfers between devices, local(): got = lax.all_to_all(sent, 'shard', split_axis=0, concat_axis=0, tiled=True)  11.5 us
    pallas_call x1, Pallas kernels, backward(): pl.pallas_call(backward_kernel, out_shape=jax.ShapeDtypeStruct(sent, jnp....  11 us
    ppermute x1, starting transfers between devices, local(): partner = lax.ppermute(send, 'dp', pairs(1, 0, 0))  8.89 us
  transfers between devices with their start and end apart: 9, of which 7 were waited for; matrix products, arithmetic and copies ran while one was open for 1% of the time, Pallas kernels for 13%

profile of v7, /device:TPU:1, one launch (start us, length us, event | category | flops | bytes accessed | tf_op | source)
XLA Modules:
  0.0 154.1 jit_solution(10598157369247358834)
XLA Ops:
  0.6 0.7 pad_add_fusion.info
  1.3 11.7 %forward.1 = (f32[4,2,2,2,16,8,128]{6,5,4,3,2,1,0:T(8,128)}, f32[4,2,2,2,16,8,128]{6,5,4,3,2,1,0:T(8,128)}, bf16[4,128,1024]{2,1,0:T(8,128)(2,1)}, bf16[4,128,1024]{2,1,0:T(8,128)(2,1)}) custom-call(s32[4]{0:T(128)} %pad_add_fusion.info, f32[256,384]{1,0:T(8,128)} %bitcast.55, s32[8,1024]{1,0:T(8,128)} %bitcast.59, f32[1,1024]{1,0:T(1,128)} %bitcast.68, ...), custom_call_target="tpu_custom_call" | custom-call | tf_op jit(solution)/shard_map/forward/pallas_call | solution.py:130
  13.0 0.0 copy-start.1
  13.0 8.9 %collective-permute-start = (f32[4,2,2,2,16,8,128]{6,5,4,3,2,1,0:T(8,128)}, f32[4,2,2,2,16,8,128]{6,5,4,3,2,1,0:T(8,128)}, u32[]{:S(2)}, u32[]{:S(2)}) collective-permute-start(f32[4,2,2,2,16,8,128]{6,5,4,3,2,1,0:T(8,128)} %get-tuple-element.10), channel_id=1, source_target_pairs={{0,1},{1,0},{2,3},{3,2},{4,5},{5,4},{6,7},{7,6},{8,9},{9,8},{10,11... | collective-permute-start | bytes 6291464 | tf_op jit(solution)/shard_map/ppermute | solution.py:476
  21.9 3.0 %lookup.1 = s32[16,32]{1,0:T(8,128)} custom-call(s32[1,8192]{1,0:T(1,128)} %home_ref.1, s32[16,16]{1,0:T(8,128)} %bitcast.65, s32[16,16]{1,0:T(8,128)} %bitcast.66, s32[1,16]{1,0:T(1,128)} %bitcast.69), custom_call_target="tpu_custom_call" | custom-call | tf_op jit(solution)/shard_map/lookup/pallas_call | solution.py:322
  25.0 0.7 convert_element_type.26
  25.7 0.3 collective-permute-done
  26.0 0.6 broadcast_in_dim.16.ids_ref
  26.7 1.6 %add_bitcast_fusion.1 = (f32[2,2,2,16,8,128]{5,4,3,2,1,0:T(8,128)S(1)}, f32[2,2,2,16,8,128]{5,4,3,2,1,0:T(8,128)S(1)}) fusion(f32[4,2,2,2,16,8,128]{6,5,4,3,2,1,0:T(8,128)} %collective-permute-done, f32[4,2,2,2,16,8,128]{6,5,4,3,2,1,0:T(8,128)} %get-tuple-element.9), kind=kLoop, calls=%fused_computation.3 | loop fusion | flops 262144 | bytes 3145728 | tf_op jit(solution)/shard_map/add | solution.py:482
  28.3 1.9 %collective-permute-start.1 = (f32[2,2,2,16,8,128]{5,4,3,2,1,0:T(8,128)S(1)}, f32[2,2,2,16,8,128]{5,4,3,2,1,0:T(8,128)S(1)}, u32[]{:S(2)}, u32[]{:S(2)}) collective-permute-start(f32[2,2,2,16,8,128]{5,4,3,2,1,0:T(8,128)S(1)} %get-tuple-element.17), channel_id=1, source_target_pairs={{0,8},{1,9},{2,10},{3,11},{4,12},{5,13},{6,14},{7,15},{8,0},{9,1},... | collective-permute-start | bytes 1572872 | tf_op jit(solution)/shard_map/ppermute | solution.py:437
  30.2 0.0 copy-start
  30.2 2.1 %collective-permute-start.3 = (f32[2,2,2,16,8,128]{5,4,3,2,1,0:T(8,128)S(1)}, f32[2,2,2,16,8,128]{5,4,3,2,1,0:T(8,128)S(1)}, u32[]{:S(2)}, u32[]{:S(2)}) collective-permute-start(f32[2,2,2,16,8,128]{5,4,3,2,1,0:T(8,128)S(1)} %get-tuple-element.18), channel_id=1, source_target_pairs={{0,2},{1,3},{2,0},{3,1},{4,6},{5,7},{6,4},{7,5},{8,10},{9,11},{10,... | collective-permute-start | bytes 1572872 | tf_op jit(solution)/shard_map/ppermute | solution.py:437
  32.3 11.0 %collective-permute-done.1 = f32[2,2,2,16,8,128]{5,4,3,2,1,0:T(8,128)S(1)} collective-permute-done((f32[2,2,2,16,8,128]{5,4,3,2,1,0:T(8,128)S(1)}, f32[2,2,2,16,8,128]{5,4,3,2,1,0:T(8,128)S(1)}, u32[]{:S(2)}, u32[]{:S(2)}) %collective-permute-start.1) | collective-permute-done | bytes 524320 | tf_op jit(solution)/shard_map/ppermute | solution.py:437
  43.3 2.1 %collective-permute-done.3 = f32[2,2,2,16,8,128]{5,4,3,2,1,0:T(8,128)S(1)} collective-permute-done((f32[2,2,2,16,8,128]{5,4,3,2,1,0:T(8,128)S(1)}, f32[2,2,2,16,8,128]{5,4,3,2,1,0:T(8,128)S(1)}, u32[]{:S(2)}, u32[]{:S(2)}) %collective-permute-start.3) | collective-permute-done | bytes 524320 | tf_op jit(solution)/shard_map/ppermute | solution.py:437
  45.4 0.0 copy-done.1
  45.4 2.2 %bitcast_add_fusion.1 = (f32[2,2,2,16,8,128]{5,4,3,2,1,0:T(8,128)S(1)}, f32[2,2,2,16,8,128]{5,4,3,2,1,0:T(8,128)}) fusion(f32[2,2,2,16,8,128]{5,4,3,2,1,0:T(8,128)S(1)} %collective-permute-done.1, f32[4,2,2,2,16,8,128]{6,5,4,3,2,1,0:T(8,128)} %collective-permute-done, f32[4,2,2,2,16,8,128]{6,5,4,3,2,1,0:T(8,128)S(1)} %copy-done.1, ...), kind=kLoop, calls=%fused_computation.1 | loop fusion | flops 524288 | bytes 4194304 | tf_op jit(solution)/shard_map/add | solution.py:486
  47.6 0.0 copy-start.3
  47.6 2.2 %collective-permute-start.2 = (f32[2,2,16,8,128]{4,3,2,1,0:T(8,128)S(1)}, f32[2,2,16,8,128]{4,3,2,1,0:T(8,128)S(1)}, u32[]{:S(2)}, u32[]{:S(2)}) collective-permute-start(f32[2,2,16,8,128]{4,3,2,1,0:T(8,128)S(1)} %slice_bitcast_fusion.2), channel_id=1, source_target_pairs={{0,2},{1,3},{2,0},{3,1},{4,6},{5,7},{6,4},{7,5},{8,10},{9,11},{10,... | collective-permute-start | bytes 786440 | tf_op jit(solution)/shard_map/ppermute | solution.py:437
  49.8 0.0 copy-done.3
  49.8 0.0 copy-done
  49.8 0.0 copy-start.2
  49.8 0.0 copy-start.4
  49.8 11.0 %backward.1 = f32[16,56,128]{2,1,0:T(8,128)} custom-call(s32[4]{0:T(128)} %pad_add_fusion.info, s32[16,16]{1,0:T(8,128)} %bitcast.67, f32[256,384]{1,0:T(8,128)} %bitcast.56, f32[16,8,128]{2,1,0:T(8,128)} %broadcast_in_dim.16.ids_ref, s32[8,1024]{1,0:T(8,128)} %bitcast.60, bf16[4,128,1024]{2,1,0:T(8,128)(2,1)S(1)} %copy-done, ...), custom_call_target="tpu_custom_call" | custom-call | tf_op jit(solution)/shard_map/backward/pallas_call | solution.py:230
  60.9 11.5 %all-to-all-start = ((f32[16,56,128]{2,1,0:T(8,128)}), f32[16,56,128]{2,1,0:T(8,128)S(1)}, u32[]{:S(2)}, u32[]{:S(2)}) async-start(f32[16,56,128]{2,1,0:T(8,128)} %backward.1), calls=%async_computation | async-start | bytes 917504 | tf_op jit(solution)/shard_map/all_to_all | solution.py:485
  72.4 0.0 copy-done.2
  72.4 2.2 %collective-permute-start.4 = (f32[2,2,16,8,128]{4,3,2,1,0:T(8,128)S(1)}, f32[2,2,16,8,128]{4,3,2,1,0:T(8,128)S(1)}, u32[]{:S(2)}, u32[]{:S(2)}) collective-permute-start(f32[2,2,16,8,128]{4,3,2,1,0:T(8,128)S(1)} %slice_bitcast_fusion), channel_id=1, source_target_pairs={{0,8},{1,9},{2,10},{3,11},{4,12},{5,13},{6,14},{7,15},{8,0},{9,1},... | collective-permute-start | bytes 786440 | tf_op jit(solution)/shard_map/ppermute | solution.py:437
  74.6 0.0 collective-permute-done.2
  74.6 0.0 copy-done.4
  74.7 5.4 %collective-permute-done.4 = f32[2,2,16,8,128]{4,3,2,1,0:T(8,128)S(1)} collective-permute-done((f32[2,2,16,8,128]{4,3,2,1,0:T(8,128)S(1)}, f32[2,2,16,8,128]{4,3,2,1,0:T(8,128)S(1)}, u32[]{:S(2)}, u32[]{:S(2)}) %collective-permute-start.4) | collective-permute-done | bytes 262176 | tf_op jit(solution)/shard_map/ppermute | solution.py:437
  80.2 3.7 %collective-permute-start.5 = (f32[2,2,16,8,128]{4,3,2,1,0:T(8,128)S(1)}, f32[2,2,16,8,128]{4,3,2,1,0:T(8,128)S(1)}, u32[]{:S(2)}, u32[]{:S(2)}) collective-permute-start(f32[2,2,16,8,128]{4,3,2,1,0:T(8,128)S(1)} %pad_maximum_fusion.1), channel_id=1, source_target_pairs={{0,24},{1,25},{2,26},{3,27},{4,28},{5,29},{6,30},{7,31},{8,16},{9,... | collective-permute-start | bytes 786440 | tf_op jit(solution)/shard_map/ppermute | solution.py:437
  83.9 4.9 %collective-permute-done.5 = f32[2,2,16,8,128]{4,3,2,1,0:T(8,128)S(1)} collective-permute-done((f32[2,2,16,8,128]{4,3,2,1,0:T(8,128)S(1)}, f32[2,2,16,8,128]{4,3,2,1,0:T(8,128)S(1)}, u32[]{:S(2)}, u32[]{:S(2)}) %collective-permute-start.5) | collective-permute-done | bytes 262176 | tf_op jit(solution)/shard_map/ppermute | solution.py:437
  88.9 3.8 %collective-permute-start.6 = (f32[2,16,8,128]{3,2,1,0:T(8,128)S(1)}, f32[2,16,8,128]{3,2,1,0:T(8,128)S(1)}, u32[]{:S(2)}, u32[]{:S(2)}) collective-permute-start(f32[2,16,8,128]{3,2,1,0:T(8,128)S(1)} %get-tuple-element.19), channel_id=1, source_target_pairs={{0,6},{1,7},{2,4},{3,5},{4,2},{5,3},{6,0},{7,1},{8,14},{9,15},{10,... | collective-permute-start | bytes 393224 | tf_op jit(solution)/shard_map/ppermute | solution.py:437
  92.7 0.0 all-to-all-done.got_ref
  92.7 0.6 slice_convert_fusion
  93.3 2.5 %serve.1.served_ref = f32[16,64,128]{2,1,0:T(8,128)} custom-call(s32[16,32]{1,0:T(8,128)} %bitcast.61, f32[512,384]{1,0:T(8,128)} %bitcast.53), custom_call_target="tpu_custom_call" | custom-call | tf_op jit(solution)/shard_map/serve/pallas_call | solution.py:276
  95.9 0.2 collective-permute-done.6.other_ref
  96.1 0.7 add_block.1
  96.8 31.4 %all_to_all.15.got_ref = f32[16,64,128]{2,1,0:T(8,128)S(1)} all-to-all(f32[16,64,128]{2,1,0:T(8,128)} %add_block.1), channel_id=1, replica_groups=mesh['shard'=16,'dp'=32] {'shard'}, dimensions={0} | all-to-all | bytes 1048576 | tf_op jit(solution)/shard_map/all_to_all | solution.py:495
  128.2 0.7 share_total.1
  128.9 15.5 %all-to-all-start.2 = ((f32[32,16,128]{2,1,0:T(8,128)}), f32[32,16,128]{2,1,0:T(8,128)S(1)}, u32[]{:S(2)}, u32[]{:S(2)}) async-start(f32[32,16,128]{2,1,0:T(8,128)} %share_total.1), calls=%async_computation.2 | async-start | bytes 524288 | tf_op jit(solution)/shard_map/all_to_all | solution.py:499
  144.4 2.6 %settle.1 = f32[512,384]{1,0:T(8,128)} custom-call(s32[16,32]{1,0:T(8,128)} %bitcast.62, f32[16,56,128]{2,1,0:T(8,128)S(1)} %all-to-all-done.got_ref, f32[512,384]{1,0:T(8,128)} %bitcast.54), custom_call_target="tpu_custom_call" | custom-call | tf_op jit(solution)/shard_map/settle/pallas_call | solution.py:373
  147.0 1.4 mask_rows.1
  148.4 5.0 %all-to-all-done.2.every_ref = f32[32,16,128]{2,1,0:T(8,128)S(1)} async-done(((f32[32,16,128]{2,1,0:T(8,128)}), f32[32,16,128]{2,1,0:T(8,128)S(1)}, u32[]{:S(2)}, u32[]{:S(2)}) %all-to-all-start.2) | async-done | bytes 262176 | tf_op jit(solution)/shard_map/all_to_all | solution.py:499
  153.4 0.7 finish.1
  (10 shorter events, 0.2 us)
Async XLA Ops:
  13.0 32.3 %copy-start.1 = (f32[4,2,2,2,16,8,128]{6,5,4,3,2,1,0:T(8,128)S(1)}, f32[4,2,2,2,16,8,128]{6,5,4,3,2,1,0:T(8,128)}, u32[]{:S(2)}) copy-start(f32[4,2,2,2,16,8,128]{6,5,4,3,2,1,0:T(8,128)} %get-tuple-element.9) | copy-start | bytes 6291460
  13.0 13.0 %collective-permute-start = (f32[4,2,2,2,16,8,128]{6,5,4,3,2,1,0:T(8,128)}, f32[4,2,2,2,16,8,128]{6,5,4,3,2,1,0:T(8,128)}, u32[]{:S(2)}, u32[]{:S(2)}) collective-permute-start(f32[4,2,2,2,16,8,128]{6,5,4,3,2,1,0:T(8,128)} %get-tuple-element.10), channel_id=1, source_target_pairs={{0,1},{1,0},{2,3},{3,2},{4,5},{5,4},{6,7},{7,6},{8,9},{9,8},{10,11... | collective-permute-start | bytes 6291464 | tf_op jit(solution)/shard_map/ppermute | solution.py:476
  28.3 15.0 %collective-permute-start.1 = (f32[2,2,2,16,8,128]{5,4,3,2,1,0:T(8,128)S(1)}, f32[2,2,2,16,8,128]{5,4,3,2,1,0:T(8,128)S(1)}, u32[]{:S(2)}, u32[]{:S(2)}) collective-permute-start(f32[2,2,2,16,8,128]{5,4,3,2,1,0:T(8,128)S(1)} %get-tuple-element.17), channel_id=1, source_target_pairs={{0,8},{1,9},{2,10},{3,11},{4,12},{5,13},{6,14},{7,15},{8,0},{9,1},... | collective-permute-start | bytes 1572872 | tf_op jit(solution)/shard_map/ppermute | solution.py:437
  30.2 19.6 %copy-start = (bf16[4,128,1024]{2,1,0:T(8,128)(2,1)S(1)}, bf16[4,128,1024]{2,1,0:T(8,128)(2,1)}, u32[]{:S(2)}) copy-start(bf16[4,128,1024]{2,1,0:T(8,128)(2,1)} %get-tuple-element.13.delta_a) | copy-start | bytes 3145732
  30.2 15.1 %collective-permute-start.3 = (f32[2,2,2,16,8,128]{5,4,3,2,1,0:T(8,128)S(1)}, f32[2,2,2,16,8,128]{5,4,3,2,1,0:T(8,128)S(1)}, u32[]{:S(2)}, u32[]{:S(2)}) collective-permute-start(f32[2,2,2,16,8,128]{5,4,3,2,1,0:T(8,128)S(1)} %get-tuple-element.18), channel_id=1, source_target_pairs={{0,2},{1,3},{2,0},{3,1},{4,6},{5,7},{6,4},{7,5},{8,10},{9,11},{10,... | collective-permute-start | bytes 1572872 | tf_op jit(solution)/shard_map/ppermute | solution.py:437
  47.6 2.2 %copy-start.3 = (f32[2,2,2,16,8,128]{5,4,3,2,1,0:T(8,128)}, f32[2,2,2,16,8,128]{5,4,3,2,1,0:T(8,128)S(1)}, u32[]{:S(2)}) copy-start(f32[2,2,2,16,8,128]{5,4,3,2,1,0:T(8,128)S(1)} %get-tuple-element.15) | copy-start | bytes 1572868
  47.6 27.0 %collective-permute-start.2 = (f32[2,2,16,8,128]{4,3,2,1,0:T(8,128)S(1)}, f32[2,2,16,8,128]{4,3,2,1,0:T(8,128)S(1)}, u32[]{:S(2)}, u32[]{:S(2)}) collective-permute-start(f32[2,2,16,8,128]{4,3,2,1,0:T(8,128)S(1)} %slice_bitcast_fusion.2), channel_id=1, source_target_pairs={{0,2},{1,3},{2,0},{3,1},{4,6},{5,7},{6,4},{7,5},{8,10},{9,11},{10,... | collective-permute-start | bytes 786440 | tf_op jit(solution)/shard_map/ppermute | solution.py:437
  49.8 22.6 %copy-start.2 = (f32[2,2,2,16,8,128]{5,4,3,2,1,0:T(8,128)S(1)}, f32[2,2,2,16,8,128]{5,4,3,2,1,0:T(8,128)}, u32[]{:S(2)}) copy-start(f32[2,2,2,16,8,128]{5,4,3,2,1,0:T(8,128)} %get-tuple-element.16) | copy-start | bytes 1572868
  49.8 24.8 %copy-start.4 = (f32[2,2,2,16,8,128]{5,4,3,2,1,0:T(8,128)S(1)}, f32[2,2,2,16,8,128]{5,4,3,2,1,0:T(8,128)}, u32[]{:S(2)}) copy-start(f32[2,2,2,16,8,128]{5,4,3,2,1,0:T(8,128)} %copy-done.3) | copy-start | bytes 1572868
  60.9 31.8 %all-to-all-start = ((f32[16,56,128]{2,1,0:T(8,128)}), f32[16,56,128]{2,1,0:T(8,128)S(1)}, u32[]{:S(2)}, u32[]{:S(2)}) async-start(f32[16,56,128]{2,1,0:T(8,128)} %backward.1), calls=%async_computation | async-start | bytes 917504 | tf_op jit(solution)/shard_map/all_to_all | solution.py:485
  72.4 7.7 %collective-permute-start.4 = (f32[2,2,16,8,128]{4,3,2,1,0:T(8,128)S(1)}, f32[2,2,16,8,128]{4,3,2,1,0:T(8,128)S(1)}, u32[]{:S(2)}, u32[]{:S(2)}) collective-permute-start(f32[2,2,16,8,128]{4,3,2,1,0:T(8,128)S(1)} %slice_bitcast_fusion), channel_id=1, source_target_pairs={{0,8},{1,9},{2,10},{3,11},{4,12},{5,13},{6,14},{7,15},{8,0},{9,1},... | collective-permute-start | bytes 786440 | tf_op jit(solution)/shard_map/ppermute | solution.py:437
  80.2 8.6 %collective-permute-start.5 = (f32[2,2,16,8,128]{4,3,2,1,0:T(8,128)S(1)}, f32[2,2,16,8,128]{4,3,2,1,0:T(8,128)S(1)}, u32[]{:S(2)}, u32[]{:S(2)}) collective-permute-start(f32[2,2,16,8,128]{4,3,2,1,0:T(8,128)S(1)} %pad_maximum_fusion.1), channel_id=1, source_target_pairs={{0,24},{1,25},{2,26},{3,27},{4,28},{5,29},{6,30},{7,31},{8,16},{9,... | collective-permute-start | bytes 786440 | tf_op jit(solution)/shard_map/ppermute | solution.py:437
  88.9 7.2 %collective-permute-start.6 = (f32[2,16,8,128]{3,2,1,0:T(8,128)S(1)}, f32[2,16,8,128]{3,2,1,0:T(8,128)S(1)}, u32[]{:S(2)}, u32[]{:S(2)}) collective-permute-start(f32[2,16,8,128]{3,2,1,0:T(8,128)S(1)} %get-tuple-element.19), channel_id=1, source_target_pairs={{0,6},{1,7},{2,4},{3,5},{4,2},{5,3},{6,0},{7,1},{8,14},{9,15},{10,... | collective-permute-start | bytes 393224 | tf_op jit(solution)/shard_map/ppermute | solution.py:437
  128.9 24.5 %all-to-all-start.2 = ((f32[32,16,128]{2,1,0:T(8,128)}), f32[32,16,128]{2,1,0:T(8,128)S(1)}, u32[]{:S(2)}, u32[]{:S(2)}) async-start(f32[32,16,128]{2,1,0:T(8,128)} %share_total.1), calls=%async_computation.2 | async-start | bytes 524288 | tf_op jit(solution)/shard_map/all_to_all | solution.py:499

commit v8 on v7

--- a/solution.py
+++ b/solution.py
@@ -148,32 +148,19 @@
     ids_ref,
     batch_ref,
     delta_a,
-    delta_hbm,
+    delta_b,
     w_a,
     w_b,
     sent_ref,
     acc_ref,
     upd_ref,
-    delta_b,
-    arrived,
 ):
     rows, width = cache_ref.shape
     embed = width // 3
     owners, capacity = leaving.shape
     step = pl.program_id(0)
     half = w_a.shape[1]
-    copy = pltpu.make_async_copy(delta_hbm, delta_b, arrived)
-
-    @pl.when(step == 0)
-    def _():
-        copy.start()
-
     back = lax.dot_general(w_a[...], delta_a[...].reshape(half, -1), NN, preferred_element_type=jnp.float32)
-
-    @pl.when(step == 0)
-    def _():
-        copy.wait()
-
     back += lax.dot_general(w_b[...], delta_b[...].reshape(half, -1), NN, preferred_element_type=jnp.float32)
     total = None
     for k in range(w_a.shape[0] // embed):
@@ -187,7 +174,11 @@
     @pl.when(step == 0)
     def _():
         acc_ref[...] = total
-        sent_ref[:, 3 * capacity :, :] = ids_ref[...]
+        spare = sent_ref.shape[1] - 3 * capacity
+        sent_ref[:, 3 * capacity :, :] = jnp.zeros((owners, spare, embed), sent_ref.dtype)
+        for i in range(owners):
+            line = ids_ref[i : i + 1, :].astype(sent_ref.dtype)
+            sent_ref[i, 3 * capacity : 3 * capacity + 1, : ids_ref.shape[1]] = line
 
     @pl.when(step > 0)
     def _():
@@ -226,7 +217,7 @@
     owners, capacity = leaving.shape
     fixed = lambda shape: pl.BlockSpec(shape, lambda j, c, e: tuple(0 for _ in shape))
     whole = pl.BlockSpec(memory_space=pltpu.VMEM)
-    sent = (owners, 3 * capacity + ids.shape[1], embed)
+    sent = (owners, 3 * capacity + 8, embed)
     return pl.pallas_call(
         backward_kernel,
         out_shape=jax.ShapeDtypeStruct(sent, jnp.float32),
@@ -238,7 +229,7 @@
                 fixed(ids.shape),
                 fixed(batch_t.shape),
                 whole,
-                pl.BlockSpec(memory_space=pl.ANY),
+                whole,
                 pl.BlockSpec((2 * embed, half), lambda j, c, e: (j, c[0])),
                 pl.BlockSpec((2 * embed, half), lambda j, c, e: (j, c[1])),
             ],
@@ -246,8 +237,6 @@
             scratch_shapes=[
                 pltpu.VMEM((2 * embed, rows), jnp.float32),
                 pltpu.VMEM((rows, width3), jnp.float32),
-                pltpu.VMEM(delta_b.shape, delta_b.dtype),
-                pltpu.SemaphoreType.DMA(()),
             ],
         ),
         name="backward",
@@ -475,13 +464,10 @@
     send, keep, delta_a, delta_b = forward(info, group, cache, batch_t, loss, head_row, w_first)
     partner = lax.ppermute(send, "dp", pairs(1, 0, 0))
     slots = lookup(home, wanted, gone, evict_counts[0], table_rows)
-    lanes = cache.shape[1] // 3
-    ids = jnp.pad(slots.astype(jnp.float32), ((0, 0), (0, lanes - slots.shape[1])))
-    ids = jnp.broadcast_to(ids[:, None, :], (group, 8, lanes))
-    partner, ids = lax.optimization_barrier((partner, ids))
+    partner, slots = lax.optimization_barrier((partner, slots))
     even_in = send_to(keep[1] + partner[1], 1, 0)
     odd_in = send_to(keep[3] + partner[3], 0, 1)
-    sent = backward(info, evict_from[0, 0], cache, ids, batch_t, on_chip(delta_a), delta_b, w_first)
+    sent = backward(info, evict_from[0, 0], cache, slots, batch_t, on_chip(delta_a), on_chip(delta_b), w_first)
     got = lax.all_to_all(sent, "shard", split_axis=0, concat_axis=0, tiled=True)
     even = keep[0] + partner[0] + even_in
     odd = keep[2] + partner[2] + odd_in

time: 155 us -> 153 us (0.987)
  Pallas kernels: 34.5 us -> 32.8 us
    pallas_call x1, Pallas kernels: 11 us -> 9.39 us  [backward(): pl.pallas_call(backward_kernel, out_shape=jax.ShapeDtypeStruct(sent, jnp....]
  transfers between devices with their start and end apart: 9 -> 9, of which waited for: 7 -> 7; matrix products, arithmetic and copies ran while one was open for 1% -> 1% of each run, Pallas kernels for 13% -> 12%
where the time goes in v8:
time: 153 us; the launch traced here: 152 us
  starting transfers between devices  51.6 us (34%)
  Pallas kernels  32.8 us (21%)
  blocking collectives  31.4 us (21%)
  waiting for transfers between devices  29.6 us (19%)
  other arithmetic  4.82 us (3%)
    all_to_all x1, blocking collectives, local(): lax.all_to_all(served, 'shard', split_axis=0, concat_axis=0, tiled=True)  31.4 us
    ppermute x6, waiting for transfers between devices, send_to(): return lax.ppermute(a, 'dp', pairs(0, x, y))  23.7 us
    ppermute x6, starting transfers between devices, send_to(): return lax.ppermute(a, 'dp', pairs(0, x, y))  15.8 us
    all_to_all x1, starting transfers between devices, local(): lax.all_to_all(every, 'dp', split_axis=0, concat_axis=0, tiled=True)  15.6 us
    pallas_call x1, Pallas kernels, forward(): pl.pallas_call(forward_kernel, out_shape=(grad, grad, delta, delta), grid...  11.8 us
    all_to_all x1, starting transfers between devices, local(): got = lax.all_to_all(sent, 'shard', split_axis=0, concat_axis=0, tiled=True)  11.5 us
    pallas_call x1, Pallas kernels, backward(): pl.pallas_call(backward_kernel, out_shape=jax.ShapeDtypeStruct(sent, jnp....  9.39 us
    ppermute x1, starting transfers between devices, local(): partner = lax.ppermute(send, 'dp', pairs(1, 0, 0))  8.74 us
  transfers between devices with their start and end apart: 9, of which 7 were waited for; matrix products, arithmetic and copies ran while one was open for 1% of the time, Pallas kernels for 12%

profile of v8, /device:TPU:1, one launch (start us, length us, event | category | flops | bytes accessed | tf_op | source)
XLA Modules:
  0.0 151.9 jit_solution(12631322767765292018)
XLA Ops:
  0.6 0.6 pad_add_fusion.info
  1.3 11.8 %forward.1 = (f32[4,2,2,2,16,8,128]{6,5,4,3,2,1,0:T(8,128)}, f32[4,2,2,2,16,8,128]{6,5,4,3,2,1,0:T(8,128)}, bf16[4,128,1024]{2,1,0:T(8,128)(2,1)}, bf16[4,128,1024]{2,1,0:T(8,128)(2,1)}) custom-call(s32[4]{0:T(128)} %pad_add_fusion.info, f32[256,384]{1,0:T(8,128)} %bitcast.55, s32[8,1024]{1,0:T(8,128)} %bitcast.59, f32[1,1024]{1,0:T(1,128)} %bitcast.68, ...), custom_call_target="tpu_custom_call" | custom-call | tf_op jit(solution)/shard_map/forward/pallas_call | solution.py:130
  13.0 8.7 %collective-permute-start = (f32[4,2,2,2,16,8,128]{6,5,4,3,2,1,0:T(8,128)}, f32[4,2,2,2,16,8,128]{6,5,4,3,2,1,0:T(8,128)S(1)}, u32[]{:S(2)}, u32[]{:S(2)}) collective-permute-start(f32[4,2,2,2,16,8,128]{6,5,4,3,2,1,0:T(8,128)} %get-tuple-element.10), channel_id=1, source_target_pairs={{0,1},{1,0},{2,3},{3,2},{4,5},{5,4},{6,7},{7,6},{8,9},{9,8},{10,11... | collective-permute-start | bytes 6291464 | tf_op jit(solution)/shard_map/ppermute | solution.py:465
  21.8 3.0 %lookup.1.ids_ref = s32[16,32]{1,0:T(8,128)} custom-call(s32[1,8192]{1,0:T(1,128)} %home_ref.1, s32[16,16]{1,0:T(8,128)} %bitcast.66, s32[16,16]{1,0:T(8,128)} %bitcast.67, s32[1,16]{1,0:T(1,128)} %bitcast.69), custom_call_target="tpu_custom_call" | custom-call | tf_op jit(solution)/shard_map/lookup/pallas_call | solution.py:311
  24.8 0.0 copy-start.2
  24.8 0.9 collective-permute-done
  25.7 0.0 copy-start.3
  25.7 2.1 %add_bitcast_fusion.1 = (f32[2,2,2,16,8,128]{5,4,3,2,1,0:T(8,128)S(1)}, f32[2,2,2,16,8,128]{5,4,3,2,1,0:T(8,128)S(1)}) fusion(f32[4,2,2,2,16,8,128]{6,5,4,3,2,1,0:T(8,128)S(1)} %collective-permute-done, f32[4,2,2,2,16,8,128]{6,5,4,3,2,1,0:T(8,128)} %get-tuple-element.9), kind=kLoop, calls=%fused_computation.3 | loop fusion | flops 262144 | bytes 3145728 | tf_op jit(solution)/shard_map/add | solution.py:468
  27.8 1.9 %collective-permute-start.1 = (f32[2,2,2,16,8,128]{5,4,3,2,1,0:T(8,128)S(1)}, f32[2,2,2,16,8,128]{5,4,3,2,1,0:T(8,128)S(1)}, u32[]{:S(2)}, u32[]{:S(2)}) collective-permute-start(f32[2,2,2,16,8,128]{5,4,3,2,1,0:T(8,128)S(1)} %get-tuple-element.17), channel_id=1, source_target_pairs={{0,8},{1,9},{2,10},{3,11},{4,12},{5,13},{6,14},{7,15},{8,0},{9,1},... | collective-permute-start | bytes 1572872 | tf_op jit(solution)/shard_map/ppermute | solution.py:426
  29.7 0.0 copy-done.3
  29.8 0.0 copy-start
  29.8 0.0 copy-start.1
  29.8 2.1 %collective-permute-start.3 = (f32[2,2,2,16,8,128]{5,4,3,2,1,0:T(8,128)S(1)}, f32[2,2,2,16,8,128]{5,4,3,2,1,0:T(8,128)S(1)}, u32[]{:S(2)}, u32[]{:S(2)}) collective-permute-start(f32[2,2,2,16,8,128]{5,4,3,2,1,0:T(8,128)S(1)} %get-tuple-element.18), channel_id=1, source_target_pairs={{0,2},{1,3},{2,0},{3,1},{4,6},{5,7},{6,4},{7,5},{8,10},{9,11},{10,... | collective-permute-start | bytes 1572872 | tf_op jit(solution)/shard_map/ppermute | solution.py:426
  31.8 11.0 %collective-permute-done.1 = f32[2,2,2,16,8,128]{5,4,3,2,1,0:T(8,128)S(1)} collective-permute-done((f32[2,2,2,16,8,128]{5,4,3,2,1,0:T(8,128)S(1)}, f32[2,2,2,16,8,128]{5,4,3,2,1,0:T(8,128)S(1)}, u32[]{:S(2)}, u32[]{:S(2)}) %collective-permute-start.1) | collective-permute-done | bytes 524320 | tf_op jit(solution)/shard_map/ppermute | solution.py:426
  42.8 2.1 %collective-permute-done.3 = f32[2,2,2,16,8,128]{5,4,3,2,1,0:T(8,128)S(1)} collective-permute-done((f32[2,2,2,16,8,128]{5,4,3,2,1,0:T(8,128)S(1)}, f32[2,2,2,16,8,128]{5,4,3,2,1,0:T(8,128)S(1)}, u32[]{:S(2)}, u32[]{:S(2)}) %collective-permute-start.3) | collective-permute-done | bytes 524320 | tf_op jit(solution)/shard_map/ppermute | solution.py:426
  44.9 0.0 copy-done.2
  44.9 1.4 bitcast_add_fusion.1
  46.3 0.7 slice_bitcast_fusion.2
  47.0 2.2 %collective-permute-start.2 = (f32[2,2,16,8,128]{4,3,2,1,0:T(8,128)}, f32[2,2,16,8,128]{4,3,2,1,0:T(8,128)S(1)}, u32[]{:S(2)}, u32[]{:S(2)}) collective-permute-start(f32[2,2,16,8,128]{4,3,2,1,0:T(8,128)} %slice_bitcast_fusion.2), channel_id=1, source_target_pairs={{0,2},{1,3},{2,0},{3,1},{4,6},{5,7},{6,4},{7,5},{8,10},{9,11},{10,... | collective-permute-start | bytes 786440 | tf_op jit(solution)/shard_map/ppermute | solution.py:426
  49.2 0.0 copy-done
  49.3 0.0 copy-done.1
  49.3 9.4 %backward.1 = f32[16,56,128]{2,1,0:T(8,128)} custom-call(s32[4]{0:T(128)} %pad_add_fusion.info, s32[16,16]{1,0:T(8,128)} %bitcast.65, f32[256,384]{1,0:T(8,128)} %bitcast.56, s32[16,32]{1,0:T(8,128)} %lookup.1.ids_ref, s32[8,1024]{1,0:T(8,128)} %bitcast.60, bf16[4,128,1024]{2,1,0:T(8,128)(2,1)S(1)} %copy-done, bf16[4,128,1024]{2,1,0:T(8,128)(2,1)S(1)} %copy-done.1, ...), custom_call_target="tpu_custom_call" | custom-call | tf_op jit(solution)/shard_map/backward/pallas_call | solution.py:221
  58.7 11.5 %all-to-all-start = ((f32[16,56,128]{2,1,0:T(8,128)}), f32[16,56,128]{2,1,0:T(8,128)S(1)}, u32[]{:S(2)}, u32[]{:S(2)}) async-start(f32[16,56,128]{2,1,0:T(8,128)} %backward.1), calls=%async_computation | async-start | bytes 917504 | tf_op jit(solution)/shard_map/all_to_all | solution.py:471
  70.2 2.2 %collective-permute-start.4 = (f32[2,2,16,8,128]{4,3,2,1,0:T(8,128)S(1)}, f32[2,2,16,8,128]{4,3,2,1,0:T(8,128)S(1)}, u32[]{:S(2)}, u32[]{:S(2)}) collective-permute-start(f32[2,2,16,8,128]{4,3,2,1,0:T(8,128)S(1)} %slice_bitcast_fusion), channel_id=1, source_target_pairs={{0,8},{1,9},{2,10},{3,11},{4,12},{5,13},{6,14},{7,15},{8,0},{9,1},... | collective-permute-start | bytes 786440 | tf_op jit(solution)/shard_map/ppermute | solution.py:426
  72.4 0.0 collective-permute-done.2
  72.4 5.4 %collective-permute-done.4 = f32[2,2,16,8,128]{4,3,2,1,0:T(8,128)S(1)} collective-permute-done((f32[2,2,16,8,128]{4,3,2,1,0:T(8,128)S(1)}, f32[2,2,16,8,128]{4,3,2,1,0:T(8,128)S(1)}, u32[]{:S(2)}, u32[]{:S(2)}) %collective-permute-start.4) | collective-permute-done | bytes 262176 | tf_op jit(solution)/shard_map/ppermute | solution.py:426
  78.0 3.7 %collective-permute-start.5 = (f32[2,2,16,8,128]{4,3,2,1,0:T(8,128)S(1)}, f32[2,2,16,8,128]{4,3,2,1,0:T(8,128)S(1)}, u32[]{:S(2)}, u32[]{:S(2)}) collective-permute-start(f32[2,2,16,8,128]{4,3,2,1,0:T(8,128)S(1)} %pad_maximum_fusion.1), channel_id=1, source_target_pairs={{0,24},{1,25},{2,26},{3,27},{4,28},{5,29},{6,30},{7,31},{8,16},{9,... | collective-permute-start | bytes 786440 | tf_op jit(solution)/shard_map/ppermute | solution.py:426
  81.7 4.9 %collective-permute-done.5 = f32[2,2,16,8,128]{4,3,2,1,0:T(8,128)S(1)} collective-permute-done((f32[2,2,16,8,128]{4,3,2,1,0:T(8,128)S(1)}, f32[2,2,16,8,128]{4,3,2,1,0:T(8,128)S(1)}, u32[]{:S(2)}, u32[]{:S(2)}) %collective-permute-start.5) | collective-permute-done | bytes 262176 | tf_op jit(solution)/shard_map/ppermute | solution.py:426
  86.6 3.8 %collective-permute-start.6 = (f32[2,16,8,128]{3,2,1,0:T(8,128)S(1)}, f32[2,16,8,128]{3,2,1,0:T(8,128)S(1)}, u32[]{:S(2)}, u32[]{:S(2)}) collective-permute-start(f32[2,16,8,128]{3,2,1,0:T(8,128)S(1)} %get-tuple-element.19), channel_id=1, source_target_pairs={{0,6},{1,7},{2,4},{3,5},{4,2},{5,3},{6,0},{7,1},{8,14},{9,15},{10,... | collective-permute-start | bytes 393224 | tf_op jit(solution)/shard_map/ppermute | solution.py:426
  90.4 0.0 all-to-all-done.got_ref
  90.5 0.6 slice_convert_fusion
  91.1 2.5 %serve.1.served_ref = f32[16,64,128]{2,1,0:T(8,128)} custom-call(s32[16,32]{1,0:T(8,128)} %bitcast.61, f32[512,384]{1,0:T(8,128)} %bitcast.53), custom_call_target="tpu_custom_call" | custom-call | tf_op jit(solution)/shard_map/serve/pallas_call | solution.py:265
  93.6 0.3 collective-permute-done.6.other_ref
  93.9 0.7 add_block.1
  94.5 31.4 %all_to_all.15.got_ref = f32[16,64,128]{2,1,0:T(8,128)S(1)} all-to-all(f32[16,64,128]{2,1,0:T(8,128)} %add_block.1), channel_id=1, replica_groups=mesh['shard'=16,'dp'=32] {'shard'}, dimensions={0} | all-to-all | bytes 1048576 | tf_op jit(solution)/shard_map/all_to_all | solution.py:481
  125.9 0.7 share_total.1
  126.7 15.6 %all-to-all-start.2 = ((f32[32,16,128]{2,1,0:T(8,128)}), f32[32,16,128]{2,1,0:T(8,128)S(1)}, u32[]{:S(2)}, u32[]{:S(2)}) async-start(f32[32,16,128]{2,1,0:T(8,128)} %share_total.1), calls=%async_computation.2 | async-start | bytes 524288 | tf_op jit(solution)/shard_map/all_to_all | solution.py:485
  142.3 2.6 %settle.1 = f32[512,384]{1,0:T(8,128)} custom-call(s32[16,32]{1,0:T(8,128)} %bitcast.62, f32[16,56,128]{2,1,0:T(8,128)S(1)} %all-to-all-done.got_ref, f32[512,384]{1,0:T(8,128)} %bitcast.54), custom_call_target="tpu_custom_call" | custom-call | tf_op jit(solution)/shard_map/settle/pallas_call | solution.py:362
  144.8 1.4 mask_rows.1
  146.3 5.0 %all-to-all-done.2.every_ref = f32[32,16,128]{2,1,0:T(8,128)S(1)} async-done(((f32[32,16,128]{2,1,0:T(8,128)}), f32[32,16,128]{2,1,0:T(8,128)S(1)}, u32[]{:S(2)}, u32[]{:S(2)}) %all-to-all-start.2) | async-done | bytes 262176 | tf_op jit(solution)/shard_map/all_to_all | solution.py:485
  151.2 0.7 finish.1
  (8 shorter events, 0.2 us)
Async XLA Ops:
  13.0 12.7 %collective-permute-start = (f32[4,2,2,2,16,8,128]{6,5,4,3,2,1,0:T(8,128)}, f32[4,2,2,2,16,8,128]{6,5,4,3,2,1,0:T(8,128)S(1)}, u32[]{:S(2)}, u32[]{:S(2)}) collective-permute-start(f32[4,2,2,2,16,8,128]{6,5,4,3,2,1,0:T(8,128)} %get-tuple-element.10), channel_id=1, source_target_pairs={{0,1},{1,0},{2,3},{3,2},{4,5},{5,4},{6,7},{7,6},{8,9},{9,8},{10,11... | collective-permute-start | bytes 6291464 | tf_op jit(solution)/shard_map/ppermute | solution.py:465
  24.8 20.1 %copy-start.2 = (f32[4,2,2,2,16,8,128]{6,5,4,3,2,1,0:T(8,128)S(1)}, f32[4,2,2,2,16,8,128]{6,5,4,3,2,1,0:T(8,128)}, u32[]{:S(2)}) copy-start(f32[4,2,2,2,16,8,128]{6,5,4,3,2,1,0:T(8,128)} %get-tuple-element.9) | copy-start | bytes 6291460
  25.7 4.0 %copy-start.3 = (f32[4,2,2,2,16,8,128]{6,5,4,3,2,1,0:T(8,128)}, f32[4,2,2,2,16,8,128]{6,5,4,3,2,1,0:T(8,128)S(1)}, u32[]{:S(2)}) copy-start(f32[4,2,2,2,16,8,128]{6,5,4,3,2,1,0:T(8,128)S(1)} %collective-permute-done) | copy-start | bytes 6291460
  27.8 15.0 %collective-permute-start.1 = (f32[2,2,2,16,8,128]{5,4,3,2,1,0:T(8,128)S(1)}, f32[2,2,2,16,8,128]{5,4,3,2,1,0:T(8,128)S(1)}, u32[]{:S(2)}, u32[]{:S(2)}) collective-permute-start(f32[2,2,2,16,8,128]{5,4,3,2,1,0:T(8,128)S(1)} %get-tuple-element.17), channel_id=1, source_target_pairs={{0,8},{1,9},{2,10},{3,11},{4,12},{5,13},{6,14},{7,15},{8,0},{9,1},... | collective-permute-start | bytes 1572872 | tf_op jit(solution)/shard_map/ppermute | solution.py:426
  29.8 19.5 %copy-start = (bf16[4,128,1024]{2,1,0:T(8,128)(2,1)S(1)}, bf16[4,128,1024]{2,1,0:T(8,128)(2,1)}, u32[]{:S(2)}) copy-start(bf16[4,128,1024]{2,1,0:T(8,128)(2,1)} %get-tuple-element.13.delta_a) | copy-start | bytes 3145732
  29.8 19.5 %copy-start.1 = (bf16[4,128,1024]{2,1,0:T(8,128)(2,1)S(1)}, bf16[4,128,1024]{2,1,0:T(8,128)(2,1)}, u32[]{:S(2)}) copy-start(bf16[4,128,1024]{2,1,0:T(8,128)(2,1)} %get-tuple-element.14.delta_b) | copy-start | bytes 3145732
  29.8 15.1 %collective-permute-start.3 = (f32[2,2,2,16,8,128]{5,4,3,2,1,0:T(8,128)S(1)}, f32[2,2,2,16,8,128]{5,4,3,2,1,0:T(8,128)S(1)}, u32[]{:S(2)}, u32[]{:S(2)}) collective-permute-start(f32[2,2,2,16,8,128]{5,4,3,2,1,0:T(8,128)S(1)} %get-tuple-element.18), channel_id=1, source_target_pairs={{0,2},{1,3},{2,0},{3,1},{4,6},{5,7},{6,4},{7,5},{8,10},{9,11},{10,... | collective-permute-start | bytes 1572872 | tf_op jit(solution)/shard_map/ppermute | solution.py:426
  47.0 25.3 %collective-permute-start.2 = (f32[2,2,16,8,128]{4,3,2,1,0:T(8,128)}, f32[2,2,16,8,128]{4,3,2,1,0:T(8,128)S(1)}, u32[]{:S(2)}, u32[]{:S(2)}) collective-permute-start(f32[2,2,16,8,128]{4,3,2,1,0:T(8,128)} %slice_bitcast_fusion.2), channel_id=1, source_target_pairs={{0,2},{1,3},{2,0},{3,1},{4,6},{5,7},{6,4},{7,5},{8,10},{9,11},{10,... | collective-permute-start | bytes 786440 | tf_op jit(solution)/shard_map/ppermute | solution.py:426
  58.7 31.8 %all-to-all-start = ((f32[16,56,128]{2,1,0:T(8,128)}), f32[16,56,128]{2,1,0:T(8,128)S(1)}, u32[]{:S(2)}, u32[]{:S(2)}) async-start(f32[16,56,128]{2,1,0:T(8,128)} %backward.1), calls=%async_computation | async-start | bytes 917504 | tf_op jit(solution)/shard_map/all_to_all | solution.py:471
  70.2 7.7 %collective-permute-start.4 = (f32[2,2,16,8,128]{4,3,2,1,0:T(8,128)S(1)}, f32[2,2,16,8,128]{4,3,2,1,0:T(8,128)S(1)}, u32[]{:S(2)}, u32[]{:S(2)}) collective-permute-start(f32[2,2,16,8,128]{4,3,2,1,0:T(8,128)S(1)} %slice_bitcast_fusion), channel_id=1, source_target_pairs={{0,8},{1,9},{2,10},{3,11},{4,12},{5,13},{6,14},{7,15},{8,0},{9,1},... | collective-permute-start | bytes 786440 | tf_op jit(solution)/shard_map/ppermute | solution.py:426
  78.0 8.6 %collective-permute-start.5 = (f32[2,2,16,8,128]{4,3,2,1,0:T(8,128)S(1)}, f32[2,2,16,8,128]{4,3,2,1,0:T(8,128)S(1)}, u32[]{:S(2)}, u32[]{:S(2)}) collective-permute-start(f32[2,2,16,8,128]{4,3,2,1,0:T(8,128)S(1)} %pad_maximum_fusion.1), channel_id=1, source_target_pairs={{0,24},{1,25},{2,26},{3,27},{4,28},{5,29},{6,30},{7,31},{8,16},{9,... | collective-permute-start | bytes 786440 | tf_op jit(solution)/shard_map/ppermute | solution.py:426
  86.6 7.2 %collective-permute-start.6 = (f32[2,16,8,128]{3,2,1,0:T(8,128)S(1)}, f32[2,16,8,128]{3,2,1,0:T(8,128)S(1)}, u32[]{:S(2)}, u32[]{:S(2)}) collective-permute-start(f32[2,16,8,128]{3,2,1,0:T(8,128)S(1)} %get-tuple-element.19), channel_id=1, source_target_pairs={{0,6},{1,7},{2,4},{3,5},{4,2},{5,3},{6,0},{7,1},{8,14},{9,15},{10,... | collective-permute-start | bytes 393224 | tf_op jit(solution)/shard_map/ppermute | solution.py:426
  126.7 24.6 %all-to-all-start.2 = ((f32[32,16,128]{2,1,0:T(8,128)}), f32[32,16,128]{2,1,0:T(8,128)S(1)}, u32[]{:S(2)}, u32[]{:S(2)}) async-start(f32[32,16,128]{2,1,0:T(8,128)} %share_total.1), calls=%async_computation.2 | async-start | bytes 524288 | tf_op jit(solution)/shard_map/all_to_all | solution.py:485
